TPU v7x, 512 devices: a whole 4x8x8 slice. The times are simulated.
512 devices in a mesh: ctx: 64 (over z, x, core), tp: 8 (over y).
Axes of the slice: x: 4, y: 8, z: 8, core: 2. Of those that a mesh axis runs over, the one named last changes fastest.
Arguments:
- ctx_queries: bfloat16 [16384, 4096], P('ctx', 'tp'), may hold values from -5 to 5
- ctx_keys: bfloat16 [16384, 1024], P('ctx', 'tp'), may hold values from -5 to 5
- ctx_values: bfloat16 [16384, 1024], P('ctx', 'tp'), may hold values from -18 to 18
- query_queries: bfloat16 [512, 4096], P(None, 'tp'), may hold values from -5 to 5
- query_keys: bfloat16 [512, 1024], P('ctx', 'tp'), may hold values from -5 to 5
- query_values: bfloat16 [512, 1024], P('ctx', 'tp'), may hold values from -18 to 18
- out_weight: bfloat16 [4096, 4096], P('tp', 'ctx'), may hold values from -0.09375 to 0.09375
Outputs:
- ctx_out: bfloat16 [16384, 4096], P('ctx', 'tp')
- query_out: bfloat16 [512, 4096], P('tp', 'ctx')
All inputs are finite; a program needn't handle non-finite values.
Results may differ from a plain program's by a relative error of at most 0.0049.
Values may be sent and summed in bfloat16 or wider, within the bound.
No kernel may reach another device: no remote copies, remote signals or barrier semaphores. Data moves between devices by JAX's collectives and lax.ppermute only.
A program may use at most 192 MiB of HBM per device.

v0:
```python
import math

import jax
import jax.numpy as jnp
from jax import lax
from jax.sharding import PartitionSpec as P

HD = 128
QL = 512


def spread(block, axis, source):
    block = jnp.where(lax.axis_index(axis) == source, block, jnp.zeros_like(block))
    return lax.psum(block, axis)


def attend_part(query_part, key_part, value_part, visible):
    scale = HD ** (-0.5)
    scores = (
        jnp.einsum("tkgd,skd->tkgs", query_part, key_part, preferred_element_type=jnp.float32)
        * scale
    )
    scores = jnp.where(visible[:, None, None, :], scores, -jnp.inf)
    top = jnp.max(scores, axis=-1)
    weights = jnp.exp(scores - top[..., None])
    total = jnp.sum(weights, axis=-1)
    probs = weights.astype(jnp.bfloat16)
    summed = jnp.einsum("tkgs,skd->tkgd", probs, value_part, preferred_element_type=jnp.float32)
    return (top, total, summed)


def body(ctx_queries, ctx_keys, ctx_values, query_queries, query_keys, query_values, out_weight):
    block_len = ctx_queries.shape[0]
    kv_local = ctx_keys.shape[1] // HD
    group = ctx_queries.shape[1] // ctx_keys.shape[1]
    index = lax.axis_index("ctx")
    anchor_keys, anchor_values = (spread(ctx_keys, "ctx", 0), spread(ctx_values, "ctx", 0))
    key_rows = jnp.concatenate([anchor_keys, ctx_keys], 0).reshape(2 * block_len, kv_local, HD)
    value_rows = jnp.concatenate([anchor_values, ctx_values], 0).reshape(
        2 * block_len, kv_local, HD
    )
    query_grid = ctx_queries.reshape(block_len, kv_local, group, HD)
    width = math.gcd(block_len, 128)

    def context_piece(start):
        rows = lax.dynamic_slice_in_dim(query_grid, start, width, 0)
        position = start + jnp.arange(width)
        own_seen = position[:, None] >= jnp.arange(block_len)[None, :]
        anchor_seen = jnp.broadcast_to(index > 0, (width, block_len))
        visible = jnp.concatenate([anchor_seen, own_seen], 1)
        top, total, summed = attend_part(rows, key_rows, value_rows, visible)
        return (summed / total[..., None]).astype(jnp.bfloat16).reshape(width, -1)

    ctx_starts = jnp.arange(block_len // width) * width
    ctx_out = lax.map(context_piece, ctx_starts).reshape(block_len, -1)
    share = query_keys.shape[0]
    own_keys = jnp.concatenate([ctx_keys, query_keys], 0).reshape(block_len + share, kv_local, HD)
    own_values = jnp.concatenate([ctx_values, query_values], 0).reshape(
        block_len + share, kv_local, HD
    )
    asked = query_queries.reshape(QL, kv_local, group, HD)
    key_pos = index * share + jnp.arange(share)
    query_width = math.gcd(QL, 128)

    def query_piece(start):
        rows = lax.dynamic_slice_in_dim(asked, start, query_width, 0)
        position = start + jnp.arange(query_width)
        visible = jnp.concatenate(
            [jnp.ones((query_width, block_len), dtype=bool), position[:, None] >= key_pos[None, :]],
            1,
        )
        return attend_part(rows, own_keys, own_values, visible)

    query_starts = jnp.arange(QL // query_width) * query_width
    tops, totals, sums = lax.map(query_piece, query_starts)
    local_top = tops.reshape(QL, kv_local, group)
    local_total = totals.reshape(QL, kv_local, group)
    local_sum = sums.reshape(QL, kv_local, group, HD)
    highest = lax.pmax(local_top, "ctx")
    factor = jnp.exp(local_top - highest)
    full_total, full_sum = lax.psum((local_total * factor, local_sum * factor[..., None]), "ctx")
    normed = (full_sum / full_total[..., None]).astype(jnp.bfloat16)
    attended = normed.reshape(QL, -1)
    rows = attended
    query_out = lax.psum_scatter(
        jnp.dot(rows, out_weight, preferred_element_type=jnp.float32),
        "tp",
        scatter_dimension=0,
        tiled=True,
    ).astype(jnp.bfloat16)
    return (ctx_out, query_out)


def solution(mesh):
    return jax.shard_map(
        body,
        mesh=mesh,
        in_specs=(
            P("ctx", "tp"),
            P("ctx", "tp"),
            P("ctx", "tp"),
            P(None, "tp"),
            P("ctx", "tp"),
            P("ctx", "tp"),
            P("tp", "ctx"),
        ),
        out_specs=(P("ctx", "tp"), P("tp", "ctx")),
        check_vma=False,
    )
```

profile of v0, /device:TPU:1, one launch (start us, length us, event | category | flops | bytes accessed | tf_op | source)
XLA Modules:
  0.0 442.6 jit_solution(15950713859537265011)
XLA Ops:
  7.2 0.7 broadcast_select_fusion
  8.1 1.3 copy.25
  9.4 16.3 %while.28 = (s32[]{:T(128)}, f32[4,128,1,4]{1,3,2,0:T(4,128)S(1)}, f32[4,128,1,4]{1,3,2,0:T(4,128)S(1)}, f32[4,128,1,4,128]{4,1,0,3,2:T(8,128)S(1)}, s32[4]{0:T(...) while((s32[]{:T(128)}, f32[4,128,1,4]{1,3,2,0:T(4,128)S(1)}, ...), condition=%wide.region_9.10_spmd.clone, body=%wide.region_6.9_spmd.clone.sunk | while | flops 70152336 | bytes 2237696 | solution.py:75
  9.4 0.6 dynamic_slice.39
  12.0 0.6 iota_add_fusion.7
  13.5 0.6 dynamic_slice.39
  16.0 0.6 iota_add_fusion.7
  17.6 0.6 dynamic_slice.39
  20.1 0.6 iota_add_fusion.7
  20.9 0.3 fusion.53
  21.7 0.6 dynamic_slice.39
  24.2 0.6 iota_add_fusion.7
  25.7 133.3 %pmax.7 = f32[512,1,4]{0,2,1:T(4,128)S(1)} all-reduce(f32[512,1,4]{0,2,1:T(4,128)S(1)} %bitcast.142), channel_id=1, replica_groups=mesh['ctx'=64,'tp'=8] {'ctx'}, use_global_device_ids=true, to_apply=%region_10.11 | all-reduce | flops 2048 | bytes 16384 | tf_op jit(solution)/shard_map/pmax | solution.py:79
  159.0 1.4 bitcast_multiply_fusion
  160.5 0.9 copy-done.3
  161.5 130.7 %psum.31 = f32[512,4]{0,1:T(4,128)S(1)} all-reduce(f32[512,4]{0,1:T(4,128)S(1)} %get-tuple-element.231), channel_id=1, replica_groups=mesh['ctx'=64,'tp'=8] {'ctx'}, use_global_device_ids=true, to_apply=%region_12.13 | all-reduce | flops 2048 | bytes 16384 | tf_op jit(solution)/shard_map/psum | solution.py:81
  292.2 0.9 maximum_bitcast_fusion.1
  293.2 0.7 copy-done.4
  293.9 105.3 %all-reduce.6.cloned.1.call-done = f32[512,1,4,128]{3,0,2,1:T(8,128)} async-done(((f32[512,1,4,128]{3,0,2,1:T(8,128)}), f32[512,1,4,128]{3,0,2,1:T(8,128)}) %all-reduce.6.cloned.1.call-update) | async-done | bytes 1048592 | tf_op jit(solution)/shard_map/psum | solution.py:81
  399.2 1.6 divide_convert_fusion
  401.0 1.0 fusion.33
  402.1 9.6 %while.27 = (s32[]{:T(128)}, bf16[2,128,512]{2,1,0:T(8,128)(2,1)S(1)}, s32[2]{0:T(128)S(1)}, pred[]{:T(512)}, bf16[256,1,4,128]{0,3,2,1:T(8,128)(2,1)S(1)}, /*in...) while((s32[]{:T(128)}, ...), condition=%wide.region_5.6_spmd, body=%wide.region_2.5_spmd.sunk | while | flops 136215680 | bytes 4402336 | solution.py:55
  402.1 0.6 dynamic_slice.37
  404.6 0.6 iota_add_fusion.6
  405.4 0.5 fusion.48
  406.3 0.5 fusion.50
  406.9 0.6 dynamic_slice.37
  409.4 0.6 iota_add_fusion.6
  410.2 0.5 fusion.48
  411.0 0.5 fusion.50
  411.7 23.0 %reduce-scatter.2.cloned.1.call-done = f32[64,64]{1,0:T(8,128)} async-done(((f32[512,64]{1,0:T(8,128)}), f32[64,64]{1,0:T(8,128)}) %reduce-scatter.2.cloned.1.call-update) | async-done | bytes 16400 | tf_op jit(solution)/shard_map/reduce_scatter | solution.py:85
  434.7 1.4 convert_element_type.23
  (70 shorter events, 5.0 us)
Async XLA Ops:
  7.2 393.8 %copy-start = (bf16[512,64]{0,1:T(8,128)(2,1)S(1)}, bf16[512,64]{0,1:T(8,128)(2,1)}, u32[]{:S(2)}) copy-start(bf16[512,64]{0,1:T(8,128)(2,1)} %param.17) | copy-start | bytes 196612
  7.2 285.0 %all-reduce.8.cloned.1.call-start = ((), (), s32[]{:S(2)}) async-start(), calls=%async_computation.3 | async-start | bytes 262144 | tf_op jit(solution)/shard_map/psum | solution.py:14
  7.9 391.3 %all-reduce.6.cloned.1.call-start = ((), (), s32[]{:S(2)}) async-start(), calls=%async_computation.1 | async-start | bytes 2097152 | tf_op jit(solution)/shard_map/psum | solution.py:81
  8.0 1.4 copy-start.1
  8.0 1.4 copy-start.2
  8.0 1.4 copy-start.5
  8.0 1.3 copy-start.6
  160.4 1.0 copy-start.3
  160.4 274.3 %reduce-scatter.2.cloned.1.call-start = ((), (), s32[]{:S(2)}) async-start(), calls=%async_computation.2 | async-start | bytes 294912 | tf_op jit(solution)/shard_map/reduce_scatter | solution.py:85
  293.1 0.8 copy-start.4
  411.7 24.4 %copy-start.7 = (bf16[2,128,512]{2,1,0:T(8,128)(2,1)}, bf16[2,128,512]{2,1,0:T(8,128)(2,1)S(1)}, u32[]{:S(2)}) copy-start(bf16[2,128,512]{2,1,0:T(8,128)(2,1)S(1)} %get-tuple-element.134) | copy-start | bytes 786436
Sparse Core Ops, SparseCore 0:
  12.1 190.6 all-reduce.7
  206.3 192.8 all-reduce.5
  402.2 32.4 reduce-scatter.1
where the time goes:
time: 448 us; the launch traced here: 443 us
  blocking collectives  264 us (59%)
  waiting for transfers between devices  128 us (29%)
  between operations  14 us (3%)
  loops' own time  11.8 us (3%)
  other arithmetic  11.2 us (2%)
  local copies, waits for them, and re-layouts  7.41 us (2%)
  matrix products  5.64 us (1%)
    pmax x1, blocking collectives, body(): highest = lax.pmax(local_top, 'ctx')  133 us
    psum x1, blocking collectives, body(): lax.psum((local_total * factor, local_sum * factor[..., None]), 'ctx')  131 us
    psum x1, waiting for transfers between devices, body(): lax.psum((local_total * factor, local_sum * factor[..., None]), 'ctx')  105 us
    reduce_scatter x1, waiting for transfers between devices, body(): lax.psum_scatter(jnp.dot(rows, out_weight, preferred_element_type=jnp.flo...  23 us
  transfers between devices with their start and end apart: 3, of which 2 were waited for; matrix products, arithmetic and copies ran while one was open for 4% of the time, Pallas kernels for 0%

commit v1 on v0

v1 whole, which is shorter than its diff:
```python
import jax
import jax.numpy as jnp
from jax import lax
from jax.experimental import pallas as pl
from jax.experimental.pallas import tpu as pltpu
from jax.sharding import Mesh
from jax.sharding import PartitionSpec as P

HD = 128
GROUP = 4
BLK = 256
QL = 512
SHARE = 8
PEERS = 32
HALF = QL // 2
SCALE = HD**-0.5
F32 = jnp.float32
BF16 = jnp.bfloat16

STATS = GROUP * HD
ANCHOR = STATS + HD
FIRST = ANCHOR + 2 * HD
SECOND = GROUP * HD + 2 * HD


def nt(a, b):
    return lax.dot_general(a, b, (((1,), (1,)), ((), ())), preferred_element_type=F32)


def nn(a, b):
    return lax.dot_general(a, b, (((1,), (0,)), ((), ())), preferred_element_type=F32)


def query_kernel(where, rows_ref, own_ref, mate_ref, out_ref):
    core, block, mate = where[0], where[1], where[2]
    rows = rows_ref[...].reshape(HALF, GROUP * HD)
    own_keys, own_values = own_ref[0:BLK, :], own_ref[BLK : 2 * BLK, :]
    mate_keys, mate_values = mate_ref[0:BLK, :], mate_ref[BLK : 2 * BLK, :]
    own_tail = own_ref[2 * BLK : 2 * BLK + 2 * SHARE, :].astype(F32)
    mate_tail = mate_ref[2 * BLK : 2 * BLK + 2 * SHARE, :].astype(F32)
    tail_keys = jnp.concatenate([own_tail[:SHARE], mate_tail[:SHARE]], 0).astype(BF16)
    tail_values = jnp.concatenate([own_tail[SHARE:], mate_tail[SHARE:]], 0).astype(BF16)

    index = lax.broadcasted_iota(jnp.int32, (HALF, 2 * SHARE), 0)
    position = (index // 32) * 64 + core * 32 + index % 32
    column = lax.broadcasted_iota(jnp.int32, (HALF, 2 * SHARE), 1)
    key_position = jnp.where(column < SHARE, block * SHARE + column, mate * SHARE + column - SHARE)
    visible = position >= key_position

    lane = lax.broadcasted_iota(jnp.int32, (HALF, HD), 1)
    stats = jnp.zeros((HALF, HD), F32)
    for h in range(GROUP):
        q = rows[:, h * HD : (h + 1) * HD]
        own = nt(q, own_keys) * SCALE
        other = nt(q, mate_keys) * SCALE
        tail = jnp.where(visible, nt(q, tail_keys) * SCALE, -jnp.inf)
        top = jnp.maximum(
            jnp.max(jnp.maximum(own, other), axis=-1, keepdims=True),
            jnp.max(tail, axis=-1, keepdims=True),
        )
        top = jnp.ceil(top * 0.5) * 2.0
        own, other, tail = jnp.exp(own - top), jnp.exp(other - top), jnp.exp(tail - top)
        total = jnp.sum(own + other, axis=-1, keepdims=True) + jnp.sum(tail, axis=-1, keepdims=True)
        summed = (
            nn(own.astype(BF16), own_values)
            + nn(other.astype(BF16), mate_values)
            + nn(tail.astype(BF16), tail_values)
        )
        out_ref[:, h * HD : (h + 1) * HD] = summed.astype(BF16)
        high = total.astype(BF16).astype(F32)
        stats = jnp.where(lane == h, top, stats)
        stats = jnp.where(lane == GROUP + h, high, stats)
        stats = jnp.where(lane == 2 * GROUP + h, total - high, stats)
    out_ref[:, STATS:ANCHOR] = stats.astype(BF16)

    @pl.when(core == 0)
    def _():
        out_ref[:, ANCHOR : ANCHOR + HD] = own_keys
        out_ref[:, ANCHOR + HD : FIRST] = own_values

    @pl.when(core != 0)
    def _():
        out_ref[:, ANCHOR : ANCHOR + HD] = mate_keys
        out_ref[:, ANCHOR + HD : FIRST] = mate_values


def query_parts(where, query_queries, own, mate):
    taken = 2 * BLK + 2 * SHARE
    return pl.pallas_call(
        query_kernel,
        out_shape=jax.ShapeDtypeStruct((HALF, FIRST), BF16),
        grid_spec=pltpu.PrefetchScalarGridSpec(
            num_scalar_prefetch=1,
            grid=(1,),
            in_specs=[
                pl.BlockSpec((8, 1, 32, GROUP * HD), lambda i, where: (0, where[0], 0, 0)),
                pl.BlockSpec((taken, HD), lambda i, where: (0, 0)),
                pl.BlockSpec((taken, HD), lambda i, where: (0, 0)),
            ],
            out_specs=pl.BlockSpec((HALF, FIRST), lambda i, where: (0, 0)),
        ),
        cost_estimate=pl.CostEstimate(
            flops=4 * HALF * GROUP * 2 * BLK * HD,
            transcendentals=HALF * GROUP * 2 * BLK,
            bytes_accessed=1 << 20,
        ),
        name="query_parts",
    )(where, query_queries.reshape(8, 2, 32, GROUP * HD), own, mate)


def merge_kernel(parts_ref, out_ref):
    stats = parts_ref[:, :, STATS:ANCHOR].astype(F32)
    factor = jnp.exp(stats - jnp.max(stats, axis=0, keepdims=True))
    for h in range(GROUP):
        weight = jnp.broadcast_to(factor[:, :, h : h + 1], (PEERS, SHARE, HD))
        totals = jnp.sum(weight * stats, axis=0)
        total = totals[:, GROUP + h : GROUP + h + 1] + totals[:, 2 * GROUP + h : 2 * GROUP + h + 1]
        part = parts_ref[:, :, h * HD : (h + 1) * HD].astype(F32)
        attended = (jnp.sum(weight * part, axis=0) / total).astype(BF16)
        out_ref[:, :, h * HD : (h + 1) * HD] = jnp.broadcast_to(attended[None], (PEERS, SHARE, HD))
    anchor = parts_ref[0, :, ANCHOR:FIRST]
    out_ref[:, :, GROUP * HD :] = jnp.broadcast_to(anchor[None], (PEERS, SHARE, 2 * HD))


def merge_parts(parts):
    return pl.pallas_call(
        merge_kernel,
        out_shape=jax.ShapeDtypeStruct((PEERS, SHARE, SECOND), BF16),
        name="merge_parts",
    )(parts)


def project_kernel(where, rows_ref, own_ref, mate_ref, out_ref):
    core = where[0]
    rows = rows_ref[:, :, : GROUP * HD].astype(F32).reshape(8, 2, 16, GROUP * HD)
    upper = rows[:, 0].reshape(128, GROUP * HD).astype(BF16)
    lower = rows[:, 1].reshape(128, GROUP * HD).astype(BF16)
    own, mate = own_ref[...], mate_ref[...]
    zero = jnp.zeros_like(own)

    def packed(weight):
        left = jnp.concatenate([weight, zero], 1)
        right = jnp.concatenate([zero, weight], 1)
        return (nn(upper, left) + nn(lower, right)).reshape(8, 16, 128)

    out_ref[pl.ds(core, 1)] = packed(own)[None]
    out_ref[pl.ds(1 - core, 1)] = packed(mate)[None]


def project(where, rows, own, mate):
    return pl.pallas_call(
        project_kernel,
        out_shape=jax.ShapeDtypeStruct((2, 8, 16, 128), F32),
        in_specs=[
            pl.BlockSpec(memory_space=pltpu.SMEM),
            pl.BlockSpec(memory_space=pltpu.VMEM),
            pl.BlockSpec(memory_space=pltpu.VMEM),
            pl.BlockSpec(memory_space=pltpu.VMEM),
        ],
        name="project",
    )(where, rows, own, mate)


def context_kernel(where, q_ref, keys_ref, values_ref, anchor_ref, out_ref):
    has_anchor = where[1] > 0
    anchor = anchor_ref[:, :, GROUP * HD :].astype(F32).reshape(BLK, 2 * HD).astype(BF16)
    anchor_keys, anchor_values = anchor[:, :HD], anchor[:, HD:]
    keys, values = keys_ref[...], values_ref[...]
    row = lax.broadcasted_iota(jnp.int32, (BLK, BLK), 0)
    column = lax.broadcasted_iota(jnp.int32, (BLK, BLK), 1)
    for h in range(GROUP):
        q = q_ref[:, h * HD : (h + 1) * HD]
        own = jnp.where(row >= column, nt(q, keys) * SCALE, -jnp.inf)
        first = jnp.where(has_anchor, nt(q, anchor_keys) * SCALE, -jnp.inf)
        top = jnp.max(jnp.maximum(own, first), axis=-1, keepdims=True)
        own, first = jnp.exp(own - top), jnp.exp(first - top)
        total = jnp.sum(own + first, axis=-1, keepdims=True)
        summed = nn(own.astype(BF16), values) + nn(first.astype(BF16), anchor_values)
        out_ref[:, h * HD : (h + 1) * HD] = (summed / total).astype(BF16)


def context(where, queries, keys, values, gathered):
    return pl.pallas_call(
        context_kernel,
        out_shape=jax.ShapeDtypeStruct((BLK, GROUP * HD), BF16),
        in_specs=[pl.BlockSpec(memory_space=pltpu.SMEM)]
        + [pl.BlockSpec(memory_space=pltpu.VMEM)] * 4,
        cost_estimate=pl.CostEstimate(
            flops=4 * BLK * GROUP * 2 * BLK * HD,
            transcendentals=BLK * GROUP * 2 * BLK,
            bytes_accessed=1 << 20,
        ),
        name="context",
    )(where, queries, keys, values, gathered)


def finish_kernel(parts_ref, out_ref):
    for k in range(2):
        summed = jnp.sum(parts_ref[k * 8 : (k + 1) * 8], axis=0)
        out_ref[k * 32 : k * 32 + 16, :] = summed[:, :64].astype(BF16)
        out_ref[k * 32 + 16 : k * 32 + 32, :] = summed[:, 64:].astype(BF16)


def finish(parts):
    return pl.pallas_call(
        finish_kernel, out_shape=jax.ShapeDtypeStruct((64, 64), BF16), name="finish"
    )(parts)


def body(ctx_queries, ctx_keys, ctx_values, query_queries, query_keys, query_values, out_weight):
    core = lax.axis_index("core")
    block = (lax.axis_index("z") * 4 + lax.axis_index("x")) * 2 + core
    mate_block = block + 1 - 2 * core
    where = jnp.stack([core, block, mate_block]).astype(jnp.int32)

    wide = jnp.pad(out_weight, ((0, 0), (0, 64)))
    own = jnp.concatenate([ctx_keys, ctx_values, query_keys, query_values, wide], 0)
    mate = lax.ppermute(own, "core", [(0, 1), (1, 0)])
    mate_weight = mate[2 * BLK + 2 * SHARE :, :64]

    parts = query_parts(where, query_queries, own, mate)
    parts = lax.all_to_all(parts.reshape(PEERS, SHARE, FIRST), ("z", "x"), 0, 0)
    message = merge_parts(parts)
    gathered = lax.all_to_all(message, ("z", "x"), 0, 0)

    sums = project(where, gathered, out_weight, mate_weight)
    sums = lax.all_to_all(sums.reshape(16, 16, 128), ("core", "tp"), 0, 0)
    ctx_out = context(where, ctx_queries, ctx_keys, ctx_values, gathered)
    query_out = finish(sums)
    return (ctx_out, query_out)


def solution(mesh):
    fine = Mesh(mesh.devices.reshape(8, 4, 2, 8), ("z", "x", "core", "tp"))
    ctx = ("z", "x", "core")
    return jax.shard_map(
        body,
        mesh=fine,
        in_specs=(
            P(ctx, "tp"),
            P(ctx, "tp"),
            P(ctx, "tp"),
            P(None, "tp"),
            P(ctx, "tp"),
            P(ctx, "tp"),
            P("tp", ctx),
        ),
        out_specs=(P(ctx, "tp"), P("tp", ctx)),
        check_vma=False,
    )
```

time: 448 us -> 85.3 us (0.19); the launches traced: 443 us -> 84.6 us
  blocking collectives: 264 us -> 23.1 us
  waiting for transfers between devices: 128 us -> 15.9 us
  starting transfers between devices: 0.12 us -> 24 us
  Pallas kernels: 0 us -> 13.4 us
  between operations: 14 us -> 0.72 us
  loops' own time: 11.8 us -> 0 us
  other arithmetic: 11.2 us -> 0.65 us
  matrix products: 5.64 us -> 0 us
    pmax x1 -> x0, blocking collectives: 133 us -> none  [body(): highest = lax.pmax(local_top, 'ctx')]
    psum x1 -> x0, blocking collectives: 131 us -> none  [body(): lax.psum((local_total * factor, local_sum * factor[..., None]), 'ctx')]
    psum x2 -> x0, waiting for transfers between devices: 105 us -> none  [the longest x1 105 us: body(): lax.psum((local_total * factor, local_sum * factor[..., None]), 'ctx')]
    all_to_all x0 -> x1, blocking collectives: none -> 23.1 us  [body(): parts = lax.all_to_all(parts.reshape(PEERS, SHARE, FIRST), ('z', 'x'), 0, 0)]
    reduce_scatter x1 -> x0, waiting for transfers between devices: 23 us -> none  [body(): lax.psum_scatter(jnp.dot(rows, out_weight, preferred_element_type=jnp.flo...]
    all_to_all x0 -> x2, waiting for transfers between devices: none -> 15.4 us  [the longest x1 11.3 us: body(): gathered = lax.all_to_all(message, ('z', 'x'), 0, 0)]
    all_to_all x0 -> x2, starting transfers between devices: none -> 15.2 us  [the longest x1 10.5 us: body(): sums = lax.all_to_all(sums.reshape(16, 16, 128), ('core', 'tp'), 0, 0)]
    pallas_call x0 -> x5, Pallas kernels: none -> 13.4 us  [the longest x1 4.28 us: query_parts(): pl.pallas_call(query_kernel, out_shape=jax.ShapeDtypeStruct((HALF, FIRST)...]
  transfers between devices with their start and end apart: 3 -> 3, of which waited for: 2 -> 3; matrix products, arithmetic and copies ran while one was open for 4% -> 3% of each run, Pallas kernels for 0% -> 4%
where the time goes in v1:
time: 85.3 us; the launch traced here: 84.6 us
  starting transfers between devices  24 us (28%)
  blocking collectives  23.1 us (27%)
  waiting for transfers between devices  15.9 us (19%)
  Pallas kernels  13.4 us (16%)
  local copies, waits for them, and re-layouts  6.94 us (8%)
    all_to_all x1, blocking collectives, body(): parts = lax.all_to_all(parts.reshape(PEERS, SHARE, FIRST), ('z', 'x'), 0, 0)  23.1 us
    all_to_all x1, waiting for transfers between devices, body(): gathered = lax.all_to_all(message, ('z', 'x'), 0, 0)  11.3 us
    all_to_all x1, starting transfers between devices, body(): sums = lax.all_to_all(sums.reshape(16, 16, 128), ('core', 'tp'), 0, 0)  10.5 us
    ppermute x1, starting transfers between devices, body(): mate = lax.ppermute(own, 'core', [(0, 1), (1, 0)])  8.79 us
    unnamed x23, local copies, waits for them, and re-layouts  5.34 us
    all_to_all x1, starting transfers between devices, body(): gathered = lax.all_to_all(message, ('z', 'x'), 0, 0)  4.74 us
    pallas_call x1, Pallas kernels, query_parts(): pl.pallas_call(query_kernel, out_shape=jax.ShapeDtypeStruct((HALF, FIRST)...  4.28 us
    all_to_all x1, waiting for transfers between devices, body(): sums = lax.all_to_all(sums.reshape(16, 16, 128), ('core', 'tp'), 0, 0)  4.06 us
  transfers between devices with their start and end apart: 3, of which 3 were waited for; matrix products, arithmetic and copies ran while one was open for 3% of the time, Pallas kernels for 4%

profile of v1, /device:TPU:1, one launch (start us, length us, event | category | flops | bytes accessed | tf_op | source)
XLA Modules:
  0.0 84.6 jit_solution(18442371722761354671)
XLA Ops:
  0.6 0.0 copy-start.5
  0.6 1.0 %copy.9.own_ref = bf16[512,64]{1,0:T(8,128)(2,1)S(1)} copy(bf16[512,64]{0,1:T(8,128)(2,1)} %param.13) | data formatting | bytes 131072 | tf_op args[6]
  1.6 0.0 copy-done.5
  1.6 0.0 copy-start.1
  1.7 0.0 copy-start.6
  1.7 0.9 %copy-done.6 = bf16[256,128]{1,0:T(8,128)(2,1)S(1)} copy-done((bf16[256,128]{1,0:T(8,128)(2,1)S(1)}, bf16[256,128]{1,0:T(8,128)(2,1)}, u32[]{:S(2)}) %copy-start.6) | copy-done | bytes 65560
  2.5 0.0 copy-start.7
  2.6 0.7 copy-done.7
  3.2 0.7 copy-done.8
  3.9 0.0 copy-done.1
  4.0 0.0 copy-start.4
  4.0 8.8 %collective-permute-start = (bf16[1040,128]{1,0:T(8,128)(2,1)S(1)}, bf16[1040,128]{1,0:T(8,128)(2,1)S(1)}, u32[]{:S(2)}, u32[]{:S(2)}) collective-permute-start(bf16[1040,128]{1,0:T(8,128)(2,1)S(1)} %pad_dynamic-update-slice_fusion.own_ref), channel_id=1, source_target_pairs={{0,8},{8,0},{1,9},{9,1},{2,10},{10,2},{3,11},{11,3},{4,12},{12,4},... | collective-permute-start | bytes 798728 | tf_op jit(solution)/shard_map/ppermute | solution.py:218
  12.8 0.7 pad_add_fusion.where
  13.4 0.5 collective-permute-done.mate_ref
  13.9 0.0 copy-start.2
  13.9 0.0 copy-done.4
  13.9 0.7 copy-done.2
  14.6 4.3 %query_parts.1 = bf16[256,896]{1,0:T(8,128)(2,1)} custom-call(s32[3]{0:T(128)} %pad_add_fusion.where, bf16[8,2,32,512]{3,2,1,0:T(8,128)(2,1)} %bitcast.7, bf16[1040,128]{1,0:T(8,128)(2,1)} %copy-done.4, bf16[1040,128]{1,0:T(8,128)(2,1)} %copy-done.2), custom_call_target="tpu_custom_call" | custom-call | flops 268435456 | bytes 1048576 | tf_op jit(solution)/shard_map/query_parts/pallas_call | solution.py:89
  18.9 23.1 %all_to_all.15.parts_ref = bf16[32,8,896]{2,1,0:T(8,128)(2,1)} all-to-all(bf16[32,8,896]{2,1,0:T(8,128)(2,1)} %bitcast.6), channel_id=1, replica_groups=mesh['z'=8,'x'=4,'core'=2,'tp'=8] {'z','x'}, dimensions={0} | all-to-all | bytes 917504 | tf_op jit(solution)/shard_map/all_to_all | solution.py:222
  42.0 2.1 %merge_parts.1 = bf16[32,8,768]{2,1,0:T(8,128)(2,1)} custom-call(bf16[32,8,896]{2,1,0:T(8,128)(2,1)} %all_to_all.15.parts_ref), custom_call_target="tpu_custom_call" | custom-call | tf_op jit(solution)/shard_map/merge_parts/pallas_call | solution.py:126
  44.1 4.7 %all-to-all-start.1 = ((bf16[32,8,768]{2,1,0:T(8,128)(2,1)}), bf16[32,8,768]{2,1,0:T(8,128)(2,1)S(1)}, u32[]{:S(2)}, u32[]{:S(2)}) async-start(bf16[32,8,768]{2,1,0:T(8,128)(2,1)} %merge_parts.1), calls=%async_computation.1 | async-start | bytes 786432 | tf_op jit(solution)/shard_map/all_to_all | solution.py:224
  48.9 1.6 %slice.4.mate_ref = bf16[512,64]{1,0:T(8,128)(2,1)} slice(bf16[1040,128]{1,0:T(8,128)(2,1)} %copy-done.2), slice={[528:1040], [0:64]} | slice | bytes 131072 | tf_op jit(solution)/shard_map/slice | solution.py:219
  50.4 11.3 %all-to-all-done.1.anchor_ref.rows_ref = bf16[32,8,768]{2,1,0:T(8,128)(2,1)S(1)} async-done(((bf16[32,8,768]{2,1,0:T(8,128)(2,1)}), bf16[32,8,768]{2,1,0:T(8,128)(2,1)S(1)}, u32[]{:S(2)}, u32[]{:S(2)}) %all-to-all-start.1) | async-done | bytes 393248 | tf_op jit(solution)/shard_map/all_to_all | solution.py:224
  61.8 0.0 copy-start
  61.8 0.7 copy-done
  62.5 2.1 %project.1 = f32[2,8,16,128]{3,2,1,0:T(8,128)} custom-call(s32[3]{0:T(128)} %pad_add_fusion.where, bf16[32,8,768]{2,1,0:T(8,128)(2,1)} %copy-done, bf16[512,64]{1,0:T(8,128)(2,1)} %copy-done.1, bf16[512,64]{1,0:T(8,128)(2,1)} %slice.4.mate_ref), custom_call_target="tpu_custom_call" | custom-call | tf_op jit(solution)/shard_map/project/pallas_call | solution.py:151
  64.6 10.5 %all-to-all-start.2 = ((f32[16,16,128]{2,1,0:T(8,128)}), f32[16,16,128]{2,1,0:T(8,128)S(1)}, u32[]{:S(2)}, u32[]{:S(2)}) async-start(f32[16,16,128]{2,1,0:T(8,128)} %bitcast.8), calls=%async_computation.2 | async-start | bytes 262144 | tf_op jit(solution)/shard_map/all_to_all | solution.py:227
  75.1 3.2 %context.1 = bf16[256,512]{1,0:T(8,128)(2,1)} custom-call(s32[3]{0:T(128)} %pad_add_fusion.where, bf16[256,512]{1,0:T(8,128)(2,1)} %q_ref.1, bf16[256,128]{1,0:T(8,128)(2,1)} %keys_ref.1, bf16[256,128]{1,0:T(8,128)(2,1)} %values_ref.1, bf16[32,8,768]{2,1,0:T(8,128)(2,1)} %copy-done), custom_call_target="tpu_custom_call" | custom-call | flops 268435456 | bytes 1048576 | tf_op jit(solution)/shard_map/context/pallas_call | solution.py:183
  78.3 4.1 %all-to-all-done.2.parts_ref = f32[16,16,128]{2,1,0:T(8,128)S(1)} async-done(((f32[16,16,128]{2,1,0:T(8,128)}), f32[16,16,128]{2,1,0:T(8,128)S(1)}, u32[]{:S(2)}, u32[]{:S(2)}) %all-to-all-start.2) | async-done | bytes 131104 | tf_op jit(solution)/shard_map/all_to_all | solution.py:227
  82.4 0.0 copy-start.3
  82.4 0.6 copy-done.3
  83.0 1.6 %finish.1 = bf16[64,64]{1,0:T(8,128)(2,1)} custom-call(f32[16,16,128]{2,1,0:T(8,128)} %copy-done.3), custom_call_target="tpu_custom_call" | custom-call | tf_op jit(solution)/shard_map/finish/pallas_call | solution.py:205
  (6 shorter events, 0.1 us)
Async XLA Ops:
  0.6 1.0 %copy-start.5 = (bf16[256,128]{1,0:T(8,128)(2,1)S(1)}, bf16[256,128]{1,0:T(8,128)(2,1)}, u32[]{:S(2)}) copy-start(bf16[256,128]{1,0:T(8,128)(2,1)} %keys_ref.1) | copy-start | bytes 196612
  1.6 2.3 %copy-start.1 = (bf16[512,64]{1,0:T(8,128)(2,1)}, bf16[512,64]{1,0:T(8,128)(2,1)S(1)}, u32[]{:S(2)}) copy-start(bf16[512,64]{1,0:T(8,128)(2,1)S(1)} %copy.9.own_ref) | copy-start | bytes 196612
  1.7 0.9 %copy-start.6 = (bf16[256,128]{1,0:T(8,128)(2,1)S(1)}, bf16[256,128]{1,0:T(8,128)(2,1)}, u32[]{:S(2)}) copy-start(bf16[256,128]{1,0:T(8,128)(2,1)} %values_ref.1) | copy-start | bytes 196612
  2.5 0.7 copy-start.7
  3.2 0.7 copy-start.8
  4.0 10.0 %copy-start.4 = (bf16[1040,128]{1,0:T(8,128)(2,1)}, bf16[1040,128]{1,0:T(8,128)(2,1)S(1)}, u32[]{:S(2)}) copy-start(bf16[1040,128]{1,0:T(8,128)(2,1)S(1)} %pad_dynamic-update-slice_fusion.own_ref) | copy-start | bytes 798724
  4.0 9.9 %collective-permute-start = (bf16[1040,128]{1,0:T(8,128)(2,1)S(1)}, bf16[1040,128]{1,0:T(8,128)(2,1)S(1)}, u32[]{:S(2)}, u32[]{:S(2)}) collective-permute-start(bf16[1040,128]{1,0:T(8,128)(2,1)S(1)} %pad_dynamic-update-slice_fusion.own_ref), channel_id=1, source_target_pairs={{0,8},{8,0},{1,9},{9,1},{2,10},{10,2},{3,11},{11,3},{4,12},{12,4},... | collective-permute-start | bytes 798728 | tf_op jit(solution)/shard_map/ppermute | solution.py:218
  13.9 0.7 copy-start.2
  44.1 17.6 %all-to-all-start.1 = ((bf16[32,8,768]{2,1,0:T(8,128)(2,1)}), bf16[32,8,768]{2,1,0:T(8,128)(2,1)S(1)}, u32[]{:S(2)}, u32[]{:S(2)}) async-start(bf16[32,8,768]{2,1,0:T(8,128)(2,1)} %merge_parts.1), calls=%async_computation.1 | async-start | bytes 786432 | tf_op jit(solution)/shard_map/all_to_all | solution.py:224
  61.8 0.7 copy-start
  64.6 17.7 %all-to-all-start.2 = ((f32[16,16,128]{2,1,0:T(8,128)}), f32[16,16,128]{2,1,0:T(8,128)S(1)}, u32[]{:S(2)}, u32[]{:S(2)}) async-start(f32[16,16,128]{2,1,0:T(8,128)} %bitcast.8), calls=%async_computation.2 | async-start | bytes 262144 | tf_op jit(solution)/shard_map/all_to_all | solution.py:227
  82.4 0.7 copy-start.3

commit v2 on v1

v2 whole, which is shorter than its diff:
```python
import jax
import jax.numpy as jnp
from jax import lax
from jax.experimental import pallas as pl
from jax.experimental.pallas import tpu as pltpu
from jax.sharding import Mesh
from jax.sharding import PartitionSpec as P

HD = 128
GROUP = 4
BLK = 256
QL = 512
SHARE = 8
PEERS = 32
HALF = QL // 2
SCALE = HD**-0.5
F32 = jnp.float32
BF16 = jnp.bfloat16

STATS = GROUP * HD
ANCHOR = STATS + HD
FIRST = ANCHOR + 2 * HD
SECOND = GROUP * HD + 2 * HD


TAIL = 2 * BLK
WEIGHT = TAIL + 2 * SHARE
PACKED = WEIGHT + GROUP * 64


def nt(a, b):
    return lax.dot_general(a, b, (((1,), (1,)), ((), ())), preferred_element_type=F32)


def nn(a, b):
    return lax.dot_general(a, b, (((1,), (0,)), ((), ())), preferred_element_type=F32)


def vmem(array):
    return pltpu.with_memory_space_constraint(array, pltpu.VMEM)


IN_VMEM = pl.BlockSpec(memory_space=pltpu.VMEM)


def position_of():
    core = lax.axis_index("core")
    return core, (lax.axis_index("z") * 4 + lax.axis_index("x")) * 2 + core


def pack_kernel(
    keys_ref, values_ref, query_keys_ref, query_values_ref, weight_ref, rows_ref, out_ref, half_ref
):
    out_ref[0:BLK, :] = keys_ref[...]
    out_ref[BLK : 2 * BLK, :] = values_ref[...]
    tail = jnp.concatenate([query_keys_ref[...].astype(F32), query_values_ref[...].astype(F32)], 0)
    out_ref[TAIL:WEIGHT, :] = tail.astype(BF16)
    for h in range(GROUP):
        start = WEIGHT + h * 64
        out_ref[start : start + 64, :] = weight_ref[:, h * HD : (h + 1) * HD]
    core, unused = position_of()
    half_ref[...] = rows_ref[:, pl.ds(core, 1)].reshape(HALF, GROUP * HD)


def pack(keys, values, query_keys, query_values, weight, rows):
    return pl.pallas_call(
        pack_kernel,
        out_shape=(pltpu.VMEM((PACKED, HD), BF16), pltpu.VMEM((HALF, GROUP * HD), BF16)),
        in_specs=[IN_VMEM] * 6,
        out_specs=(IN_VMEM, IN_VMEM),
        name="pack",
    )(keys, values, query_keys, query_values, weight, rows.reshape(8, 2, 32, GROUP * HD))


def query_kernel(rows_ref, own_ref, mate_ref, out_ref):
    core, block = position_of()
    mate = block + 1 - 2 * core
    rows = rows_ref[...]
    own_keys, own_values = own_ref[0:BLK, :], own_ref[BLK : 2 * BLK, :]
    mate_keys, mate_values = mate_ref[0:BLK, :], mate_ref[BLK : 2 * BLK, :]
    own_tail, mate_tail = own_ref[TAIL:WEIGHT, :].astype(F32), mate_ref[TAIL:WEIGHT, :].astype(F32)
    tail_keys = jnp.concatenate([own_tail[:SHARE], mate_tail[:SHARE]], 0).astype(BF16)
    tail_values = jnp.concatenate([own_tail[SHARE:], mate_tail[SHARE:]], 0).astype(BF16)

    index = lax.broadcasted_iota(jnp.int32, (HALF, 2 * SHARE), 0)
    position = (index // 32) * 64 + core * 32 + index % 32
    column = lax.broadcasted_iota(jnp.int32, (HALF, 2 * SHARE), 1)
    own_seen = (column < SHARE) & (position >= block * SHARE + column)
    mate_seen = (column >= SHARE) & (position >= mate * SHARE + column - SHARE)

    lane = lax.broadcasted_iota(jnp.int32, (HALF, HD), 1)
    stats = jnp.zeros((HALF, HD), F32)

    def attend(q, keys, values, tail, seen):
        scores = nt(q, keys) * SCALE
        tail = jnp.where(seen, tail, -jnp.inf)
        top = jnp.maximum(
            jnp.max(scores, axis=-1, keepdims=True), jnp.max(tail, axis=-1, keepdims=True)
        )
        weights, tail = jnp.exp(scores - top), jnp.exp(tail - top)
        total = jnp.sum(weights, axis=-1, keepdims=True) + jnp.sum(tail, axis=-1, keepdims=True)
        summed = nn(weights.astype(BF16), values) + nn(tail.astype(BF16), tail_values)
        return top, total, summed

    for h in range(GROUP):
        q = rows[:, h * HD : (h + 1) * HD]
        tail = nt(q, tail_keys) * SCALE
        top0, total0, summed0 = attend(q, own_keys, own_values, tail, own_seen)
        top1, total1, summed1 = attend(q, mate_keys, mate_values, tail, mate_seen)
        top = jnp.maximum(top0, top1)
        factor0, factor1 = jnp.exp(top0 - top), jnp.exp(top1 - top)
        out_ref[:, h * HD : (h + 1) * HD] = (summed0 * factor0 + summed1 * factor1).astype(BF16)
        total = total0 * factor0 + total1 * factor1
        first = top.astype(BF16).astype(F32)
        second = (top - first).astype(BF16).astype(F32)
        high = total.astype(BF16).astype(F32)
        terms = (first, second, top - first - second, high, total - high)
        for i, term in enumerate(terms):
            stats = jnp.where(lane == i * GROUP + h, term, stats)
    out_ref[:, STATS:ANCHOR] = stats.astype(BF16)

    @pl.when(core == 0)
    def _():
        out_ref[:, ANCHOR : ANCHOR + HD] = own_keys
        out_ref[:, ANCHOR + HD : FIRST] = own_values

    @pl.when(core != 0)
    def _():
        out_ref[:, ANCHOR : ANCHOR + HD] = mate_keys
        out_ref[:, ANCHOR + HD : FIRST] = mate_values


def query_parts(rows, own, mate):
    return pl.pallas_call(
        query_kernel,
        out_shape=pltpu.VMEM((HALF, FIRST), BF16),
        in_specs=[IN_VMEM] * 3,
        out_specs=IN_VMEM,
        name="query_parts",
    )(vmem(rows), vmem(own), vmem(mate))


def merge_kernel(parts_ref, out_ref):
    stats = parts_ref[:, :, STATS:ANCHOR].astype(F32)
    flat = stats.reshape(PEERS * SHARE, HD)
    top = flat + (pltpu.roll(flat, HD - GROUP, 1) + pltpu.roll(flat, HD - 2 * GROUP, 1))
    top = top.reshape(PEERS, SHARE, HD)
    factor = jnp.exp(top - jnp.max(top, axis=0, keepdims=True))
    for h in range(GROUP):
        weight = jnp.broadcast_to(factor[:, :, h : h + 1], (PEERS, SHARE, HD))
        totals = jnp.sum(weight * stats, axis=0)
        high, low = 3 * GROUP + h, 4 * GROUP + h
        total = totals[:, high : high + 1] + totals[:, low : low + 1]
        part = parts_ref[:, :, h * HD : (h + 1) * HD].astype(F32)
        attended = (jnp.sum(weight * part, axis=0) / total).astype(BF16)
        out_ref[:, :, h * HD : (h + 1) * HD] = jnp.broadcast_to(attended[None], (PEERS, SHARE, HD))
    anchor = parts_ref[0, :, ANCHOR:FIRST]
    out_ref[:, :, GROUP * HD :] = jnp.broadcast_to(anchor[None], (PEERS, SHARE, 2 * HD))


def merge_parts(parts):
    return pl.pallas_call(
        merge_kernel,
        out_shape=pltpu.VMEM((PEERS, SHARE, SECOND), BF16),
        in_specs=[IN_VMEM],
        out_specs=IN_VMEM,
        name="merge_parts",
    )(vmem(parts))


def project_kernel(rows_ref, own_ref, mate_ref, out_ref):
    core, unused = position_of()
    rows = rows_ref[:, :, : GROUP * HD].astype(F32).reshape(8, 2, 16, GROUP * HD)
    upper = rows[:, 0].reshape(128, GROUP * HD).astype(BF16)
    lower = rows[:, 1].reshape(128, GROUP * HD).astype(BF16)

    def packed(ref):
        pieces = [ref[WEIGHT + h * 64 : WEIGHT + (h + 1) * 64, :] for h in range(GROUP)]
        weight = jnp.concatenate(pieces, 1)
        zero = jnp.zeros_like(weight)
        left = jnp.concatenate([weight, zero], 0)
        right = jnp.concatenate([zero, weight], 0)
        return (nt(upper, left) + nt(lower, right)).reshape(8, 16, 128)

    out_ref[pl.ds(core, 1)] = packed(own_ref)[None]
    out_ref[pl.ds(1 - core, 1)] = packed(mate_ref)[None]


def project(rows, own, mate):
    return pl.pallas_call(
        project_kernel,
        out_shape=pltpu.VMEM((2, 8, 16, 128), F32),
        in_specs=[IN_VMEM] * 3,
        out_specs=IN_VMEM,
        name="project",
    )(vmem(rows), vmem(own), vmem(mate))


def context_kernel(q_ref, keys_ref, values_ref, anchor_ref, out_ref):
    has_anchor = position_of()[1] > 0
    anchor = anchor_ref[:, :, GROUP * HD :].astype(F32).reshape(BLK, 2 * HD).astype(BF16)
    anchor_keys, anchor_values = anchor[:, :HD], anchor[:, HD:]
    keys, values = keys_ref[...], values_ref[...]
    row = lax.broadcasted_iota(jnp.int32, (BLK, BLK), 0)
    column = lax.broadcasted_iota(jnp.int32, (BLK, BLK), 1)
    for h in range(GROUP):
        q = q_ref[:, h * HD : (h + 1) * HD]
        own = jnp.where(row >= column, nt(q, keys) * SCALE, -jnp.inf)
        first = jnp.where(has_anchor, nt(q, anchor_keys) * SCALE, -jnp.inf)
        top = jnp.max(jnp.maximum(own, first), axis=-1, keepdims=True)
        own, first = jnp.exp(own - top), jnp.exp(first - top)
        total = jnp.sum(own + first, axis=-1, keepdims=True)
        summed = nn(own.astype(BF16), values) + nn(first.astype(BF16), anchor_values)
        out_ref[:, h * HD : (h + 1) * HD] = (summed / total).astype(BF16)


def context(queries, keys, values, gathered):
    return pl.pallas_call(
        context_kernel,
        out_shape=jax.ShapeDtypeStruct((BLK, GROUP * HD), BF16),
        in_specs=[IN_VMEM] * 4,
        cost_estimate=pl.CostEstimate(
            flops=4 * BLK * GROUP * 2 * BLK * HD,
            transcendentals=BLK * GROUP * 2 * BLK,
            bytes_accessed=1 << 20,
        ),
        name="context",
    )(queries, keys, values, vmem(gathered))


def finish_kernel(parts_ref, out_ref):
    for k in range(2):
        summed = jnp.sum(parts_ref[k * 8 : (k + 1) * 8], axis=0)
        out_ref[k * 32 : k * 32 + 16, :] = summed[:, :64].astype(BF16)
        out_ref[k * 32 + 16 : k * 32 + 32, :] = summed[:, 64:].astype(BF16)


def finish(parts):
    return pl.pallas_call(
        finish_kernel,
        out_shape=jax.ShapeDtypeStruct((64, 64), BF16),
        in_specs=[IN_VMEM],
        name="finish",
    )(vmem(parts))


def body(ctx_queries, ctx_keys, ctx_values, query_queries, query_keys, query_values, out_weight):
    own, rows = pack(ctx_keys, ctx_values, query_keys, query_values, out_weight.T, query_queries)
    mate = lax.ppermute(own, "core", [(0, 1), (1, 0)])

    parts = query_parts(rows, own, mate)
    parts = lax.all_to_all(parts.reshape(PEERS, SHARE, FIRST), ("z", "x"), 0, 0)
    message = merge_parts(parts)
    gathered = lax.all_to_all(message, ("z", "x"), 0, 0)

    sums = project(gathered, own, mate)
    sums = lax.all_to_all(sums.reshape(16, 16, 128), ("core", "tp"), 0, 0)
    ctx_out = context(ctx_queries, ctx_keys, ctx_values, gathered)
    query_out = finish(sums)
    return (ctx_out, query_out)


def solution(mesh):
    fine = Mesh(mesh.devices.reshape(8, 4, 2, 8), ("z", "x", "core", "tp"))
    ctx = ("z", "x", "core")
    return jax.shard_map(
        body,
        mesh=fine,
        in_specs=(
            P(ctx, "tp"),
            P(ctx, "tp"),
            P(ctx, "tp"),
            P(None, "tp"),
            P(ctx, "tp"),
            P(ctx, "tp"),
            P("tp", ctx),
        ),
        out_specs=(P(ctx, "tp"), P("tp", ctx)),
        check_vma=False,
    )
```

time: 85.3 us -> 74.2 us (0.87)
  blocking collectives: 23.1 us -> 40.2 us
  waiting for transfers between devices: 15.9 us -> 5.26 us
  local copies, waits for them, and re-layouts: 6.94 us -> 0 us
  Pallas kernels: 13.4 us -> 8.51 us
  starting transfers between devices: 24 us -> 19.2 us
    all_to_all x0 -> x1, blocking collectives: none -> 17.4 us  [body(): gathered = lax.all_to_all(message, ('z', 'x'), 0, 0)]
    all_to_all x1 -> x0, waiting for transfers between devices: 11.3 us -> none  [body(): gathered = lax.all_to_all(message, ('z', 'x'), 0, 0)]
    unnamed x23 -> x0, local copies, waits for them, and re-layouts: 5.34 us -> none
    all_to_all x1 -> x0, starting transfers between devices: 4.74 us -> none  [body(): gathered = lax.all_to_all(message, ('z', 'x'), 0, 0)]
    pallas_call x3 -> x4, Pallas kernels: 8.54 us -> 4.74 us  [the longest x1 2.09 us: query_parts(): pl.pallas_call(query_kernel, out_shape=pltpu.VMEM((HALF, FIRST), BF16), i...]
    slice x1 -> x0, local copies, waits for them, and re-layouts: 1.56 us -> none  [body(): mate_weight = mate[2 * BLK + 2 * SHARE:, :64]]
    pallas_call x1, Pallas kernels: 1.59 us -> 0.69 us  [finish(): pl.pallas_call(finish_kernel, out_shape=jax.ShapeDtypeStruct((64, 64), BF...]
  transfers between devices with their start and end apart: 3 -> 2, of which waited for: 3 -> 2; matrix products, arithmetic and copies ran while one was open for 3% -> 0% of each run, Pallas kernels for 4% -> 4%
where the time goes in v2:
time: 74.2 us; the launch traced here: 73.9 us
  blocking collectives  40.2 us (54%)
  starting transfers between devices  19.2 us (26%)
  Pallas kernels  8.51 us (11%)
  waiting for transfers between devices  5.26 us (7%)
    all_to_all x1, blocking collectives, body(): parts = lax.all_to_all(parts.reshape(PEERS, SHARE, FIRST), ('z', 'x'), 0, 0)  22.8 us
    all_to_all x1, blocking collectives, body(): gathered = lax.all_to_all(message, ('z', 'x'), 0, 0)  17.4 us
    all_to_all x1, starting transfers between devices, body(): sums = lax.all_to_all(sums.reshape(16, 16, 128), ('core', 'tp'), 0, 0)  10.4 us
    ppermute x1, starting transfers between devices, body(): mate = lax.ppermute(own, 'core', [(0, 1), (1, 0)])  8.79 us
    all_to_all x1, waiting for transfers between devices, body(): sums = lax.all_to_all(sums.reshape(16, 16, 128), ('core', 'tp'), 0, 0)  4.2 us
    pallas_call x1, Pallas kernels, context(): pl.pallas_call(context_kernel, out_shape=jax.ShapeDtypeStruct((BLK, GROUP...  3.09 us
    pallas_call x1, Pallas kernels, query_parts(): pl.pallas_call(query_kernel, out_shape=pltpu.VMEM((HALF, FIRST), BF16), i...  2.09 us
  transfers between devices with their start and end apart: 2, of which 2 were waited for; matrix products, arithmetic and copies ran while one was open for 0% of the time, Pallas kernels for 4%

profile of v2, /device:TPU:1, one launch (start us, length us, event | category | flops | bytes accessed | tf_op | source)
XLA Modules:
  0.0 73.9 jit_solution(17425198612277451254)
XLA Ops:
  0.6 1.2 %pack.1 = (bf16[784,128]{1,0:T(8,128)(2,1)S(1)}, bf16[256,512]{1,0:T(8,128)(2,1)S(1)}) custom-call(bf16[256,128]{1,0:T(8,128)(2,1)} %keys_ref.3, bf16[256,128]{1,0:T(8,128)(2,1)} %values_ref.3, bf16[8,128]{1,0:T(8,128)(2,1)} %query_keys_ref.1, bf16[8,128]{1,0:T(8,128)(2,1)} %query_values_ref.1, bf16[64,512]{1,0:T(8,128)(2,1)} %bitcast.6, ...), custom_call_target="tpu_custom_call" | custom-call | tf_op jit(solution)/shard_map/pack/pallas_call | solution.py:66
  1.9 8.8 %collective-permute-start = (bf16[784,128]{1,0:T(8,128)(2,1)S(1)}, bf16[784,128]{1,0:T(8,128)(2,1)S(1)}, u32[]{:S(2)}, u32[]{:S(2)}) collective-permute-start(bf16[784,128]{1,0:T(8,128)(2,1)S(1)} %get-tuple-element.5.own_ref), channel_id=1, source_target_pairs={{0,8},{8,0},{1,9},{9,1},{2,10},{10,2},{3,11},{11,3},{4,12},{12,4},... | collective-permute-start | bytes 602120 | tf_op jit(solution)/shard_map/ppermute | solution.py:249
  10.7 1.1 %collective-permute-done.mate_ref = bf16[784,128]{1,0:T(8,128)(2,1)S(1)} collective-permute-done((bf16[784,128]{1,0:T(8,128)(2,1)S(1)}, bf16[784,128]{1,0:T(8,128)(2,1)S(1)}, u32[]{:S(2)}, u32[]{:S(2)}) %collective-permute-start) | collective-permute-done | bytes 200736 | tf_op jit(solution)/shard_map/ppermute | solution.py:249
  11.7 2.1 %query_parts.1 = bf16[256,896]{1,0:T(8,128)(2,1)S(1)} custom-call(bf16[256,512]{1,0:T(8,128)(2,1)S(1)} %get-tuple-element.4.rows_ref, bf16[784,128]{1,0:T(8,128)(2,1)S(1)} %get-tuple-element.5.own_ref, bf16[784,128]{1,0:T(8,128)(2,1)S(1)} %collective-permute-done.mate_ref), custom_call_target="tpu_custom_call" | custom-call | tf_op jit(solution)/shard_map/query_parts/pallas_call | solution.py:134
  13.8 22.8 %all_to_all.15.parts_ref = bf16[32,8,896]{2,1,0:T(8,128)(2,1)S(1)} all-to-all(bf16[32,8,896]{2,1,0:T(8,128)(2,1)S(1)} %bitcast.4), channel_id=1, replica_groups=mesh['z'=8,'x'=4,'core'=2,'tp'=8] {'z','x'}, dimensions={0} | all-to-all | bytes 917504 | tf_op jit(solution)/shard_map/all_to_all | solution.py:252
  36.6 0.5 merge_parts.1
  37.1 17.4 %all_to_all.16.anchor_ref.rows_ref = bf16[32,8,768]{2,1,0:T(8,128)(2,1)S(1)} all-to-all(bf16[32,8,768]{2,1,0:T(8,128)(2,1)S(1)} %merge_parts.1), channel_id=1, replica_groups=mesh['z'=8,'x'=4,'core'=2,'tp'=8] {'z','x'}, dimensions={0} | all-to-all | bytes 786432 | tf_op jit(solution)/shard_map/all_to_all | solution.py:254
  54.5 0.9 %project.1 = f32[2,8,16,128]{3,2,1,0:T(8,128)} custom-call(bf16[32,8,768]{2,1,0:T(8,128)(2,1)S(1)} %all_to_all.16.anchor_ref.rows_ref, bf16[784,128]{1,0:T(8,128)(2,1)S(1)} %get-tuple-element.5.own_ref, bf16[784,128]{1,0:T(8,128)(2,1)S(1)} %collective-permute-done.mate_ref), custom_call_target="tpu_custom_call" | custom-call | tf_op jit(solution)/shard_map/project/pallas_call | solution.py:190
  55.4 10.4 %all-to-all-start.2 = ((f32[16,16,128]{2,1,0:T(8,128)}), f32[16,16,128]{2,1,0:T(8,128)S(1)}, u32[]{:S(2)}, u32[]{:S(2)}) async-start(f32[16,16,128]{2,1,0:T(8,128)} %bitcast.3), calls=%async_computation.2 | async-start | bytes 262144 | tf_op jit(solution)/shard_map/all_to_all | solution.py:257
  65.9 3.1 %context.1 = bf16[256,512]{1,0:T(8,128)(2,1)} custom-call(bf16[256,512]{1,0:T(8,128)(2,1)} %q_ref.1, bf16[256,128]{1,0:T(8,128)(2,1)} %keys_ref.3, bf16[256,128]{1,0:T(8,128)(2,1)} %values_ref.3, bf16[32,8,768]{2,1,0:T(8,128)(2,1)S(1)} %all_to_all.16.anchor_ref.rows_ref), custom_call_target="tpu_custom_call" | custom-call | flops 268435456 | bytes 1048576 | tf_op jit(solution)/shard_map/context/pallas_call | solution.py:218
  69.0 4.2 %all-to-all-done.2.parts_ref = f32[16,16,128]{2,1,0:T(8,128)S(1)} async-done(((f32[16,16,128]{2,1,0:T(8,128)}), f32[16,16,128]{2,1,0:T(8,128)S(1)}, u32[]{:S(2)}, u32[]{:S(2)}) %all-to-all-start.2) | async-done | bytes 131104 | tf_op jit(solution)/shard_map/all_to_all | solution.py:257
  73.2 0.7 finish.1
Async XLA Ops:
  1.9 9.8 %collective-permute-start = (bf16[784,128]{1,0:T(8,128)(2,1)S(1)}, bf16[784,128]{1,0:T(8,128)(2,1)S(1)}, u32[]{:S(2)}, u32[]{:S(2)}) collective-permute-start(bf16[784,128]{1,0:T(8,128)(2,1)S(1)} %get-tuple-element.5.own_ref), channel_id=1, source_target_pairs={{0,8},{8,0},{1,9},{9,1},{2,10},{10,2},{3,11},{11,3},{4,12},{12,4},... | collective-permute-start | bytes 602120 | tf_op jit(solution)/shard_map/ppermute | solution.py:249
  55.4 17.7 %all-to-all-start.2 = ((f32[16,16,128]{2,1,0:T(8,128)}), f32[16,16,128]{2,1,0:T(8,128)S(1)}, u32[]{:S(2)}, u32[]{:S(2)}) async-start(f32[16,16,128]{2,1,0:T(8,128)} %bitcast.3), calls=%async_computation.2 | async-start | bytes 262144 | tf_op jit(solution)/shard_map/all_to_all | solution.py:257

commit v3 on v2

--- a/solution.py
+++ b/solution.py
@@ -168,9 +168,9 @@
     )(vmem(parts))
 
 
-def project_kernel(rows_ref, own_ref, mate_ref, out_ref):
-    core, unused = position_of()
-    rows = rows_ref[:, :, : GROUP * HD].astype(F32).reshape(8, 2, 16, GROUP * HD)
+def tail_kernel(gathered_ref, own_ref, mate_ref, q_ref, sums_ref, out_ref):
+    core, block = position_of()
+    rows = gathered_ref[:, :, : GROUP * HD].astype(F32).reshape(8, 2, 16, GROUP * HD)
     upper = rows[:, 0].reshape(128, GROUP * HD).astype(BF16)
     lower = rows[:, 1].reshape(128, GROUP * HD).astype(BF16)
 
@@ -182,25 +182,13 @@
         right = jnp.concatenate([zero, weight], 0)
         return (nt(upper, left) + nt(lower, right)).reshape(8, 16, 128)
 
-    out_ref[pl.ds(core, 1)] = packed(own_ref)[None]
-    out_ref[pl.ds(1 - core, 1)] = packed(mate_ref)[None]
-
-
-def project(rows, own, mate):
-    return pl.pallas_call(
-        project_kernel,
-        out_shape=pltpu.VMEM((2, 8, 16, 128), F32),
-        in_specs=[IN_VMEM] * 3,
-        out_specs=IN_VMEM,
-        name="project",
-    )(vmem(rows), vmem(own), vmem(mate))
-
-
-def context_kernel(q_ref, keys_ref, values_ref, anchor_ref, out_ref):
-    has_anchor = position_of()[1] > 0
-    anchor = anchor_ref[:, :, GROUP * HD :].astype(F32).reshape(BLK, 2 * HD).astype(BF16)
+    sums_ref[pl.ds(core, 1)] = packed(own_ref)[None]
+    sums_ref[pl.ds(1 - core, 1)] = packed(mate_ref)[None]
+
+    has_anchor = block > 0
+    anchor = gathered_ref[:, :, GROUP * HD :].astype(F32).reshape(BLK, 2 * HD).astype(BF16)
     anchor_keys, anchor_values = anchor[:, :HD], anchor[:, HD:]
-    keys, values = keys_ref[...], values_ref[...]
+    keys, values = own_ref[0:BLK, :], own_ref[BLK : 2 * BLK, :]
     row = lax.broadcasted_iota(jnp.int32, (BLK, BLK), 0)
     column = lax.broadcasted_iota(jnp.int32, (BLK, BLK), 1)
     for h in range(GROUP):
@@ -214,18 +202,17 @@
         out_ref[:, h * HD : (h + 1) * HD] = (summed / total).astype(BF16)
 
 
-def context(queries, keys, values, gathered):
-    return pl.pallas_call(
-        context_kernel,
-        out_shape=jax.ShapeDtypeStruct((BLK, GROUP * HD), BF16),
+def project_and_attend(gathered, own, mate, queries):
+    return pl.pallas_call(
+        tail_kernel,
+        out_shape=(
+            pltpu.VMEM((2, 8, 16, 128), F32),
+            jax.ShapeDtypeStruct((BLK, GROUP * HD), BF16),
+        ),
         in_specs=[IN_VMEM] * 4,
-        cost_estimate=pl.CostEstimate(
-            flops=4 * BLK * GROUP * 2 * BLK * HD,
-            transcendentals=BLK * GROUP * 2 * BLK,
-            bytes_accessed=1 << 20,
-        ),
-        name="context",
-    )(queries, keys, values, vmem(gathered))
+        out_specs=(IN_VMEM, IN_VMEM),
+        name="project_and_attend",
+    )(vmem(gathered), vmem(own), vmem(mate), vmem(queries))
 
 
 def finish_kernel(parts_ref, out_ref):
@@ -253,9 +240,8 @@
     message = merge_parts(parts)
     gathered = lax.all_to_all(message, ("z", "x"), 0, 0)
 
-    sums = project(gathered, own, mate)
+    sums, ctx_out = project_and_attend(gathered, own, mate, ctx_queries)
     sums = lax.all_to_all(sums.reshape(16, 16, 128), ("core", "tp"), 0, 0)
-    ctx_out = context(ctx_queries, ctx_keys, ctx_values, gathered)
     query_out = finish(sums)
     return (ctx_out, query_out)
 

time: 74.2 us -> 75.3 us (1.015)
  blocking collectives: 40.2 us -> 57.8 us
  starting transfers between devices: 19.2 us -> 8.79 us
  waiting for transfers between devices: 5.26 us -> 1.05 us
  Pallas kernels: 8.51 us -> 6.71 us
    all_to_all x0 -> x1, blocking collectives: none -> 17.5 us  [body(): sums = lax.all_to_all(sums.reshape(16, 16, 128), ('core', 'tp'), 0, 0)]
    all_to_all x1 -> x0, starting transfers between devices: 10.4 us -> none  [body(): sums = lax.all_to_all(sums.reshape(16, 16, 128), ('core', 'tp'), 0, 0)]
    all_to_all x1 -> x0, waiting for transfers between devices: 4.2 us -> none  [body(): sums = lax.all_to_all(sums.reshape(16, 16, 128), ('core', 'tp'), 0, 0)]
    pallas_call x2 -> x1, Pallas kernels: 4.03 us -> 2.23 us  [project_and_attend(): pl.pallas_call(tail_kernel, out_shape=(pltpu.VMEM((2, 8, 16, 128), F32),...]
  transfers between devices with their start and end apart: 2 -> 1, of which waited for: 2 -> 1; matrix products, arithmetic and copies ran while one was open for 0% -> 0% of each run, Pallas kernels for 4% -> 0%
where the time goes in v3:
time: 75.3 us; the launch traced here: 75.1 us
  blocking collectives  57.8 us (77%)
  starting transfers between devices  8.79 us (12%)
  Pallas kernels  6.71 us (9%)
  waiting for transfers between devices  1.05 us (1%)
    all_to_all x1, blocking collectives, body(): parts = lax.all_to_all(parts.reshape(PEERS, SHARE, FIRST), ('z', 'x'), 0, 0)  22.8 us
    all_to_all x1, blocking collectives, body(): gathered = lax.all_to_all(message, ('z', 'x'), 0, 0)  17.5 us
    all_to_all x1, blocking collectives, body(): sums = lax.all_to_all(sums.reshape(16, 16, 128), ('core', 'tp'), 0, 0)  17.5 us
    ppermute x1, starting transfers between devices, body(): mate = lax.ppermute(own, 'core', [(0, 1), (1, 0)])  8.79 us
    pallas_call x1, Pallas kernels, project_and_attend(): pl.pallas_call(tail_kernel, out_shape=(pltpu.VMEM((2, 8, 16, 128), F32),...  2.23 us
    pallas_call x1, Pallas kernels, query_parts(): pl.pallas_call(query_kernel, out_shape=pltpu.VMEM((HALF, FIRST), BF16), i...  2.09 us
  transfers between devices with their start and end apart: 1, of which 1 were waited for; matrix products, arithmetic and copies ran while one was open for 0% of the time, Pallas kernels for 0%

profile of v3, /device:TPU:1, one launch (start us, length us, event | category | flops | bytes accessed | tf_op | source)
XLA Modules:
  0.0 75.1 jit_solution(1503663749950646460)
XLA Ops:
  0.6 1.2 %pack.1 = (bf16[784,128]{1,0:T(8,128)(2,1)S(1)}, bf16[256,512]{1,0:T(8,128)(2,1)S(1)}) custom-call(bf16[256,128]{1,0:T(8,128)(2,1)} %keys_ref.1, bf16[256,128]{1,0:T(8,128)(2,1)} %values_ref.1, bf16[8,128]{1,0:T(8,128)(2,1)} %query_keys_ref.1, bf16[8,128]{1,0:T(8,128)(2,1)} %query_values_ref.1, bf16[64,512]{1,0:T(8,128)(2,1)} %bitcast.7, ...), custom_call_target="tpu_custom_call" | custom-call | tf_op jit(solution)/shard_map/pack/pallas_call | solution.py:66
  1.9 8.8 %collective-permute-start = (bf16[784,128]{1,0:T(8,128)(2,1)S(1)}, bf16[784,128]{1,0:T(8,128)(2,1)S(1)}, u32[]{:S(2)}, u32[]{:S(2)}) collective-permute-start(bf16[784,128]{1,0:T(8,128)(2,1)S(1)} %get-tuple-element.7.own_ref), channel_id=1, source_target_pairs={{0,8},{8,0},{1,9},{9,1},{2,10},{10,2},{3,11},{11,3},{4,12},{12,4},... | collective-permute-start | bytes 602120 | tf_op jit(solution)/shard_map/ppermute | solution.py:236
  10.7 1.1 %collective-permute-done.mate_ref = bf16[784,128]{1,0:T(8,128)(2,1)S(1)} collective-permute-done((bf16[784,128]{1,0:T(8,128)(2,1)S(1)}, bf16[784,128]{1,0:T(8,128)(2,1)S(1)}, u32[]{:S(2)}, u32[]{:S(2)}) %collective-permute-start) | collective-permute-done | bytes 200736 | tf_op jit(solution)/shard_map/ppermute | solution.py:236
  11.7 2.1 %query_parts.1 = bf16[256,896]{1,0:T(8,128)(2,1)S(1)} custom-call(bf16[256,512]{1,0:T(8,128)(2,1)S(1)} %get-tuple-element.6.rows_ref, bf16[784,128]{1,0:T(8,128)(2,1)S(1)} %get-tuple-element.7.own_ref, bf16[784,128]{1,0:T(8,128)(2,1)S(1)} %collective-permute-done.mate_ref), custom_call_target="tpu_custom_call" | custom-call | tf_op jit(solution)/shard_map/query_parts/pallas_call | solution.py:134
  13.8 22.8 %all_to_all.15.parts_ref = bf16[32,8,896]{2,1,0:T(8,128)(2,1)S(1)} all-to-all(bf16[32,8,896]{2,1,0:T(8,128)(2,1)S(1)} %bitcast.4), channel_id=1, replica_groups=mesh['z'=8,'x'=4,'core'=2,'tp'=8] {'z','x'}, dimensions={0} | all-to-all | bytes 917504 | tf_op jit(solution)/shard_map/all_to_all | solution.py:239
  36.6 0.5 merge_parts.1
  37.1 0.0 copy-start
  37.1 17.5 %all_to_all.16.gathered_ref = bf16[32,8,768]{2,1,0:T(8,128)(2,1)S(1)} all-to-all(bf16[32,8,768]{2,1,0:T(8,128)(2,1)S(1)} %merge_parts.1), channel_id=1, replica_groups=mesh['z'=8,'x'=4,'core'=2,'tp'=8] {'z','x'}, dimensions={0} | all-to-all | bytes 786432 | tf_op jit(solution)/shard_map/all_to_all | solution.py:241
  54.6 0.0 copy-done
  54.6 2.2 %project_and_attend.1 = (f32[2,8,16,128]{3,2,1,0:T(8,128)S(1)}, bf16[256,512]{1,0:T(8,128)(2,1)}) custom-call(bf16[32,8,768]{2,1,0:T(8,128)(2,1)S(1)} %all_to_all.16.gathered_ref, bf16[784,128]{1,0:T(8,128)(2,1)S(1)} %get-tuple-element.7.own_ref, bf16[784,128]{1,0:T(8,128)(2,1)S(1)} %collective-permute-done.mate_ref, bf16[256,512]{1,0:T(8,128)(2,1)S(1)} %copy-done), custom_call_target="tpu_custom_call" | custom-call | tf_op jit(solution)/shard_map/project_and_attend/pallas_call | solution.py:206
  56.9 17.5 %all_to_all.17.parts_ref = f32[16,16,128]{2,1,0:T(8,128)S(1)} all-to-all(f32[16,16,128]{2,1,0:T(8,128)S(1)} %bitcast.5), channel_id=1, replica_groups=mesh['z'=8,'x'=4,'core'=2,'tp'=8] {'core','tp'}, dimensions={0} | all-to-all | bytes 262144 | tf_op jit(solution)/shard_map/all_to_all | solution.py:244
  74.4 0.7 finish.1
Async XLA Ops:
  1.9 9.8 %collective-permute-start = (bf16[784,128]{1,0:T(8,128)(2,1)S(1)}, bf16[784,128]{1,0:T(8,128)(2,1)S(1)}, u32[]{:S(2)}, u32[]{:S(2)}) collective-permute-start(bf16[784,128]{1,0:T(8,128)(2,1)S(1)} %get-tuple-element.7.own_ref), channel_id=1, source_target_pairs={{0,8},{8,0},{1,9},{9,1},{2,10},{10,2},{3,11},{11,3},{4,12},{12,4},... | collective-permute-start | bytes 602120 | tf_op jit(solution)/shard_map/ppermute | solution.py:236
  37.1 17.6 %copy-start = (bf16[256,512]{1,0:T(8,128)(2,1)S(1)}, bf16[256,512]{1,0:T(8,128)(2,1)}, u32[]{:S(2)}) copy-start(bf16[256,512]{1,0:T(8,128)(2,1)} %q_ref.1) | copy-start | bytes 786436

commit v4 on v2

--- a/solution.py
+++ b/solution.py
@@ -19,10 +19,8 @@
 
 STATS = GROUP * HD
 ANCHOR = STATS + HD
-FIRST = ANCHOR + 2 * HD
+FIRST = ANCHOR + HD
 SECOND = GROUP * HD + 2 * HD
-
-
 TAIL = 2 * BLK
 WEIGHT = TAIL + 2 * SHARE
 PACKED = WEIGHT + GROUP * 64
@@ -121,13 +119,11 @@
 
     @pl.when(core == 0)
     def _():
-        out_ref[:, ANCHOR : ANCHOR + HD] = own_keys
-        out_ref[:, ANCHOR + HD : FIRST] = own_values
+        out_ref[:, ANCHOR:FIRST] = own_keys
 
     @pl.when(core != 0)
     def _():
-        out_ref[:, ANCHOR : ANCHOR + HD] = mate_keys
-        out_ref[:, ANCHOR + HD : FIRST] = mate_values
+        out_ref[:, ANCHOR:FIRST] = mate_values
 
 
 def query_parts(rows, own, mate):
@@ -154,8 +150,9 @@
         part = parts_ref[:, :, h * HD : (h + 1) * HD].astype(F32)
         attended = (jnp.sum(weight * part, axis=0) / total).astype(BF16)
         out_ref[:, :, h * HD : (h + 1) * HD] = jnp.broadcast_to(attended[None], (PEERS, SHARE, HD))
-    anchor = parts_ref[0, :, ANCHOR:FIRST]
-    out_ref[:, :, GROUP * HD :] = jnp.broadcast_to(anchor[None], (PEERS, SHARE, 2 * HD))
+    anchor = jnp.broadcast_to(parts_ref[0, :, ANCHOR:FIRST][None], (PEERS, SHARE, HD))
+    out_ref[:, :, GROUP * HD : (GROUP + 1) * HD] = anchor
+    out_ref[:, :, (GROUP + 1) * HD :] = anchor
 
 
 def merge_parts(parts):
@@ -168,7 +165,7 @@
     )(vmem(parts))
 
 
-def project_kernel(rows_ref, own_ref, mate_ref, out_ref):
+def project_kernel(rows_ref, own_ref, mate_ref, out_ref, half_ref):
     core, unused = position_of()
     rows = rows_ref[:, :, : GROUP * HD].astype(F32).reshape(8, 2, 16, GROUP * HD)
     upper = rows[:, 0].reshape(128, GROUP * HD).astype(BF16)
@@ -184,23 +181,27 @@
 
     out_ref[pl.ds(core, 1)] = packed(own_ref)[None]
     out_ref[pl.ds(1 - core, 1)] = packed(mate_ref)[None]
+    half = rows_ref[:, :, GROUP * HD : (GROUP + 1) * HD].astype(F32)
+    half_ref[...] = half.reshape(BLK, HD).astype(BF16)
 
 
 def project(rows, own, mate):
     return pl.pallas_call(
         project_kernel,
-        out_shape=pltpu.VMEM((2, 8, 16, 128), F32),
+        out_shape=(pltpu.VMEM((2, 8, 16, 128), F32), pltpu.VMEM((BLK, HD), BF16)),
         in_specs=[IN_VMEM] * 3,
-        out_specs=IN_VMEM,
+        out_specs=(IN_VMEM, IN_VMEM),
         name="project",
     )(vmem(rows), vmem(own), vmem(mate))
 
 
-def context_kernel(q_ref, keys_ref, values_ref, anchor_ref, out_ref):
-    has_anchor = position_of()[1] > 0
-    anchor = anchor_ref[:, :, GROUP * HD :].astype(F32).reshape(BLK, 2 * HD).astype(BF16)
-    anchor_keys, anchor_values = anchor[:, :HD], anchor[:, HD:]
-    keys, values = keys_ref[...], values_ref[...]
+def context_kernel(q_ref, own_ref, half_ref, other_ref, out_ref):
+    core, block = position_of()
+    has_anchor = block > 0
+    half, other = half_ref[...].astype(F32), other_ref[...].astype(F32)
+    anchor_keys = jnp.where(core == 0, half, other).astype(BF16)
+    anchor_values = jnp.where(core == 0, other, half).astype(BF16)
+    keys, values = own_ref[0:BLK, :], own_ref[BLK : 2 * BLK, :]
     row = lax.broadcasted_iota(jnp.int32, (BLK, BLK), 0)
     column = lax.broadcasted_iota(jnp.int32, (BLK, BLK), 1)
     for h in range(GROUP):
@@ -214,7 +215,7 @@
         out_ref[:, h * HD : (h + 1) * HD] = (summed / total).astype(BF16)
 
 
-def context(queries, keys, values, gathered):
+def context(queries, own, half, other):
     return pl.pallas_call(
         context_kernel,
         out_shape=jax.ShapeDtypeStruct((BLK, GROUP * HD), BF16),
@@ -225,7 +226,7 @@
             bytes_accessed=1 << 20,
         ),
         name="context",
-    )(queries, keys, values, vmem(gathered))
+    )(vmem(queries), vmem(own), vmem(half), vmem(other))
 
 
 def finish_kernel(parts_ref, out_ref):
@@ -253,9 +254,10 @@
     message = merge_parts(parts)
     gathered = lax.all_to_all(message, ("z", "x"), 0, 0)
 
-    sums = project(gathered, own, mate)
+    sums, half = project(gathered, own, mate)
     sums = lax.all_to_all(sums.reshape(16, 16, 128), ("core", "tp"), 0, 0)
-    ctx_out = context(ctx_queries, ctx_keys, ctx_values, gathered)
+    other = lax.ppermute(half, "core", [(0, 1), (1, 0)])
+    ctx_out = context(ctx_queries, own, half, other)
     query_out = finish(sums)
     return (ctx_out, query_out)
 

time: 74.2 us -> 73 us (0.984)
  starting transfers between devices: 19.2 us -> 21.4 us
  blocking collectives: 40.2 us -> 38.8 us
  waiting for transfers between devices: 5.26 us -> 4.22 us
  Pallas kernels: 8.51 us -> 7.55 us
    all_to_all x1, waiting for transfers between devices: 4.2 us -> 2.04 us  [body(): sums = lax.all_to_all(sums.reshape(16, 16, 128), ('core', 'tp'), 0, 0)]
    ppermute x0 -> x1, starting transfers between devices: none -> 2 us  [body(): other = lax.ppermute(half, 'core', [(0, 1), (1, 0)])]
    all_to_all x1, blocking collectives: 22.8 us -> 21.2 us  [body(): parts = lax.all_to_all(parts.reshape(PEERS, SHARE, FIRST), ('z', 'x'), 0, 0)]
    ppermute x0 -> x1, waiting for transfers between devices: none -> 1.12 us  [body(): other = lax.ppermute(half, 'core', [(0, 1), (1, 0)])]
    pallas_call x1, Pallas kernels: 3.09 us -> 2.11 us  [context(): pl.pallas_call(context_kernel, out_shape=jax.ShapeDtypeStruct((BLK, GROUP...]
  transfers between devices with their start and end apart: 2 -> 3, of which waited for: 2 -> 3; matrix products, arithmetic and copies ran while one was open for 0% -> 0% of each run, Pallas kernels for 4% -> 3%
where the time goes in v4:
time: 73 us; the launch traced here: 72.7 us
  blocking collectives  38.8 us (53%)
  starting transfers between devices  21.4 us (29%)
  Pallas kernels  7.55 us (10%)
  waiting for transfers between devices  4.22 us (6%)
    all_to_all x1, blocking collectives, body(): parts = lax.all_to_all(parts.reshape(PEERS, SHARE, FIRST), ('z', 'x'), 0, 0)  21.2 us
    all_to_all x1, blocking collectives, body(): gathered = lax.all_to_all(message, ('z', 'x'), 0, 0)  17.6 us
    all_to_all x1, starting transfers between devices, body(): sums = lax.all_to_all(sums.reshape(16, 16, 128), ('core', 'tp'), 0, 0)  10.6 us
    ppermute x1, starting transfers between devices, body(): mate = lax.ppermute(own, 'core', [(0, 1), (1, 0)])  8.79 us
    pallas_call x1, Pallas kernels, context(): pl.pallas_call(context_kernel, out_shape=jax.ShapeDtypeStruct((BLK, GROUP...  2.11 us
    pallas_call x1, Pallas kernels, query_parts(): pl.pallas_call(query_kernel, out_shape=pltpu.VMEM((HALF, FIRST), BF16), i...  2.1 us
    all_to_all x1, waiting for transfers between devices, body(): sums = lax.all_to_all(sums.reshape(16, 16, 128), ('core', 'tp'), 0, 0)  2.04 us
    ppermute x1, starting transfers between devices, body(): other = lax.ppermute(half, 'core', [(0, 1), (1, 0)])  2 us
  transfers between devices with their start and end apart: 3, of which 3 were waited for; matrix products, arithmetic and copies ran while one was open for 0% of the time, Pallas kernels for 3%

profile of v4, /device:TPU:1, one launch (start us, length us, event | category | flops | bytes accessed | tf_op | source)
XLA Modules:
  0.0 72.7 jit_solution(6931271368197713789)
XLA Ops:
  0.6 1.2 %pack.1 = (bf16[784,128]{1,0:T(8,128)(2,1)S(1)}, bf16[256,512]{1,0:T(8,128)(2,1)S(1)}) custom-call(bf16[256,128]{1,0:T(8,128)(2,1)} %keys_ref.1, bf16[256,128]{1,0:T(8,128)(2,1)} %values_ref.1, bf16[8,128]{1,0:T(8,128)(2,1)} %query_keys_ref.1, bf16[8,128]{1,0:T(8,128)(2,1)} %query_values_ref.1, bf16[64,512]{1,0:T(8,128)(2,1)} %bitcast.6, ...), custom_call_target="tpu_custom_call" | custom-call | tf_op jit(solution)/shard_map/pack/pallas_call | solution.py:64
  1.9 8.8 %collective-permute-start = (bf16[784,128]{1,0:T(8,128)(2,1)S(1)}, bf16[784,128]{1,0:T(8,128)(2,1)S(1)}, u32[]{:S(2)}, u32[]{:S(2)}) collective-permute-start(bf16[784,128]{1,0:T(8,128)(2,1)S(1)} %get-tuple-element.6.own_ref), channel_id=1, source_target_pairs={{0,8},{8,0},{1,9},{9,1},{2,10},{10,2},{3,11},{11,3},{4,12},{12,4},... | collective-permute-start | bytes 602120 | tf_op jit(solution)/shard_map/ppermute | solution.py:250
  10.7 1.1 %collective-permute-done.mate_ref = bf16[784,128]{1,0:T(8,128)(2,1)S(1)} collective-permute-done((bf16[784,128]{1,0:T(8,128)(2,1)S(1)}, bf16[784,128]{1,0:T(8,128)(2,1)S(1)}, u32[]{:S(2)}, u32[]{:S(2)}) %collective-permute-start) | collective-permute-done | bytes 200736 | tf_op jit(solution)/shard_map/ppermute | solution.py:250
  11.7 2.1 %query_parts.1 = bf16[256,768]{1,0:T(8,128)(2,1)S(1)} custom-call(bf16[256,512]{1,0:T(8,128)(2,1)S(1)} %get-tuple-element.7.rows_ref, bf16[784,128]{1,0:T(8,128)(2,1)S(1)} %get-tuple-element.6.own_ref, bf16[784,128]{1,0:T(8,128)(2,1)S(1)} %collective-permute-done.mate_ref), custom_call_target="tpu_custom_call" | custom-call | tf_op jit(solution)/shard_map/query_parts/pallas_call | solution.py:130
  13.8 21.2 %all_to_all.15.parts_ref = bf16[32,8,768]{2,1,0:T(8,128)(2,1)S(1)} all-to-all(bf16[32,8,768]{2,1,0:T(8,128)(2,1)S(1)} %bitcast.4), channel_id=1, replica_groups=mesh['z'=8,'x'=4,'core'=2,'tp'=8] {'z','x'}, dimensions={0} | all-to-all | bytes 786432 | tf_op jit(solution)/shard_map/all_to_all | solution.py:253
  35.0 0.5 merge_parts.1
  35.5 17.6 %all_to_all.16.rows_ref = bf16[32,8,768]{2,1,0:T(8,128)(2,1)S(1)} all-to-all(bf16[32,8,768]{2,1,0:T(8,128)(2,1)S(1)} %merge_parts.1), channel_id=1, replica_groups=mesh['z'=8,'x'=4,'core'=2,'tp'=8] {'z','x'}, dimensions={0} | all-to-all | bytes 786432 | tf_op jit(solution)/shard_map/all_to_all | solution.py:255
  53.1 0.9 %project.1 = (f32[2,8,16,128]{3,2,1,0:T(8,128)}, bf16[256,128]{1,0:T(8,128)(2,1)S(1)}) custom-call(bf16[32,8,768]{2,1,0:T(8,128)(2,1)S(1)} %all_to_all.16.rows_ref, bf16[784,128]{1,0:T(8,128)(2,1)S(1)} %get-tuple-element.6.own_ref, bf16[784,128]{1,0:T(8,128)(2,1)S(1)} %collective-permute-done.mate_ref), custom_call_target="tpu_custom_call" | custom-call | tf_op jit(solution)/shard_map/project/pallas_call | solution.py:189
  54.1 0.0 copy-start
  54.1 10.6 %all-to-all-start.2 = ((f32[16,16,128]{2,1,0:T(8,128)}), f32[16,16,128]{2,1,0:T(8,128)S(1)}, u32[]{:S(2)}, u32[]{:S(2)}) async-start(f32[16,16,128]{2,1,0:T(8,128)} %bitcast.3), calls=%async_computation.2 | async-start | bytes 262144 | tf_op jit(solution)/shard_map/all_to_all | solution.py:258
  64.7 2.0 %collective-permute-start.1 = (bf16[256,128]{1,0:T(8,128)(2,1)S(1)}, bf16[256,128]{1,0:T(8,128)(2,1)S(1)}, u32[]{:S(2)}, u32[]{:S(2)}) collective-permute-start(bf16[256,128]{1,0:T(8,128)(2,1)S(1)} %get-tuple-element.8.half_ref), channel_id=1, source_target_pairs={{0,8},{8,0},{1,9},{9,1},{2,10},{10,2},{3,11},{11,3},{4,12},{12,4},... | collective-permute-start | bytes 196616 | tf_op jit(solution)/shard_map/ppermute | solution.py:259
  66.7 1.1 %collective-permute-done.1.other_ref = bf16[256,128]{1,0:T(8,128)(2,1)S(1)} collective-permute-done((bf16[256,128]{1,0:T(8,128)(2,1)S(1)}, bf16[256,128]{1,0:T(8,128)(2,1)S(1)}, u32[]{:S(2)}, u32[]{:S(2)}) %collective-permute-start.1) | collective-permute-done | bytes 65568 | tf_op jit(solution)/shard_map/ppermute | solution.py:259
  67.9 0.0 copy-done
  67.9 2.1 %context.1 = bf16[256,512]{1,0:T(8,128)(2,1)} custom-call(bf16[256,512]{1,0:T(8,128)(2,1)S(1)} %copy-done, bf16[784,128]{1,0:T(8,128)(2,1)S(1)} %get-tuple-element.6.own_ref, bf16[256,128]{1,0:T(8,128)(2,1)S(1)} %get-tuple-element.8.half_ref, bf16[256,128]{1,0:T(8,128)(2,1)S(1)} %collective-permute-done.1.other_ref), custom_call_target="tpu_custom_call" | custom-call | flops 268435456 | bytes 1048576 | tf_op jit(solution)/shard_map/context/pallas_call | solution.py:219
  70.0 2.0 %all-to-all-done.2.parts_ref = f32[16,16,128]{2,1,0:T(8,128)S(1)} async-done(((f32[16,16,128]{2,1,0:T(8,128)}), f32[16,16,128]{2,1,0:T(8,128)S(1)}, u32[]{:S(2)}, u32[]{:S(2)}) %all-to-all-start.2) | async-done | bytes 131104 | tf_op jit(solution)/shard_map/all_to_all | solution.py:258
  72.0 0.7 finish.1
Async XLA Ops:
  1.9 9.8 %collective-permute-start = (bf16[784,128]{1,0:T(8,128)(2,1)S(1)}, bf16[784,128]{1,0:T(8,128)(2,1)S(1)}, u32[]{:S(2)}, u32[]{:S(2)}) collective-permute-start(bf16[784,128]{1,0:T(8,128)(2,1)S(1)} %get-tuple-element.6.own_ref), channel_id=1, source_target_pairs={{0,8},{8,0},{1,9},{9,1},{2,10},{10,2},{3,11},{11,3},{4,12},{12,4},... | collective-permute-start | bytes 602120 | tf_op jit(solution)/shard_map/ppermute | solution.py:250
  54.1 13.8 %copy-start = (bf16[256,512]{1,0:T(8,128)(2,1)S(1)}, bf16[256,512]{1,0:T(8,128)(2,1)}, u32[]{:S(2)}) copy-start(bf16[256,512]{1,0:T(8,128)(2,1)} %q_ref.1) | copy-start | bytes 786436
  54.1 17.9 %all-to-all-start.2 = ((f32[16,16,128]{2,1,0:T(8,128)}), f32[16,16,128]{2,1,0:T(8,128)S(1)}, u32[]{:S(2)}, u32[]{:S(2)}) async-start(f32[16,16,128]{2,1,0:T(8,128)} %bitcast.3), calls=%async_computation.2 | async-start | bytes 262144 | tf_op jit(solution)/shard_map/all_to_all | solution.py:258
  64.7 3.1 %collective-permute-start.1 = (bf16[256,128]{1,0:T(8,128)(2,1)S(1)}, bf16[256,128]{1,0:T(8,128)(2,1)S(1)}, u32[]{:S(2)}, u32[]{:S(2)}) collective-permute-start(bf16[256,128]{1,0:T(8,128)(2,1)S(1)} %get-tuple-element.8.half_ref), channel_id=1, source_target_pairs={{0,8},{8,0},{1,9},{9,1},{2,10},{10,2},{3,11},{11,3},{4,12},{12,4},... | collective-permute-start | bytes 196616 | tf_op jit(solution)/shard_map/ppermute | solution.py:259

commit v5 on v4

--- a/solution.py
+++ b/solution.py
@@ -70,41 +70,59 @@
     )(keys, values, query_keys, query_values, weight, rows.reshape(8, 2, 32, GROUP * HD))
 
 
-def query_kernel(rows_ref, own_ref, mate_ref, out_ref):
-    core, block = position_of()
-    mate = block + 1 - 2 * core
+def attend_block(rows_ref, pack_ref, core, block):
     rows = rows_ref[...]
-    own_keys, own_values = own_ref[0:BLK, :], own_ref[BLK : 2 * BLK, :]
-    mate_keys, mate_values = mate_ref[0:BLK, :], mate_ref[BLK : 2 * BLK, :]
-    own_tail, mate_tail = own_ref[TAIL:WEIGHT, :].astype(F32), mate_ref[TAIL:WEIGHT, :].astype(F32)
-    tail_keys = jnp.concatenate([own_tail[:SHARE], mate_tail[:SHARE]], 0).astype(BF16)
-    tail_values = jnp.concatenate([own_tail[SHARE:], mate_tail[SHARE:]], 0).astype(BF16)
-
+    keys, values = pack_ref[0:BLK, :], pack_ref[BLK : 2 * BLK, :]
+    tail_keys = pack_ref[TAIL:WEIGHT, :]
+    tail = tail_keys.astype(F32)
+    tail_values = jnp.concatenate([tail[SHARE:], tail[:SHARE]], 0).astype(BF16)
     index = lax.broadcasted_iota(jnp.int32, (HALF, 2 * SHARE), 0)
     position = (index // 32) * 64 + core * 32 + index % 32
     column = lax.broadcasted_iota(jnp.int32, (HALF, 2 * SHARE), 1)
-    own_seen = (column < SHARE) & (position >= block * SHARE + column)
-    mate_seen = (column >= SHARE) & (position >= mate * SHARE + column - SHARE)
-
+    seen = (column < SHARE) & (position >= block * SHARE + column)
+    parts = []
+    for h in range(GROUP):
+        q = rows[:, h * HD : (h + 1) * HD]
+        scores = nt(q, keys) * SCALE
+        last = jnp.where(seen, nt(q, tail_keys) * SCALE, -jnp.inf)
+        top = jnp.maximum(
+            jnp.max(scores, axis=-1, keepdims=True), jnp.max(last, axis=-1, keepdims=True)
+        )
+        weights, last = jnp.exp(scores - top), jnp.exp(last - top)
+        total = jnp.sum(weights, axis=-1, keepdims=True) + jnp.sum(last, axis=-1, keepdims=True)
+        parts.append((top, total, nn(weights.astype(BF16), values) + nn(last.astype(BF16), tail_values)))
+    return parts
+
+
+def own_kernel(rows_ref, own_ref, summed_ref, stats_ref):
+    core, block = position_of()
     lane = lax.broadcasted_iota(jnp.int32, (HALF, HD), 1)
     stats = jnp.zeros((HALF, HD), F32)
-
-    def attend(q, keys, values, tail, seen):
-        scores = nt(q, keys) * SCALE
-        tail = jnp.where(seen, tail, -jnp.inf)
-        top = jnp.maximum(
-            jnp.max(scores, axis=-1, keepdims=True), jnp.max(tail, axis=-1, keepdims=True)
-        )
-        weights, tail = jnp.exp(scores - top), jnp.exp(tail - top)
-        total = jnp.sum(weights, axis=-1, keepdims=True) + jnp.sum(tail, axis=-1, keepdims=True)
-        summed = nn(weights.astype(BF16), values) + nn(tail.astype(BF16), tail_values)
-        return top, total, summed
-
-    for h in range(GROUP):
-        q = rows[:, h * HD : (h + 1) * HD]
-        tail = nt(q, tail_keys) * SCALE
-        top0, total0, summed0 = attend(q, own_keys, own_values, tail, own_seen)
-        top1, total1, summed1 = attend(q, mate_keys, mate_values, tail, mate_seen)
+    for h, (top, total, summed) in enumerate(attend_block(rows_ref, own_ref, core, block)):
+        summed_ref[:, h * HD : (h + 1) * HD] = summed
+        stats = jnp.where(lane == h, top, jnp.where(lane == GROUP + h, total, stats))
+    stats_ref[...] = stats
+
+
+def query_own(rows, own):
+    return pl.pallas_call(
+        own_kernel,
+        out_shape=(pltpu.VMEM((HALF, GROUP * HD), F32), pltpu.VMEM((HALF, HD), F32)),
+        in_specs=[IN_VMEM] * 2,
+        out_specs=(IN_VMEM, IN_VMEM),
+        name="query_own",
+    )(vmem(rows), vmem(own))
+
+
+def mate_kernel(rows_ref, own_ref, mate_ref, summed_ref, stats_ref, out_ref):
+    core, block = position_of()
+    mate = block + 1 - 2 * core
+    lane = lax.broadcasted_iota(jnp.int32, (HALF, HD), 1)
+    stats = jnp.zeros((HALF, HD), F32)
+    before = stats_ref[...]
+    for h, (top1, total1, summed1) in enumerate(attend_block(rows_ref, mate_ref, core, mate)):
+        top0, total0 = before[:, h : h + 1], before[:, GROUP + h : GROUP + h + 1]
+        summed0 = summed_ref[:, h * HD : (h + 1) * HD]
         top = jnp.maximum(top0, top1)
         factor0, factor1 = jnp.exp(top0 - top), jnp.exp(top1 - top)
         out_ref[:, h * HD : (h + 1) * HD] = (summed0 * factor0 + summed1 * factor1).astype(BF16)
@@ -119,21 +137,21 @@
 
     @pl.when(core == 0)
     def _():
-        out_ref[:, ANCHOR:FIRST] = own_keys
+        out_ref[:, ANCHOR:FIRST] = own_ref[0:BLK, :]
 
     @pl.when(core != 0)
     def _():
-        out_ref[:, ANCHOR:FIRST] = mate_values
-
-
-def query_parts(rows, own, mate):
-    return pl.pallas_call(
-        query_kernel,
+        out_ref[:, ANCHOR:FIRST] = mate_ref[BLK : 2 * BLK, :]
+
+
+def query_parts(rows, own, mate, summed, stats):
+    return pl.pallas_call(
+        mate_kernel,
         out_shape=pltpu.VMEM((HALF, FIRST), BF16),
-        in_specs=[IN_VMEM] * 3,
+        in_specs=[IN_VMEM] * 5,
         out_specs=IN_VMEM,
         name="query_parts",
-    )(vmem(rows), vmem(own), vmem(mate))
+    )(vmem(rows), vmem(own), vmem(mate), vmem(summed), vmem(stats))
 
 
 def merge_kernel(parts_ref, out_ref):
@@ -249,7 +267,8 @@
     own, rows = pack(ctx_keys, ctx_values, query_keys, query_values, out_weight.T, query_queries)
     mate = lax.ppermute(own, "core", [(0, 1), (1, 0)])
 
-    parts = query_parts(rows, own, mate)
+    summed, stats = query_own(rows, own)
+    parts = query_parts(rows, own, mate, summed, stats)
     parts = lax.all_to_all(parts.reshape(PEERS, SHARE, FIRST), ("z", "x"), 0, 0)
     message = merge_parts(parts)
     gathered = lax.all_to_all(message, ("z", "x"), 0, 0)

time: 73 us -> 74.1 us (1.015)
  Pallas kernels: 7.55 us -> 9.67 us
  waiting for transfers between devices: 4.22 us -> 3.17 us
    pallas_call x1 -> x2, Pallas kernels: 2.1 us -> 4.22 us  [the longest x1 2.86 us: query_parts(): pl.pallas_call(mate_kernel, out_shape=pltpu.VMEM((HALF, FIRST), BF16), in...]
    ppermute x1, waiting for transfers between devices: 1.05 us -> 0.01 us  [body(): mate = lax.ppermute(own, 'core', [(0, 1), (1, 0)])]
  transfers between devices with their start and end apart: 3 -> 3, of which waited for: 3 -> 2; matrix products, arithmetic and copies ran while one was open for 0% -> 0% of each run, Pallas kernels for 3% -> 5%
where the time goes in v5:
time: 74.1 us; the launch traced here: 73.8 us
  blocking collectives  38.8 us (52%)
  starting transfers between devices  21.5 us (29%)
  Pallas kernels  9.67 us (13%)
  waiting for transfers between devices  3.17 us (4%)
    all_to_all x1, blocking collectives, body(): parts = lax.all_to_all(parts.reshape(PEERS, SHARE, FIRST), ('z', 'x'), 0, 0)  21.7 us
    all_to_all x1, blocking collectives, body(): gathered = lax.all_to_all(message, ('z', 'x'), 0, 0)  17.1 us
    all_to_all x1, starting transfers between devices, body(): sums = lax.all_to_all(sums.reshape(16, 16, 128), ('core', 'tp'), 0, 0)  10.7 us
    ppermute x1, starting transfers between devices, body(): mate = lax.ppermute(own, 'core', [(0, 1), (1, 0)])  8.79 us
    pallas_call x1, Pallas kernels, query_parts(): pl.pallas_call(mate_kernel, out_shape=pltpu.VMEM((HALF, FIRST), BF16), in...  2.86 us
    pallas_call x1, Pallas kernels, context(): pl.pallas_call(context_kernel, out_shape=jax.ShapeDtypeStruct((BLK, GROUP...  2.11 us
    all_to_all x1, waiting for transfers between devices, body(): sums = lax.all_to_all(sums.reshape(16, 16, 128), ('core', 'tp'), 0, 0)  2.04 us
    ppermute x1, starting transfers between devices, body(): other = lax.ppermute(half, 'core', [(0, 1), (1, 0)])  2 us
  transfers between devices with their start and end apart: 3, of which 2 were waited for; matrix products, arithmetic and copies ran while one was open for 0% of the time, Pallas kernels for 5%

profile of v5, /device:TPU:1, one launch (start us, length us, event | category | flops | bytes accessed | tf_op | source)
XLA Modules:
  0.0 73.8 jit_solution(730968018213759613)
XLA Ops:
  0.6 1.2 %pack.1 = (bf16[784,128]{1,0:T(8,128)(2,1)S(1)}, bf16[256,512]{1,0:T(8,128)(2,1)S(1)}) custom-call(bf16[256,128]{1,0:T(8,128)(2,1)} %keys_ref.1, bf16[256,128]{1,0:T(8,128)(2,1)} %values_ref.1, bf16[8,128]{1,0:T(8,128)(2,1)} %query_keys_ref.1, bf16[8,128]{1,0:T(8,128)(2,1)} %query_values_ref.1, bf16[64,512]{1,0:T(8,128)(2,1)} %bitcast.6, ...), custom_call_target="tpu_custom_call" | custom-call | tf_op jit(solution)/shard_map/pack/pallas_call | solution.py:64
  1.9 8.8 %collective-permute-start = (bf16[784,128]{1,0:T(8,128)(2,1)S(1)}, bf16[784,128]{1,0:T(8,128)(2,1)S(1)}, u32[]{:S(2)}, u32[]{:S(2)}) collective-permute-start(bf16[784,128]{1,0:T(8,128)(2,1)S(1)} %get-tuple-element.8.own_ref), channel_id=1, source_target_pairs={{0,8},{8,0},{1,9},{9,1},{2,10},{10,2},{3,11},{11,3},{4,12},{12,4},... | collective-permute-start | bytes 602120 | tf_op jit(solution)/shard_map/ppermute | solution.py:268
  10.7 1.4 %query_own.1 = (f32[256,512]{1,0:T(8,128)S(1)}, f32[256,128]{1,0:T(8,128)S(1)}) custom-call(bf16[256,512]{1,0:T(8,128)(2,1)S(1)} %get-tuple-element.9.rows_ref, bf16[784,128]{1,0:T(8,128)(2,1)S(1)} %get-tuple-element.8.own_ref), custom_call_target="tpu_custom_call" | custom-call | tf_op jit(solution)/shard_map/query_own/pallas_call | solution.py:108
  12.0 0.0 collective-permute-done.mate_ref
  12.0 2.9 %query_parts.1 = bf16[256,768]{1,0:T(8,128)(2,1)S(1)} custom-call(bf16[256,512]{1,0:T(8,128)(2,1)S(1)} %get-tuple-element.9.rows_ref, bf16[784,128]{1,0:T(8,128)(2,1)S(1)} %get-tuple-element.8.own_ref, bf16[784,128]{1,0:T(8,128)(2,1)S(1)} %collective-permute-done.mate_ref, f32[256,512]{1,0:T(8,128)S(1)} %get-tuple-element.10.summed_ref, ...), custom_call_target="tpu_custom_call" | custom-call | tf_op jit(solution)/shard_map/query_parts/pallas_call | solution.py:148
  14.9 21.7 %all_to_all.15.parts_ref = bf16[32,8,768]{2,1,0:T(8,128)(2,1)S(1)} all-to-all(bf16[32,8,768]{2,1,0:T(8,128)(2,1)S(1)} %bitcast.4), channel_id=1, replica_groups=mesh['z'=8,'x'=4,'core'=2,'tp'=8] {'z','x'}, dimensions={0} | all-to-all | bytes 786432 | tf_op jit(solution)/shard_map/all_to_all | solution.py:272
  36.6 0.5 merge_parts.1
  37.1 17.1 %all_to_all.16.rows_ref = bf16[32,8,768]{2,1,0:T(8,128)(2,1)S(1)} all-to-all(bf16[32,8,768]{2,1,0:T(8,128)(2,1)S(1)} %merge_parts.1), channel_id=1, replica_groups=mesh['z'=8,'x'=4,'core'=2,'tp'=8] {'z','x'}, dimensions={0} | all-to-all | bytes 786432 | tf_op jit(solution)/shard_map/all_to_all | solution.py:274
  54.2 0.9 %project.1 = (f32[2,8,16,128]{3,2,1,0:T(8,128)}, bf16[256,128]{1,0:T(8,128)(2,1)S(1)}) custom-call(bf16[32,8,768]{2,1,0:T(8,128)(2,1)S(1)} %all_to_all.16.rows_ref, bf16[784,128]{1,0:T(8,128)(2,1)S(1)} %get-tuple-element.8.own_ref, bf16[784,128]{1,0:T(8,128)(2,1)S(1)} %collective-permute-done.mate_ref), custom_call_target="tpu_custom_call" | custom-call | tf_op jit(solution)/shard_map/project/pallas_call | solution.py:207
  55.2 0.0 copy-start
  55.2 10.7 %all-to-all-start.2 = ((f32[16,16,128]{2,1,0:T(8,128)}), f32[16,16,128]{2,1,0:T(8,128)S(1)}, u32[]{:S(2)}, u32[]{:S(2)}) async-start(f32[16,16,128]{2,1,0:T(8,128)} %bitcast.3), calls=%async_computation.2 | async-start | bytes 262144 | tf_op jit(solution)/shard_map/all_to_all | solution.py:277
  65.8 2.0 %collective-permute-start.1 = (bf16[256,128]{1,0:T(8,128)(2,1)S(1)}, bf16[256,128]{1,0:T(8,128)(2,1)S(1)}, u32[]{:S(2)}, u32[]{:S(2)}) collective-permute-start(bf16[256,128]{1,0:T(8,128)(2,1)S(1)} %get-tuple-element.12.half_ref), channel_id=1, source_target_pairs={{0,8},{8,0},{1,9},{9,1},{2,10},{10,2},{3,11},{11,3},{4,12},{12,4},... | collective-permute-start | bytes 196616 | tf_op jit(solution)/shard_map/ppermute | solution.py:278
  67.8 1.1 %collective-permute-done.1.other_ref = bf16[256,128]{1,0:T(8,128)(2,1)S(1)} collective-permute-done((bf16[256,128]{1,0:T(8,128)(2,1)S(1)}, bf16[256,128]{1,0:T(8,128)(2,1)S(1)}, u32[]{:S(2)}, u32[]{:S(2)}) %collective-permute-start.1) | collective-permute-done | bytes 65568 | tf_op jit(solution)/shard_map/ppermute | solution.py:278
  69.0 0.0 copy-done
  69.0 2.1 %context.1 = bf16[256,512]{1,0:T(8,128)(2,1)} custom-call(bf16[256,512]{1,0:T(8,128)(2,1)S(1)} %copy-done, bf16[784,128]{1,0:T(8,128)(2,1)S(1)} %get-tuple-element.8.own_ref, bf16[256,128]{1,0:T(8,128)(2,1)S(1)} %get-tuple-element.12.half_ref, bf16[256,128]{1,0:T(8,128)(2,1)S(1)} %collective-permute-done.1.other_ref), custom_call_target="tpu_custom_call" | custom-call | flops 268435456 | bytes 1048576 | tf_op jit(solution)/shard_map/context/pallas_call | solution.py:237
  71.1 2.0 %all-to-all-done.2.parts_ref = f32[16,16,128]{2,1,0:T(8,128)S(1)} async-done(((f32[16,16,128]{2,1,0:T(8,128)}), f32[16,16,128]{2,1,0:T(8,128)S(1)}, u32[]{:S(2)}, u32[]{:S(2)}) %all-to-all-start.2) | async-done | bytes 131104 | tf_op jit(solution)/shard_map/all_to_all | solution.py:277
  73.1 0.7 finish.1
Async XLA Ops:
  1.9 10.2 %collective-permute-start = (bf16[784,128]{1,0:T(8,128)(2,1)S(1)}, bf16[784,128]{1,0:T(8,128)(2,1)S(1)}, u32[]{:S(2)}, u32[]{:S(2)}) collective-permute-start(bf16[784,128]{1,0:T(8,128)(2,1)S(1)} %get-tuple-element.8.own_ref), channel_id=1, source_target_pairs={{0,8},{8,0},{1,9},{9,1},{2,10},{10,2},{3,11},{11,3},{4,12},{12,4},... | collective-permute-start | bytes 602120 | tf_op jit(solution)/shard_map/ppermute | solution.py:268
  55.2 13.8 %copy-start = (bf16[256,512]{1,0:T(8,128)(2,1)S(1)}, bf16[256,512]{1,0:T(8,128)(2,1)}, u32[]{:S(2)}) copy-start(bf16[256,512]{1,0:T(8,128)(2,1)} %q_ref.1) | copy-start | bytes 786436
  55.2 18.0 %all-to-all-start.2 = ((f32[16,16,128]{2,1,0:T(8,128)}), f32[16,16,128]{2,1,0:T(8,128)S(1)}, u32[]{:S(2)}, u32[]{:S(2)}) async-start(f32[16,16,128]{2,1,0:T(8,128)} %bitcast.3), calls=%async_computation.2 | async-start | bytes 262144 | tf_op jit(solution)/shard_map/all_to_all | solution.py:277
  65.8 3.1 %collective-permute-start.1 = (bf16[256,128]{1,0:T(8,128)(2,1)S(1)}, bf16[256,128]{1,0:T(8,128)(2,1)S(1)}, u32[]{:S(2)}, u32[]{:S(2)}) collective-permute-start(bf16[256,128]{1,0:T(8,128)(2,1)S(1)} %get-tuple-element.12.half_ref), channel_id=1, source_target_pairs={{0,8},{8,0},{1,9},{9,1},{2,10},{10,2},{3,11},{11,3},{4,12},{12,4},... | collective-permute-start | bytes 196616 | tf_op jit(solution)/shard_map/ppermute | solution.py:278

commit v6 on v4

--- a/solution.py
+++ b/solution.py
@@ -20,7 +20,7 @@
 STATS = GROUP * HD
 ANCHOR = STATS + HD
 FIRST = ANCHOR + HD
-SECOND = GROUP * HD + 2 * HD
+SECOND = GROUP * HD + HD
 TAIL = 2 * BLK
 WEIGHT = TAIL + 2 * SHARE
 PACKED = WEIGHT + GROUP * 64
@@ -152,7 +152,6 @@
         out_ref[:, :, h * HD : (h + 1) * HD] = jnp.broadcast_to(attended[None], (PEERS, SHARE, HD))
     anchor = jnp.broadcast_to(parts_ref[0, :, ANCHOR:FIRST][None], (PEERS, SHARE, HD))
     out_ref[:, :, GROUP * HD : (GROUP + 1) * HD] = anchor
-    out_ref[:, :, (GROUP + 1) * HD :] = anchor
 
 
 def merge_parts(parts):

time: 73 us -> 71.8 us (0.984)
  blocking collectives: 38.8 us -> 37.2 us
    all_to_all x1, blocking collectives: 17.6 us -> 16 us  [body(): gathered = lax.all_to_all(message, ('z', 'x'), 0, 0)]
where the time goes in v6:
time: 71.8 us; the launch traced here: 71.5 us
  blocking collectives  37.2 us (52%)
  starting transfers between devices  21.9 us (31%)
  Pallas kernels  7.53 us (10%)
  waiting for transfers between devices  4.22 us (6%)
    all_to_all x1, blocking collectives, body(): parts = lax.all_to_all(parts.reshape(PEERS, SHARE, FIRST), ('z', 'x'), 0, 0)  21.2 us
    all_to_all x1, blocking collectives, body(): gathered = lax.all_to_all(message, ('z', 'x'), 0, 0)  16 us
    all_to_all x1, starting transfers between devices, body(): sums = lax.all_to_all(sums.reshape(16, 16, 128), ('core', 'tp'), 0, 0)  11.1 us
    ppermute x1, starting transfers between devices, body(): mate = lax.ppermute(own, 'core', [(0, 1), (1, 0)])  8.79 us
    pallas_call x1, Pallas kernels, context(): pl.pallas_call(context_kernel, out_shape=jax.ShapeDtypeStruct((BLK, GROUP...  2.11 us
    pallas_call x1, Pallas kernels, query_parts(): pl.pallas_call(query_kernel, out_shape=pltpu.VMEM((HALF, FIRST), BF16), i...  2.1 us
    all_to_all x1, waiting for transfers between devices, body(): sums = lax.all_to_all(sums.reshape(16, 16, 128), ('core', 'tp'), 0, 0)  2.04 us
    ppermute x1, starting transfers between devices, body(): other = lax.ppermute(half, 'core', [(0, 1), (1, 0)])  2 us
  transfers between devices with their start and end apart: 3, of which 3 were waited for; matrix products, arithmetic and copies ran while one was open for 0% of the time, Pallas kernels for 3%

profile of v6, /device:TPU:1, one launch (start us, length us, event | category | flops | bytes accessed | tf_op | source)
XLA Modules:
  0.0 71.5 jit_solution(14217995086635132112)
XLA Ops:
  0.6 1.2 %pack.1 = (bf16[784,128]{1,0:T(8,128)(2,1)S(1)}, bf16[256,512]{1,0:T(8,128)(2,1)S(1)}) custom-call(bf16[256,128]{1,0:T(8,128)(2,1)} %keys_ref.1, bf16[256,128]{1,0:T(8,128)(2,1)} %values_ref.1, bf16[8,128]{1,0:T(8,128)(2,1)} %query_keys_ref.1, bf16[8,128]{1,0:T(8,128)(2,1)} %query_values_ref.1, bf16[64,512]{1,0:T(8,128)(2,1)} %bitcast.6, ...), custom_call_target="tpu_custom_call" | custom-call | tf_op jit(solution)/shard_map/pack/pallas_call | solution.py:64
  1.9 8.8 %collective-permute-start = (bf16[784,128]{1,0:T(8,128)(2,1)S(1)}, bf16[784,128]{1,0:T(8,128)(2,1)S(1)}, u32[]{:S(2)}, u32[]{:S(2)}) collective-permute-start(bf16[784,128]{1,0:T(8,128)(2,1)S(1)} %get-tuple-element.6.own_ref), channel_id=1, source_target_pairs={{0,8},{8,0},{1,9},{9,1},{2,10},{10,2},{3,11},{11,3},{4,12},{12,4},... | collective-permute-start | bytes 602120 | tf_op jit(solution)/shard_map/ppermute | solution.py:249
  10.7 1.1 %collective-permute-done.mate_ref = bf16[784,128]{1,0:T(8,128)(2,1)S(1)} collective-permute-done((bf16[784,128]{1,0:T(8,128)(2,1)S(1)}, bf16[784,128]{1,0:T(8,128)(2,1)S(1)}, u32[]{:S(2)}, u32[]{:S(2)}) %collective-permute-start) | collective-permute-done | bytes 200736 | tf_op jit(solution)/shard_map/ppermute | solution.py:249
  11.7 2.1 %query_parts.1 = bf16[256,768]{1,0:T(8,128)(2,1)S(1)} custom-call(bf16[256,512]{1,0:T(8,128)(2,1)S(1)} %get-tuple-element.7.rows_ref, bf16[784,128]{1,0:T(8,128)(2,1)S(1)} %get-tuple-element.6.own_ref, bf16[784,128]{1,0:T(8,128)(2,1)S(1)} %collective-permute-done.mate_ref), custom_call_target="tpu_custom_call" | custom-call | tf_op jit(solution)/shard_map/query_parts/pallas_call | solution.py:130
  13.8 21.2 %all_to_all.15.parts_ref = bf16[32,8,768]{2,1,0:T(8,128)(2,1)S(1)} all-to-all(bf16[32,8,768]{2,1,0:T(8,128)(2,1)S(1)} %bitcast.4), channel_id=1, replica_groups=mesh['z'=8,'x'=4,'core'=2,'tp'=8] {'z','x'}, dimensions={0} | all-to-all | bytes 786432 | tf_op jit(solution)/shard_map/all_to_all | solution.py:252
  35.0 0.5 merge_parts.1
  35.5 16.0 %all_to_all.16.rows_ref = bf16[32,8,640]{2,1,0:T(8,128)(2,1)S(1)} all-to-all(bf16[32,8,640]{2,1,0:T(8,128)(2,1)S(1)} %merge_parts.1), channel_id=1, replica_groups=mesh['z'=8,'x'=4,'core'=2,'tp'=8] {'z','x'}, dimensions={0} | all-to-all | bytes 655360 | tf_op jit(solution)/shard_map/all_to_all | solution.py:254
  51.5 0.9 %project.1 = (f32[2,8,16,128]{3,2,1,0:T(8,128)}, bf16[256,128]{1,0:T(8,128)(2,1)S(1)}) custom-call(bf16[32,8,640]{2,1,0:T(8,128)(2,1)S(1)} %all_to_all.16.rows_ref, bf16[784,128]{1,0:T(8,128)(2,1)S(1)} %get-tuple-element.6.own_ref, bf16[784,128]{1,0:T(8,128)(2,1)S(1)} %collective-permute-done.mate_ref), custom_call_target="tpu_custom_call" | custom-call | tf_op jit(solution)/shard_map/project/pallas_call | solution.py:188
  52.4 0.0 copy-start
  52.4 11.1 %all-to-all-start.2 = ((f32[16,16,128]{2,1,0:T(8,128)}), f32[16,16,128]{2,1,0:T(8,128)S(1)}, u32[]{:S(2)}, u32[]{:S(2)}) async-start(f32[16,16,128]{2,1,0:T(8,128)} %bitcast.3), calls=%async_computation.2 | async-start | bytes 262144 | tf_op jit(solution)/shard_map/all_to_all | solution.py:257
  63.5 2.0 %collective-permute-start.1 = (bf16[256,128]{1,0:T(8,128)(2,1)S(1)}, bf16[256,128]{1,0:T(8,128)(2,1)S(1)}, u32[]{:S(2)}, u32[]{:S(2)}) collective-permute-start(bf16[256,128]{1,0:T(8,128)(2,1)S(1)} %get-tuple-element.8.half_ref), channel_id=1, source_target_pairs={{0,8},{8,0},{1,9},{9,1},{2,10},{10,2},{3,11},{11,3},{4,12},{12,4},... | collective-permute-start | bytes 196616 | tf_op jit(solution)/shard_map/ppermute | solution.py:258
  65.5 1.1 %collective-permute-done.1.other_ref = bf16[256,128]{1,0:T(8,128)(2,1)S(1)} collective-permute-done((bf16[256,128]{1,0:T(8,128)(2,1)S(1)}, bf16[256,128]{1,0:T(8,128)(2,1)S(1)}, u32[]{:S(2)}, u32[]{:S(2)}) %collective-permute-start.1) | collective-permute-done | bytes 65568 | tf_op jit(solution)/shard_map/ppermute | solution.py:258
  66.6 0.0 copy-done
  66.6 2.1 %context.1 = bf16[256,512]{1,0:T(8,128)(2,1)} custom-call(bf16[256,512]{1,0:T(8,128)(2,1)S(1)} %copy-done, bf16[784,128]{1,0:T(8,128)(2,1)S(1)} %get-tuple-element.6.own_ref, bf16[256,128]{1,0:T(8,128)(2,1)S(1)} %get-tuple-element.8.half_ref, bf16[256,128]{1,0:T(8,128)(2,1)S(1)} %collective-permute-done.1.other_ref), custom_call_target="tpu_custom_call" | custom-call | flops 268435456 | bytes 1048576 | tf_op jit(solution)/shard_map/context/pallas_call | solution.py:218
  68.7 2.0 %all-to-all-done.2.parts_ref = f32[16,16,128]{2,1,0:T(8,128)S(1)} async-done(((f32[16,16,128]{2,1,0:T(8,128)}), f32[16,16,128]{2,1,0:T(8,128)S(1)}, u32[]{:S(2)}, u32[]{:S(2)}) %all-to-all-start.2) | async-done | bytes 131104 | tf_op jit(solution)/shard_map/all_to_all | solution.py:257
  70.8 0.7 finish.1
Async XLA Ops:
  1.9 9.8 %collective-permute-start = (bf16[784,128]{1,0:T(8,128)(2,1)S(1)}, bf16[784,128]{1,0:T(8,128)(2,1)S(1)}, u32[]{:S(2)}, u32[]{:S(2)}) collective-permute-start(bf16[784,128]{1,0:T(8,128)(2,1)S(1)} %get-tuple-element.6.own_ref), channel_id=1, source_target_pairs={{0,8},{8,0},{1,9},{9,1},{2,10},{10,2},{3,11},{11,3},{4,12},{12,4},... | collective-permute-start | bytes 602120 | tf_op jit(solution)/shard_map/ppermute | solution.py:249
  52.4 14.2 %copy-start = (bf16[256,512]{1,0:T(8,128)(2,1)S(1)}, bf16[256,512]{1,0:T(8,128)(2,1)}, u32[]{:S(2)}) copy-start(bf16[256,512]{1,0:T(8,128)(2,1)} %q_ref.1) | copy-start | bytes 786436
  52.4 18.4 %all-to-all-start.2 = ((f32[16,16,128]{2,1,0:T(8,128)}), f32[16,16,128]{2,1,0:T(8,128)S(1)}, u32[]{:S(2)}, u32[]{:S(2)}) async-start(f32[16,16,128]{2,1,0:T(8,128)} %bitcast.3), calls=%async_computation.2 | async-start | bytes 262144 | tf_op jit(solution)/shard_map/all_to_all | solution.py:257
  63.5 3.1 %collective-permute-start.1 = (bf16[256,128]{1,0:T(8,128)(2,1)S(1)}, bf16[256,128]{1,0:T(8,128)(2,1)S(1)}, u32[]{:S(2)}, u32[]{:S(2)}) collective-permute-start(bf16[256,128]{1,0:T(8,128)(2,1)S(1)} %get-tuple-element.8.half_ref), channel_id=1, source_target_pairs={{0,8},{8,0},{1,9},{9,1},{2,10},{10,2},{3,11},{11,3},{4,12},{12,4},... | collective-permute-start | bytes 196616 | tf_op jit(solution)/shard_map/ppermute | solution.py:258

commit v7 on v6

--- a/solution.py
+++ b/solution.py
@@ -46,28 +46,37 @@
     return core, (lax.axis_index("z") * 4 + lax.axis_index("x")) * 2 + core
 
 
-def pack_kernel(
-    keys_ref, values_ref, query_keys_ref, query_values_ref, weight_ref, rows_ref, out_ref, half_ref
-):
-    out_ref[0:BLK, :] = keys_ref[...]
-    out_ref[BLK : 2 * BLK, :] = values_ref[...]
-    tail = jnp.concatenate([query_keys_ref[...].astype(F32), query_values_ref[...].astype(F32)], 0)
+def pack_kernel(keys, values, query_keys, query_values, weight, rows, out_ref, half_ref, tail_ref, sems):
+    core, unused = position_of()
+    pieces = [
+        (keys, out_ref.at[0:BLK]),
+        (values, out_ref.at[BLK:TAIL]),
+        (rows.at[:, core], half_ref),
+        (query_keys, tail_ref.at[0]),
+        (query_values, tail_ref.at[1]),
+    ]
+    for h in range(GROUP):
+        start = WEIGHT + h * 64
+        pieces.append((weight.at[:, h * HD : (h + 1) * HD], out_ref.at[start : start + 64]))
+    copies = [pltpu.make_async_copy(a, b, sems.at[i]) for i, (a, b) in enumerate(pieces)]
+    for copy in copies:
+        copy.start()
+    for copy in copies:
+        copy.wait()
+    tail = tail_ref[...].astype(F32).reshape(2 * SHARE, HD)
     out_ref[TAIL:WEIGHT, :] = tail.astype(BF16)
-    for h in range(GROUP):
-        start = WEIGHT + h * 64
-        out_ref[start : start + 64, :] = weight_ref[:, h * HD : (h + 1) * HD]
-    core, unused = position_of()
-    half_ref[...] = rows_ref[:, pl.ds(core, 1)].reshape(HALF, GROUP * HD)
 
 
 def pack(keys, values, query_keys, query_values, weight, rows):
-    return pl.pallas_call(
+    packed, half = pl.pallas_call(
         pack_kernel,
-        out_shape=(pltpu.VMEM((PACKED, HD), BF16), pltpu.VMEM((HALF, GROUP * HD), BF16)),
-        in_specs=[IN_VMEM] * 6,
+        out_shape=(pltpu.VMEM((PACKED, HD), BF16), pltpu.VMEM((8, 32, GROUP * HD), BF16)),
+        in_specs=[pl.BlockSpec(memory_space=pl.ANY)] * 6,
         out_specs=(IN_VMEM, IN_VMEM),
+        scratch_shapes=[pltpu.VMEM((2, SHARE, HD), BF16), pltpu.SemaphoreType.DMA((9,))],
         name="pack",
     )(keys, values, query_keys, query_values, weight, rows.reshape(8, 2, 32, GROUP * HD))
+    return packed, half.reshape(HALF, GROUP * HD)
 
 
 def query_kernel(rows_ref, own_ref, mate_ref, out_ref):
@@ -77,34 +86,29 @@
     own_keys, own_values = own_ref[0:BLK, :], own_ref[BLK : 2 * BLK, :]
     mate_keys, mate_values = mate_ref[0:BLK, :], mate_ref[BLK : 2 * BLK, :]
     own_tail, mate_tail = own_ref[TAIL:WEIGHT, :].astype(F32), mate_ref[TAIL:WEIGHT, :].astype(F32)
-    tail_keys = jnp.concatenate([own_tail[:SHARE], mate_tail[:SHARE]], 0).astype(BF16)
-    tail_values = jnp.concatenate([own_tail[SHARE:], mate_tail[SHARE:]], 0).astype(BF16)
-
-    index = lax.broadcasted_iota(jnp.int32, (HALF, 2 * SHARE), 0)
+    spare = jnp.zeros((HD - 2 * SHARE, HD), F32)
+    tail_keys = jnp.concatenate([own_tail[:SHARE], mate_tail[:SHARE], spare], 0).astype(BF16)
+    tail_values = jnp.concatenate([own_tail[SHARE:], mate_tail[SHARE:], spare], 0).astype(BF16)
+
+    index = lax.broadcasted_iota(jnp.int32, (HALF, HD), 0)
     position = (index // 32) * 64 + core * 32 + index % 32
-    column = lax.broadcasted_iota(jnp.int32, (HALF, 2 * SHARE), 1)
-    own_seen = (column < SHARE) & (position >= block * SHARE + column)
-    mate_seen = (column >= SHARE) & (position >= mate * SHARE + column - SHARE)
-
     lane = lax.broadcasted_iota(jnp.int32, (HALF, HD), 1)
+    key_position = jnp.where(lane < SHARE, block * SHARE + lane, mate * SHARE + lane - SHARE)
+    seen = (lane < 2 * SHARE) & (position >= key_position)
     stats = jnp.zeros((HALF, HD), F32)
 
-    def attend(q, keys, values, tail, seen):
-        scores = nt(q, keys) * SCALE
-        tail = jnp.where(seen, tail, -jnp.inf)
-        top = jnp.maximum(
-            jnp.max(scores, axis=-1, keepdims=True), jnp.max(tail, axis=-1, keepdims=True)
-        )
-        weights, tail = jnp.exp(scores - top), jnp.exp(tail - top)
-        total = jnp.sum(weights, axis=-1, keepdims=True) + jnp.sum(tail, axis=-1, keepdims=True)
-        summed = nn(weights.astype(BF16), values) + nn(tail.astype(BF16), tail_values)
-        return top, total, summed
-
     for h in range(GROUP):
         q = rows[:, h * HD : (h + 1) * HD]
-        tail = nt(q, tail_keys) * SCALE
-        top0, total0, summed0 = attend(q, own_keys, own_values, tail, own_seen)
-        top1, total1, summed1 = attend(q, mate_keys, mate_values, tail, mate_seen)
+        own, other = nt(q, own_keys) * SCALE, nt(q, mate_keys) * SCALE
+        tail = jnp.where(seen, nt(q, tail_keys) * SCALE, -jnp.inf)
+        top0 = jnp.maximum(jnp.maximum(own[:, :HD], own[:, HD:]), tail)
+        top0 = jnp.max(top0, axis=-1, keepdims=True)
+        top1 = jnp.max(other, axis=-1, keepdims=True)
+        own, tail, other = jnp.exp(own - top0), jnp.exp(tail - top0), jnp.exp(other - top1)
+        total0 = jnp.sum(own[:, :HD] + own[:, HD:] + tail, axis=-1, keepdims=True)
+        total1 = jnp.sum(other, axis=-1, keepdims=True)
+        summed0 = nn(own.astype(BF16), own_values) + nn(tail.astype(BF16), tail_values)
+        summed1 = nn(other.astype(BF16), mate_values)
         top = jnp.maximum(top0, top1)
         factor0, factor1 = jnp.exp(top0 - top), jnp.exp(top1 - top)
         out_ref[:, h * HD : (h + 1) * HD] = (summed0 * factor0 + summed1 * factor1).astype(BF16)

time: 71.8 us -> 71.6 us (level)
  no operation moved by 1% of the time
where the time goes in v7:
time: 71.6 us; the launch traced here: 71.2 us
  blocking collectives  37.2 us (52%)
  starting transfers between devices  21.9 us (31%)
  Pallas kernels  7.3 us (10%)
  waiting for transfers between devices  4.22 us (6%)
    all_to_all x1, blocking collectives, body(): parts = lax.all_to_all(parts.reshape(PEERS, SHARE, FIRST), ('z', 'x'), 0, 0)  21.2 us
    all_to_all x1, blocking collectives, body(): gathered = lax.all_to_all(message, ('z', 'x'), 0, 0)  16 us
    all_to_all x1, starting transfers between devices, body(): sums = lax.all_to_all(sums.reshape(16, 16, 128), ('core', 'tp'), 0, 0)  11.1 us
    ppermute x1, starting transfers between devices, body(): mate = lax.ppermute(own, 'core', [(0, 1), (1, 0)])  8.79 us
    pallas_call x1, Pallas kernels, context(): pl.pallas_call(context_kernel, out_shape=jax.ShapeDtypeStruct((BLK, GROUP...  2.11 us
    all_to_all x1, waiting for transfers between devices, body(): sums = lax.all_to_all(sums.reshape(16, 16, 128), ('core', 'tp'), 0, 0)  2.04 us
    ppermute x1, starting transfers between devices, body(): other = lax.ppermute(half, 'core', [(0, 1), (1, 0)])  2 us
    pallas_call x1, Pallas kernels, query_parts(): pl.pallas_call(query_kernel, out_shape=pltpu.VMEM((HALF, FIRST), BF16), i...  1.97 us
  transfers between devices with their start and end apart: 3, of which 3 were waited for; matrix products, arithmetic and copies ran while one was open for 0% of the time, Pallas kernels for 3%

profile of v7, /device:TPU:1, one launch (start us, length us, event | category | flops | bytes accessed | tf_op | source)
XLA Modules:
  0.0 71.2 jit_solution(7267546421834114997)
XLA Ops:
  0.6 1.1 %pack.1 = (bf16[784,128]{1,0:T(8,128)(2,1)S(1)}, bf16[8,32,512]{2,1,0:T(8,128)(2,1)S(1)}) custom-call(bf16[256,128]{1,0:T(8,128)(2,1)} %keys.1, bf16[256,128]{1,0:T(8,128)(2,1)} %values.1, bf16[8,128]{1,0:T(8,128)(2,1)} %query_keys.1, bf16[8,128]{1,0:T(8,128)(2,1)} %query_values.1, bf16[64,512]{1,0:T(8,128)(2,1)} %bitcast.8, bf16[8,2,32,512]{3,2,1,0:T(8,128)(2,1)} %bitcast.7), custom_call_target="tpu_custom_call" | custom-call | tf_op jit(solution)/shard_map/pack/pallas_call | solution.py:71
  1.8 8.8 %collective-permute-start = (bf16[784,128]{1,0:T(8,128)(2,1)S(1)}, bf16[784,128]{1,0:T(8,128)(2,1)S(1)}, u32[]{:S(2)}, u32[]{:S(2)}) collective-permute-start(bf16[784,128]{1,0:T(8,128)(2,1)S(1)} %get-tuple-element.6.own_ref), channel_id=1, source_target_pairs={{0,8},{8,0},{1,9},{9,1},{2,10},{10,2},{3,11},{11,3},{4,12},{12,4},... | collective-permute-start | bytes 602120 | tf_op jit(solution)/shard_map/ppermute | solution.py:253
  10.6 1.1 %collective-permute-done.mate_ref = bf16[784,128]{1,0:T(8,128)(2,1)S(1)} collective-permute-done((bf16[784,128]{1,0:T(8,128)(2,1)S(1)}, bf16[784,128]{1,0:T(8,128)(2,1)S(1)}, u32[]{:S(2)}, u32[]{:S(2)}) %collective-permute-start) | collective-permute-done | bytes 200736 | tf_op jit(solution)/shard_map/ppermute | solution.py:253
  11.6 2.0 %query_parts.1 = bf16[256,768]{1,0:T(8,128)(2,1)S(1)} custom-call(bf16[256,512]{1,0:T(8,128)(2,1)S(1)} %bitcast.6, bf16[784,128]{1,0:T(8,128)(2,1)S(1)} %get-tuple-element.6.own_ref, bf16[784,128]{1,0:T(8,128)(2,1)S(1)} %collective-permute-done.mate_ref), custom_call_target="tpu_custom_call" | custom-call | tf_op jit(solution)/shard_map/query_parts/pallas_call | solution.py:134
  13.6 21.2 %all_to_all.15.parts_ref = bf16[32,8,768]{2,1,0:T(8,128)(2,1)S(1)} all-to-all(bf16[32,8,768]{2,1,0:T(8,128)(2,1)S(1)} %bitcast.5), channel_id=1, replica_groups=mesh['z'=8,'x'=4,'core'=2,'tp'=8] {'z','x'}, dimensions={0} | all-to-all | bytes 786432 | tf_op jit(solution)/shard_map/all_to_all | solution.py:256
  34.8 0.5 merge_parts.1
  35.3 16.0 %all_to_all.16.rows_ref = bf16[32,8,640]{2,1,0:T(8,128)(2,1)S(1)} all-to-all(bf16[32,8,640]{2,1,0:T(8,128)(2,1)S(1)} %merge_parts.1), channel_id=1, replica_groups=mesh['z'=8,'x'=4,'core'=2,'tp'=8] {'z','x'}, dimensions={0} | all-to-all | bytes 655360 | tf_op jit(solution)/shard_map/all_to_all | solution.py:258
  51.2 0.9 %project.1 = (f32[2,8,16,128]{3,2,1,0:T(8,128)}, bf16[256,128]{1,0:T(8,128)(2,1)S(1)}) custom-call(bf16[32,8,640]{2,1,0:T(8,128)(2,1)S(1)} %all_to_all.16.rows_ref, bf16[784,128]{1,0:T(8,128)(2,1)S(1)} %get-tuple-element.6.own_ref, bf16[784,128]{1,0:T(8,128)(2,1)S(1)} %collective-permute-done.mate_ref), custom_call_target="tpu_custom_call" | custom-call | tf_op jit(solution)/shard_map/project/pallas_call | solution.py:192
  52.2 0.0 copy-start
  52.2 11.1 %all-to-all-start.2 = ((f32[16,16,128]{2,1,0:T(8,128)}), f32[16,16,128]{2,1,0:T(8,128)S(1)}, u32[]{:S(2)}, u32[]{:S(2)}) async-start(f32[16,16,128]{2,1,0:T(8,128)} %bitcast.4), calls=%async_computation.2 | async-start | bytes 262144 | tf_op jit(solution)/shard_map/all_to_all | solution.py:261
  63.2 2.0 %collective-permute-start.1 = (bf16[256,128]{1,0:T(8,128)(2,1)S(1)}, bf16[256,128]{1,0:T(8,128)(2,1)S(1)}, u32[]{:S(2)}, u32[]{:S(2)}) collective-permute-start(bf16[256,128]{1,0:T(8,128)(2,1)S(1)} %get-tuple-element.8.half_ref), channel_id=1, source_target_pairs={{0,8},{8,0},{1,9},{9,1},{2,10},{10,2},{3,11},{11,3},{4,12},{12,4},... | collective-permute-start | bytes 196616 | tf_op jit(solution)/shard_map/ppermute | solution.py:262
  65.3 1.1 %collective-permute-done.1.other_ref = bf16[256,128]{1,0:T(8,128)(2,1)S(1)} collective-permute-done((bf16[256,128]{1,0:T(8,128)(2,1)S(1)}, bf16[256,128]{1,0:T(8,128)(2,1)S(1)}, u32[]{:S(2)}, u32[]{:S(2)}) %collective-permute-start.1) | collective-permute-done | bytes 65568 | tf_op jit(solution)/shard_map/ppermute | solution.py:262
  66.4 0.0 copy-done
  66.4 2.1 %context.1 = bf16[256,512]{1,0:T(8,128)(2,1)} custom-call(bf16[256,512]{1,0:T(8,128)(2,1)S(1)} %copy-done, bf16[784,128]{1,0:T(8,128)(2,1)S(1)} %get-tuple-element.6.own_ref, bf16[256,128]{1,0:T(8,128)(2,1)S(1)} %get-tuple-element.8.half_ref, bf16[256,128]{1,0:T(8,128)(2,1)S(1)} %collective-permute-done.1.other_ref), custom_call_target="tpu_custom_call" | custom-call | flops 268435456 | bytes 1048576 | tf_op jit(solution)/shard_map/context/pallas_call | solution.py:222
  68.5 2.0 %all-to-all-done.2.parts_ref = f32[16,16,128]{2,1,0:T(8,128)S(1)} async-done(((f32[16,16,128]{2,1,0:T(8,128)}), f32[16,16,128]{2,1,0:T(8,128)S(1)}, u32[]{:S(2)}, u32[]{:S(2)}) %all-to-all-start.2) | async-done | bytes 131104 | tf_op jit(solution)/shard_map/all_to_all | solution.py:261
  70.5 0.7 finish.1
Async XLA Ops:
  1.8 9.8 %collective-permute-start = (bf16[784,128]{1,0:T(8,128)(2,1)S(1)}, bf16[784,128]{1,0:T(8,128)(2,1)S(1)}, u32[]{:S(2)}, u32[]{:S(2)}) collective-permute-start(bf16[784,128]{1,0:T(8,128)(2,1)S(1)} %get-tuple-element.6.own_ref), channel_id=1, source_target_pairs={{0,8},{8,0},{1,9},{9,1},{2,10},{10,2},{3,11},{11,3},{4,12},{12,4},... | collective-permute-start | bytes 602120 | tf_op jit(solution)/shard_map/ppermute | solution.py:253
  52.2 14.2 %copy-start = (bf16[256,512]{1,0:T(8,128)(2,1)S(1)}, bf16[256,512]{1,0:T(8,128)(2,1)}, u32[]{:S(2)}) copy-start(bf16[256,512]{1,0:T(8,128)(2,1)} %q_ref.1) | copy-start | bytes 786436
  52.2 18.4 %all-to-all-start.2 = ((f32[16,16,128]{2,1,0:T(8,128)}), f32[16,16,128]{2,1,0:T(8,128)S(1)}, u32[]{:S(2)}, u32[]{:S(2)}) async-start(f32[16,16,128]{2,1,0:T(8,128)} %bitcast.4), calls=%async_computation.2 | async-start | bytes 262144 | tf_op jit(solution)/shard_map/all_to_all | solution.py:261
  63.2 3.1 %collective-permute-start.1 = (bf16[256,128]{1,0:T(8,128)(2,1)S(1)}, bf16[256,128]{1,0:T(8,128)(2,1)S(1)}, u32[]{:S(2)}, u32[]{:S(2)}) collective-permute-start(bf16[256,128]{1,0:T(8,128)(2,1)S(1)} %get-tuple-element.8.half_ref), channel_id=1, source_target_pairs={{0,8},{8,0},{1,9},{9,1},{2,10},{10,2},{3,11},{11,3},{4,12},{12,4},... | collective-permute-start | bytes 196616 | tf_op jit(solution)/shard_map/ppermute | solution.py:262

commit v8 on v7

--- a/solution.py
+++ b/solution.py
@@ -97,22 +97,26 @@
     seen = (lane < 2 * SHARE) & (position >= key_position)
     stats = jnp.zeros((HALF, HD), F32)
 
-    for h in range(GROUP):
-        q = rows[:, h * HD : (h + 1) * HD]
-        own, other = nt(q, own_keys) * SCALE, nt(q, mate_keys) * SCALE
-        tail = jnp.where(seen, nt(q, tail_keys) * SCALE, -jnp.inf)
-        top0 = jnp.maximum(jnp.maximum(own[:, :HD], own[:, HD:]), tail)
-        top0 = jnp.max(top0, axis=-1, keepdims=True)
-        top1 = jnp.max(other, axis=-1, keepdims=True)
-        own, tail, other = jnp.exp(own - top0), jnp.exp(tail - top0), jnp.exp(other - top1)
-        total0 = jnp.sum(own[:, :HD] + own[:, HD:] + tail, axis=-1, keepdims=True)
-        total1 = jnp.sum(other, axis=-1, keepdims=True)
-        summed0 = nn(own.astype(BF16), own_values) + nn(tail.astype(BF16), tail_values)
-        summed1 = nn(other.astype(BF16), mate_values)
-        top = jnp.maximum(top0, top1)
-        factor0, factor1 = jnp.exp(top0 - top), jnp.exp(top1 - top)
-        out_ref[:, h * HD : (h + 1) * HD] = (summed0 * factor0 + summed1 * factor1).astype(BF16)
-        total = total0 * factor0 + total1 * factor1
+    q = jnp.concatenate([rows[:, h * HD : (h + 1) * HD] for h in range(GROUP)], 0)
+    seen = jnp.concatenate([jnp.where(seen, 0.0, -jnp.inf)] * GROUP, 0)
+    own, other = nt(q, own_keys) * SCALE, nt(q, mate_keys) * SCALE
+    tail = nt(q, tail_keys) * SCALE + seen
+    tops0 = jnp.maximum(jnp.maximum(own[:, :HD], own[:, HD:]), tail)
+    tops0 = jnp.max(tops0, axis=-1, keepdims=True)
+    tops1 = jnp.max(other, axis=-1, keepdims=True)
+    own, tail, other = jnp.exp(own - tops0), jnp.exp(tail - tops0), jnp.exp(other - tops1)
+    totals0 = jnp.sum(own[:, :HD] + own[:, HD:] + tail, axis=-1, keepdims=True)
+    totals1 = jnp.sum(other, axis=-1, keepdims=True)
+    summed0 = nn(own.astype(BF16), own_values) + nn(tail.astype(BF16), tail_values)
+    summed1 = nn(other.astype(BF16), mate_values)
+    tops = jnp.maximum(tops0, tops1)
+    factor0, factor1 = jnp.exp(tops0 - tops), jnp.exp(tops1 - tops)
+    summed = (summed0 * factor0 + summed1 * factor1).astype(BF16)
+    totals = totals0 * factor0 + totals1 * factor1
+    for h in range(GROUP):
+        mine = slice(h * HALF, (h + 1) * HALF)
+        out_ref[:, h * HD : (h + 1) * HD] = summed[mine]
+        top, total = tops[mine], totals[mine]
         first = top.astype(BF16).astype(F32)
         second = (top - first).astype(BF16).astype(F32)
         high = total.astype(BF16).astype(F32)
@@ -124,6 +128,7 @@
     @pl.when(core == 0)
     def _():
         out_ref[:, ANCHOR:FIRST] = own_keys
+        pl.delay(2000)
 
     @pl.when(core != 0)
     def _():

time: 71.6 us -> 70.1 us (0.979)
  blocking collectives: 37.2 us -> 35.2 us
  starting transfers between devices: 21.9 us -> 22.7 us
    all_to_all x1, blocking collectives: 21.2 us -> 18.8 us  [body(): parts = lax.all_to_all(parts.reshape(PEERS, SHARE, FIRST), ('z', 'x'), 0, 0)]
    all_to_all x1, starting transfers between devices: 11.1 us -> 11.9 us  [body(): sums = lax.all_to_all(sums.reshape(16, 16, 128), ('core', 'tp'), 0, 0)]
where the time goes in v8:
time: 70.1 us; the launch traced here: 69.8 us
  blocking collectives  35.2 us (50%)
  starting transfers between devices  22.7 us (32%)
  Pallas kernels  7.04 us (10%)
  waiting for transfers between devices  4.22 us (6%)
    all_to_all x1, blocking collectives, body(): parts = lax.all_to_all(parts.reshape(PEERS, SHARE, FIRST), ('z', 'x'), 0, 0)  18.8 us
    all_to_all x1, blocking collectives, body(): gathered = lax.all_to_all(message, ('z', 'x'), 0, 0)  16.3 us
    all_to_all x1, starting transfers between devices, body(): sums = lax.all_to_all(sums.reshape(16, 16, 128), ('core', 'tp'), 0, 0)  11.9 us
    ppermute x1, starting transfers between devices, body(): mate = lax.ppermute(own, 'core', [(0, 1), (1, 0)])  8.79 us
    pallas_call x1, Pallas kernels, context(): pl.pallas_call(context_kernel, out_shape=jax.ShapeDtypeStruct((BLK, GROUP...  2.11 us
    all_to_all x1, waiting for transfers between devices, body(): sums = lax.all_to_all(sums.reshape(16, 16, 128), ('core', 'tp'), 0, 0)  2.04 us
    ppermute x1, starting transfers between devices, body(): other = lax.ppermute(half, 'core', [(0, 1), (1, 0)])  2 us
    pallas_call x1, Pallas kernels, query_parts(): pl.pallas_call(query_kernel, out_shape=pltpu.VMEM((HALF, FIRST), BF16), i...  1.7 us
  transfers between devices with their start and end apart: 3, of which 3 were waited for; matrix products, arithmetic and copies ran while one was open for 0% of the time, Pallas kernels for 3%

profile of v8, /device:TPU:1, one launch (start us, length us, event | category | flops | bytes accessed | tf_op | source)
XLA Modules:
  0.0 69.8 jit_solution(5378185743412968701)
XLA Ops:
  0.6 1.1 %pack.1 = (bf16[784,128]{1,0:T(8,128)(2,1)S(1)}, bf16[8,32,512]{2,1,0:T(8,128)(2,1)S(1)}) custom-call(bf16[256,128]{1,0:T(8,128)(2,1)} %keys.1, bf16[256,128]{1,0:T(8,128)(2,1)} %values.1, bf16[8,128]{1,0:T(8,128)(2,1)} %query_keys.1, bf16[8,128]{1,0:T(8,128)(2,1)} %query_values.1, bf16[64,512]{1,0:T(8,128)(2,1)} %bitcast.8, bf16[8,2,32,512]{3,2,1,0:T(8,128)(2,1)} %bitcast.7), custom_call_target="tpu_custom_call" | custom-call | tf_op jit(solution)/shard_map/pack/pallas_call | solution.py:71
  1.8 8.8 %collective-permute-start = (bf16[784,128]{1,0:T(8,128)(2,1)S(1)}, bf16[784,128]{1,0:T(8,128)(2,1)S(1)}, u32[]{:S(2)}, u32[]{:S(2)}) collective-permute-start(bf16[784,128]{1,0:T(8,128)(2,1)S(1)} %get-tuple-element.6.own_ref), channel_id=1, source_target_pairs={{0,8},{8,0},{1,9},{9,1},{2,10},{10,2},{3,11},{11,3},{4,12},{12,4},... | collective-permute-start | bytes 602120 | tf_op jit(solution)/shard_map/ppermute | solution.py:258
  10.6 1.1 %collective-permute-done.mate_ref = bf16[784,128]{1,0:T(8,128)(2,1)S(1)} collective-permute-done((bf16[784,128]{1,0:T(8,128)(2,1)S(1)}, bf16[784,128]{1,0:T(8,128)(2,1)S(1)}, u32[]{:S(2)}, u32[]{:S(2)}) %collective-permute-start) | collective-permute-done | bytes 200736 | tf_op jit(solution)/shard_map/ppermute | solution.py:258
  11.6 1.7 %query_parts.1 = bf16[256,768]{1,0:T(8,128)(2,1)S(1)} custom-call(bf16[256,512]{1,0:T(8,128)(2,1)S(1)} %bitcast.6, bf16[784,128]{1,0:T(8,128)(2,1)S(1)} %get-tuple-element.6.own_ref, bf16[784,128]{1,0:T(8,128)(2,1)S(1)} %collective-permute-done.mate_ref), custom_call_target="tpu_custom_call" | custom-call | tf_op jit(solution)/shard_map/query_parts/pallas_call | solution.py:139
  13.3 18.8 %all_to_all.15.parts_ref = bf16[32,8,768]{2,1,0:T(8,128)(2,1)S(1)} all-to-all(bf16[32,8,768]{2,1,0:T(8,128)(2,1)S(1)} %bitcast.5), channel_id=1, replica_groups=mesh['z'=8,'x'=4,'core'=2,'tp'=8] {'z','x'}, dimensions={0} | all-to-all | bytes 786432 | tf_op jit(solution)/shard_map/all_to_all | solution.py:261
  32.2 0.5 merge_parts.1
  32.6 16.3 %all_to_all.16.rows_ref = bf16[32,8,640]{2,1,0:T(8,128)(2,1)S(1)} all-to-all(bf16[32,8,640]{2,1,0:T(8,128)(2,1)S(1)} %merge_parts.1), channel_id=1, replica_groups=mesh['z'=8,'x'=4,'core'=2,'tp'=8] {'z','x'}, dimensions={0} | all-to-all | bytes 655360 | tf_op jit(solution)/shard_map/all_to_all | solution.py:263
  49.0 0.9 %project.1 = (f32[2,8,16,128]{3,2,1,0:T(8,128)}, bf16[256,128]{1,0:T(8,128)(2,1)S(1)}) custom-call(bf16[32,8,640]{2,1,0:T(8,128)(2,1)S(1)} %all_to_all.16.rows_ref, bf16[784,128]{1,0:T(8,128)(2,1)S(1)} %get-tuple-element.6.own_ref, bf16[784,128]{1,0:T(8,128)(2,1)S(1)} %collective-permute-done.mate_ref), custom_call_target="tpu_custom_call" | custom-call | tf_op jit(solution)/shard_map/project/pallas_call | solution.py:197
  49.9 0.0 copy-start
  49.9 11.9 %all-to-all-start.2 = ((f32[16,16,128]{2,1,0:T(8,128)}), f32[16,16,128]{2,1,0:T(8,128)S(1)}, u32[]{:S(2)}, u32[]{:S(2)}) async-start(f32[16,16,128]{2,1,0:T(8,128)} %bitcast.4), calls=%async_computation.2 | async-start | bytes 262144 | tf_op jit(solution)/shard_map/all_to_all | solution.py:266
  61.8 2.0 %collective-permute-start.1 = (bf16[256,128]{1,0:T(8,128)(2,1)S(1)}, bf16[256,128]{1,0:T(8,128)(2,1)S(1)}, u32[]{:S(2)}, u32[]{:S(2)}) collective-permute-start(bf16[256,128]{1,0:T(8,128)(2,1)S(1)} %get-tuple-element.8.half_ref), channel_id=1, source_target_pairs={{0,8},{8,0},{1,9},{9,1},{2,10},{10,2},{3,11},{11,3},{4,12},{12,4},... | collective-permute-start | bytes 196616 | tf_op jit(solution)/shard_map/ppermute | solution.py:267
  63.9 1.1 %collective-permute-done.1.other_ref = bf16[256,128]{1,0:T(8,128)(2,1)S(1)} collective-permute-done((bf16[256,128]{1,0:T(8,128)(2,1)S(1)}, bf16[256,128]{1,0:T(8,128)(2,1)S(1)}, u32[]{:S(2)}, u32[]{:S(2)}) %collective-permute-start.1) | collective-permute-done | bytes 65568 | tf_op jit(solution)/shard_map/ppermute | solution.py:267
  65.0 0.0 copy-done
  65.0 2.1 %context.1 = bf16[256,512]{1,0:T(8,128)(2,1)} custom-call(bf16[256,512]{1,0:T(8,128)(2,1)S(1)} %copy-done, bf16[784,128]{1,0:T(8,128)(2,1)S(1)} %get-tuple-element.6.own_ref, bf16[256,128]{1,0:T(8,128)(2,1)S(1)} %get-tuple-element.8.half_ref, bf16[256,128]{1,0:T(8,128)(2,1)S(1)} %collective-permute-done.1.other_ref), custom_call_target="tpu_custom_call" | custom-call | flops 268435456 | bytes 1048576 | tf_op jit(solution)/shard_map/context/pallas_call | solution.py:227
  67.1 2.0 %all-to-all-done.2.parts_ref = f32[16,16,128]{2,1,0:T(8,128)S(1)} async-done(((f32[16,16,128]{2,1,0:T(8,128)}), f32[16,16,128]{2,1,0:T(8,128)S(1)}, u32[]{:S(2)}, u32[]{:S(2)}) %all-to-all-start.2) | async-done | bytes 131104 | tf_op jit(solution)/shard_map/all_to_all | solution.py:266
  69.1 0.7 finish.1
Async XLA Ops:
  1.8 9.8 %collective-permute-start = (bf16[784,128]{1,0:T(8,128)(2,1)S(1)}, bf16[784,128]{1,0:T(8,128)(2,1)S(1)}, u32[]{:S(2)}, u32[]{:S(2)}) collective-permute-start(bf16[784,128]{1,0:T(8,128)(2,1)S(1)} %get-tuple-element.6.own_ref), channel_id=1, source_target_pairs={{0,8},{8,0},{1,9},{9,1},{2,10},{10,2},{3,11},{11,3},{4,12},{12,4},... | collective-permute-start | bytes 602120 | tf_op jit(solution)/shard_map/ppermute | solution.py:258
  49.9 15.1 %copy-start = (bf16[256,512]{1,0:T(8,128)(2,1)S(1)}, bf16[256,512]{1,0:T(8,128)(2,1)}, u32[]{:S(2)}) copy-start(bf16[256,512]{1,0:T(8,128)(2,1)} %q_ref.1) | copy-start | bytes 786436
  49.9 19.2 %all-to-all-start.2 = ((f32[16,16,128]{2,1,0:T(8,128)}), f32[16,16,128]{2,1,0:T(8,128)S(1)}, u32[]{:S(2)}, u32[]{:S(2)}) async-start(f32[16,16,128]{2,1,0:T(8,128)} %bitcast.4), calls=%async_computation.2 | async-start | bytes 262144 | tf_op jit(solution)/shard_map/all_to_all | solution.py:266
  61.8 3.1 %collective-permute-start.1 = (bf16[256,128]{1,0:T(8,128)(2,1)S(1)}, bf16[256,128]{1,0:T(8,128)(2,1)S(1)}, u32[]{:S(2)}, u32[]{:S(2)}) collective-permute-start(bf16[256,128]{1,0:T(8,128)(2,1)S(1)} %get-tuple-element.8.half_ref), channel_id=1, source_target_pairs={{0,8},{8,0},{1,9},{9,1},{2,10},{10,2},{3,11},{11,3},{4,12},{12,4},... | collective-permute-start | bytes 196616 | tf_op jit(solution)/shard_map/ppermute | solution.py:267

commit v9 on v8

--- a/solution.py
+++ b/solution.py
@@ -79,12 +79,38 @@
     return packed, half.reshape(HALF, GROUP * HD)
 
 
-def query_kernel(rows_ref, own_ref, mate_ref, out_ref):
+def stacked(rows_ref):
+    return jnp.concatenate([rows_ref[:, h * HD : (h + 1) * HD] for h in range(GROUP)], 0)
+
+
+def spread(column):
+    return jnp.broadcast_to(column, (GROUP * HALF, HD))
+
+
+def own_kernel(rows_ref, own_ref, top_ref, total_ref, summed_ref):
+    keys, values = own_ref[0:BLK, :], own_ref[BLK:TAIL, :]
+    scores = nt(stacked(rows_ref), keys) * SCALE
+    top = jnp.max(scores, axis=-1, keepdims=True)
+    weights = jnp.exp(scores - top)
+    top_ref[...] = spread(top)
+    total_ref[...] = spread(jnp.sum(weights, axis=-1, keepdims=True))
+    summed_ref[...] = nn(weights.astype(BF16), values)
+
+
+def query_own(rows, own):
+    return pl.pallas_call(
+        own_kernel,
+        out_shape=(pltpu.VMEM((GROUP * HALF, HD), F32),) * 3,
+        in_specs=[IN_VMEM] * 2,
+        out_specs=(IN_VMEM,) * 3,
+        name="query_own",
+    )(vmem(rows), vmem(own))
+
+
+def mate_kernel(rows_ref, own_ref, mate_ref, top_ref, total_ref, summed_ref, out_ref):
     core, block = position_of()
     mate = block + 1 - 2 * core
-    rows = rows_ref[...]
-    own_keys, own_values = own_ref[0:BLK, :], own_ref[BLK : 2 * BLK, :]
-    mate_keys, mate_values = mate_ref[0:BLK, :], mate_ref[BLK : 2 * BLK, :]
+    keys, values = mate_ref[0:BLK, :], mate_ref[BLK:TAIL, :]
     own_tail, mate_tail = own_ref[TAIL:WEIGHT, :].astype(F32), mate_ref[TAIL:WEIGHT, :].astype(F32)
     spare = jnp.zeros((HD - 2 * SHARE, HD), F32)
     tail_keys = jnp.concatenate([own_tail[:SHARE], mate_tail[:SHARE], spare], 0).astype(BF16)
@@ -95,24 +121,23 @@
     lane = lax.broadcasted_iota(jnp.int32, (HALF, HD), 1)
     key_position = jnp.where(lane < SHARE, block * SHARE + lane, mate * SHARE + lane - SHARE)
     seen = (lane < 2 * SHARE) & (position >= key_position)
+    seen = jnp.concatenate([jnp.where(seen, 0.0, -jnp.inf)] * GROUP, 0)
+
+    q = stacked(rows_ref)
+    scores = nt(q, keys) * SCALE
+    tail = nt(q, tail_keys) * SCALE + seen
+    top1 = jnp.maximum(jnp.maximum(scores[:, :HD], scores[:, HD:]), tail)
+    top1 = jnp.max(top1, axis=-1, keepdims=True)
+    weights, tail = jnp.exp(scores - top1), jnp.exp(tail - top1)
+    total1 = jnp.sum(weights[:, :HD] + weights[:, HD:] + tail, axis=-1, keepdims=True)
+    summed1 = nn(weights.astype(BF16), values) + nn(tail.astype(BF16), tail_values)
+    top0, top1 = top_ref[...], spread(top1)
+    tops = jnp.maximum(top0, top1)
+    factor0, factor1 = jnp.exp(top0 - tops), jnp.exp(top1 - tops)
+    summed = (summed_ref[...] * factor0 + summed1 * factor1).astype(BF16)
+    totals = total_ref[...] * factor0 + spread(total1) * factor1
+
     stats = jnp.zeros((HALF, HD), F32)
-
-    q = jnp.concatenate([rows[:, h * HD : (h + 1) * HD] for h in range(GROUP)], 0)
-    seen = jnp.concatenate([jnp.where(seen, 0.0, -jnp.inf)] * GROUP, 0)
-    own, other = nt(q, own_keys) * SCALE, nt(q, mate_keys) * SCALE
-    tail = nt(q, tail_keys) * SCALE + seen
-    tops0 = jnp.maximum(jnp.maximum(own[:, :HD], own[:, HD:]), tail)
-    tops0 = jnp.max(tops0, axis=-1, keepdims=True)
-    tops1 = jnp.max(other, axis=-1, keepdims=True)
-    own, tail, other = jnp.exp(own - tops0), jnp.exp(tail - tops0), jnp.exp(other - tops1)
-    totals0 = jnp.sum(own[:, :HD] + own[:, HD:] + tail, axis=-1, keepdims=True)
-    totals1 = jnp.sum(other, axis=-1, keepdims=True)
-    summed0 = nn(own.astype(BF16), own_values) + nn(tail.astype(BF16), tail_values)
-    summed1 = nn(other.astype(BF16), mate_values)
-    tops = jnp.maximum(tops0, tops1)
-    factor0, factor1 = jnp.exp(tops0 - tops), jnp.exp(tops1 - tops)
-    summed = (summed0 * factor0 + summed1 * factor1).astype(BF16)
-    totals = totals0 * factor0 + totals1 * factor1
     for h in range(GROUP):
         mine = slice(h * HALF, (h + 1) * HALF)
         out_ref[:, h * HD : (h + 1) * HD] = summed[mine]
@@ -127,22 +152,22 @@
 
     @pl.when(core == 0)
     def _():
-        out_ref[:, ANCHOR:FIRST] = own_keys
-        pl.delay(2000)
+        out_ref[:, ANCHOR:FIRST] = own_ref[0:BLK, :]
+        pl.delay(2500)
 
     @pl.when(core != 0)
     def _():
-        out_ref[:, ANCHOR:FIRST] = mate_values
-
-
-def query_parts(rows, own, mate):
-    return pl.pallas_call(
-        query_kernel,
+        out_ref[:, ANCHOR:FIRST] = values
+
+
+def query_parts(rows, own, mate, parts):
+    return pl.pallas_call(
+        mate_kernel,
         out_shape=pltpu.VMEM((HALF, FIRST), BF16),
-        in_specs=[IN_VMEM] * 3,
+        in_specs=[IN_VMEM] * 6,
         out_specs=IN_VMEM,
         name="query_parts",
-    )(vmem(rows), vmem(own), vmem(mate))
+    )(vmem(rows), vmem(own), vmem(mate), *(vmem(part) for part in parts))
 
 
 def merge_kernel(parts_ref, out_ref):
@@ -173,7 +198,7 @@
     )(vmem(parts))
 
 
-def project_kernel(rows_ref, own_ref, mate_ref, out_ref, half_ref):
+def project_kernel(rows_ref, own_ref, mate_ref, out_ref):
     core, unused = position_of()
     rows = rows_ref[:, :, : GROUP * HD].astype(F32).reshape(8, 2, 16, GROUP * HD)
     upper = rows[:, 0].reshape(128, GROUP * HD).astype(BF16)
@@ -189,18 +214,31 @@
 
     out_ref[pl.ds(core, 1)] = packed(own_ref)[None]
     out_ref[pl.ds(1 - core, 1)] = packed(mate_ref)[None]
+
+
+def project(rows, own, mate):
+    return pl.pallas_call(
+        project_kernel,
+        out_shape=pltpu.VMEM((2, 8, 16, 128), F32),
+        in_specs=[IN_VMEM] * 3,
+        out_specs=IN_VMEM,
+        name="project",
+    )(vmem(rows), vmem(own), vmem(mate))
+
+
+def half_kernel(rows_ref, half_ref):
     half = rows_ref[:, :, GROUP * HD : (GROUP + 1) * HD].astype(F32)
     half_ref[...] = half.reshape(BLK, HD).astype(BF16)
 
 
-def project(rows, own, mate):
-    return pl.pallas_call(
-        project_kernel,
-        out_shape=(pltpu.VMEM((2, 8, 16, 128), F32), pltpu.VMEM((BLK, HD), BF16)),
-        in_specs=[IN_VMEM] * 3,
-        out_specs=(IN_VMEM, IN_VMEM),
-        name="project",
-    )(vmem(rows), vmem(own), vmem(mate))
+def anchor_half(rows):
+    return pl.pallas_call(
+        half_kernel,
+        out_shape=pltpu.VMEM((BLK, HD), BF16),
+        in_specs=[IN_VMEM],
+        out_specs=IN_VMEM,
+        name="anchor_half",
+    )(vmem(rows))
 
 
 def context_kernel(q_ref, own_ref, half_ref, other_ref, out_ref):
@@ -257,12 +295,13 @@
     own, rows = pack(ctx_keys, ctx_values, query_keys, query_values, out_weight.T, query_queries)
     mate = lax.ppermute(own, "core", [(0, 1), (1, 0)])
 
-    parts = query_parts(rows, own, mate)
-    parts = lax.all_to_all(parts.reshape(PEERS, SHARE, FIRST), ("z", "x"), 0, 0)
+    parts = query_parts(rows, own, mate, query_own(rows, own))
+    parts = lax.all_to_all(parts.reshape(PEERS, SHARE, FIRST), ("x", "z"), 0, 0)
     message = merge_parts(parts)
-    gathered = lax.all_to_all(message, ("z", "x"), 0, 0)
-
-    sums, half = project(gathered, own, mate)
+    gathered = lax.all_to_all(message, ("x", "z"), 0, 0)
+
+    sums = project(gathered, own, mate)
+    half = anchor_half(gathered)
     sums = lax.all_to_all(sums.reshape(16, 16, 128), ("core", "tp"), 0, 0)
     other = lax.ppermute(half, "core", [(0, 1), (1, 0)])
     ctx_out = context(ctx_queries, own, half, other)

time: 70.1 us -> 68.9 us (0.983)
  blocking collectives: 35.2 us -> 33.9 us
  waiting for transfers between devices: 4.22 us -> 3.42 us
    all_to_all x2, blocking collectives: 35.2 us -> 33.9 us  [the longest x1 17.6 us: body(): parts = lax.all_to_all(parts.reshape(PEERS, SHARE, FIRST), ('x', 'z'), 0, 0)]
    pallas_call x2 -> x4, Pallas kernels: 2.64 us -> 3.07 us  [the longest x1 1.48 us: query_parts(): pl.pallas_call(mate_kernel, out_shape=pltpu.VMEM((HALF, FIRST), BF16), in...]
  transfers between devices with their start and end apart: 3 -> 3, of which waited for: 3 -> 3; matrix products, arithmetic and copies ran while one was open for 0% -> 0% of each run, Pallas kernels for 3% -> 4%
where the time goes in v9:
time: 68.9 us; the launch traced here: 68.6 us
  blocking collectives  33.9 us (49%)
  starting transfers between devices  23.1 us (34%)
  Pallas kernels  7.46 us (11%)
  waiting for transfers between devices  3.42 us (5%)
  between operations  0.7 us (1%)
    all_to_all x1, blocking collectives, body(): parts = lax.all_to_all(parts.reshape(PEERS, SHARE, FIRST), ('x', 'z'), 0, 0)  17.6 us
    all_to_all x1, blocking collectives, body(): gathered = lax.all_to_all(message, ('x', 'z'), 0, 0)  16.3 us
    all_to_all x1, starting transfers between devices, body(): sums = lax.all_to_all(sums.reshape(16, 16, 128), ('core', 'tp'), 0, 0)  12.2 us
    ppermute x1, starting transfers between devices, body(): mate = lax.ppermute(own, 'core', [(0, 1), (1, 0)])  8.79 us
    ppermute x1, starting transfers between devices, body(): other = lax.ppermute(half, 'core', [(0, 1), (1, 0)])  2.14 us
    pallas_call x1, Pallas kernels, context(): pl.pallas_call(context_kernel, out_shape=jax.ShapeDtypeStruct((BLK, GROUP...  2.11 us
    all_to_all x1, waiting for transfers between devices, body(): sums = lax.all_to_all(sums.reshape(16, 16, 128), ('core', 'tp'), 0, 0)  1.87 us
    pallas_call x1, Pallas kernels, query_parts(): pl.pallas_call(mate_kernel, out_shape=pltpu.VMEM((HALF, FIRST), BF16), in...  1.48 us
  transfers between devices with their start and end apart: 3, of which 3 were waited for; matrix products, arithmetic and copies ran while one was open for 0% of the time, Pallas kernels for 4%

profile of v9, /device:TPU:1, one launch (start us, length us, event | category | flops | bytes accessed | tf_op | source)
XLA Modules:
  0.0 68.6 jit_solution(9413039445009795771)
XLA Ops:
  0.6 1.1 %pack.1 = (bf16[784,128]{1,0:T(8,128)(2,1)S(1)}, bf16[8,32,512]{2,1,0:T(8,128)(2,1)S(1)}) custom-call(bf16[256,128]{1,0:T(8,128)(2,1)} %keys.1, bf16[256,128]{1,0:T(8,128)(2,1)} %values.1, bf16[8,128]{1,0:T(8,128)(2,1)} %query_keys.1, bf16[8,128]{1,0:T(8,128)(2,1)} %query_values.1, bf16[64,512]{1,0:T(8,128)(2,1)} %bitcast.9, bf16[8,2,32,512]{3,2,1,0:T(8,128)(2,1)} %bitcast.8), custom_call_target="tpu_custom_call" | custom-call | tf_op jit(solution)/shard_map/pack/pallas_call | solution.py:71
  1.8 8.8 %collective-permute-start = (bf16[784,128]{1,0:T(8,128)(2,1)S(1)}, bf16[784,128]{1,0:T(8,128)(2,1)S(1)}, u32[]{:S(2)}, u32[]{:S(2)}) collective-permute-start(bf16[784,128]{1,0:T(8,128)(2,1)S(1)} %get-tuple-element.7.own_ref), channel_id=1, source_target_pairs={{0,8},{8,0},{1,9},{9,1},{2,10},{10,2},{3,11},{11,3},{4,12},{12,4},... | collective-permute-start | bytes 602120 | tf_op jit(solution)/shard_map/ppermute | solution.py:296
  10.6 0.6 query_own.1
  11.2 0.4 collective-permute-done.mate_ref
  11.6 1.5 %query_parts.1 = bf16[256,768]{1,0:T(8,128)(2,1)S(1)} custom-call(bf16[256,512]{1,0:T(8,128)(2,1)S(1)} %bitcast.7, bf16[784,128]{1,0:T(8,128)(2,1)S(1)} %get-tuple-element.7.own_ref, bf16[784,128]{1,0:T(8,128)(2,1)S(1)} %collective-permute-done.mate_ref, f32[1024,128]{1,0:T(8,128)S(1)} %get-tuple-element.9.top_ref, ...), custom_call_target="tpu_custom_call" | custom-call | tf_op jit(solution)/shard_map/query_parts/pallas_call | solution.py:164
  13.1 17.6 %all_to_all.15.parts_ref = bf16[32,8,768]{2,1,0:T(8,128)(2,1)S(1)} all-to-all(bf16[32,8,768]{2,1,0:T(8,128)(2,1)S(1)} %bitcast.5), channel_id=1, replica_groups=mesh['z'=8,'x'=4,'core'=2,'tp'=8] {'x','z'}, dimensions={0} | all-to-all | bytes 786432 | tf_op jit(solution)/shard_map/all_to_all | solution.py:299
  30.7 0.5 merge_parts.1
  31.1 16.3 %all_to_all.16.rows_ref = bf16[32,8,640]{2,1,0:T(8,128)(2,1)S(1)} all-to-all(bf16[32,8,640]{2,1,0:T(8,128)(2,1)S(1)} %merge_parts.1), channel_id=1, replica_groups=mesh['z'=8,'x'=4,'core'=2,'tp'=8] {'x','z'}, dimensions={0} | all-to-all | bytes 655360 | tf_op jit(solution)/shard_map/all_to_all | solution.py:301
  47.5 0.9 %project.1 = f32[2,8,16,128]{3,2,1,0:T(8,128)} custom-call(bf16[32,8,640]{2,1,0:T(8,128)(2,1)S(1)} %all_to_all.16.rows_ref, bf16[784,128]{1,0:T(8,128)(2,1)S(1)} %get-tuple-element.7.own_ref, bf16[784,128]{1,0:T(8,128)(2,1)S(1)} %collective-permute-done.mate_ref), custom_call_target="tpu_custom_call" | custom-call | tf_op jit(solution)/shard_map/project/pallas_call | solution.py:220
  48.4 12.2 %all-to-all-start.2 = ((f32[16,16,128]{2,1,0:T(8,128)}), f32[16,16,128]{2,1,0:T(8,128)S(1)}, u32[]{:S(2)}, u32[]{:S(2)}) async-start(f32[16,16,128]{2,1,0:T(8,128)} %bitcast.4), calls=%async_computation.2 | async-start | bytes 262144 | tf_op jit(solution)/shard_map/all_to_all | solution.py:305
  60.6 0.0 copy-start
  60.7 2.1 %collective-permute-start.1 = (bf16[256,128]{1,0:T(8,128)(2,1)S(1)}, bf16[256,128]{1,0:T(8,128)(2,1)S(1)}, u32[]{:S(2)}, u32[]{:S(2)}) collective-permute-start(bf16[256,128]{1,0:T(8,128)(2,1)S(1)} %anchor_half.1.half_ref), channel_id=1, source_target_pairs={{0,8},{8,0},{1,9},{9,1},{2,10},{10,2},{3,11},{11,3},{4,12},{12,4},... | collective-permute-start | bytes 196616 | tf_op jit(solution)/shard_map/ppermute | solution.py:306
  62.8 1.1 %collective-permute-done.1.other_ref = bf16[256,128]{1,0:T(8,128)(2,1)S(1)} collective-permute-done((bf16[256,128]{1,0:T(8,128)(2,1)S(1)}, bf16[256,128]{1,0:T(8,128)(2,1)S(1)}, u32[]{:S(2)}, u32[]{:S(2)}) %collective-permute-start.1) | collective-permute-done | bytes 65568 | tf_op jit(solution)/shard_map/ppermute | solution.py:306
  63.9 0.0 copy-done
  63.9 2.1 %context.1 = bf16[256,512]{1,0:T(8,128)(2,1)} custom-call(bf16[256,512]{1,0:T(8,128)(2,1)S(1)} %copy-done, bf16[784,128]{1,0:T(8,128)(2,1)S(1)} %get-tuple-element.7.own_ref, bf16[256,128]{1,0:T(8,128)(2,1)S(1)} %anchor_half.1.half_ref, bf16[256,128]{1,0:T(8,128)(2,1)S(1)} %collective-permute-done.1.other_ref), custom_call_target="tpu_custom_call" | custom-call | flops 268435456 | bytes 1048576 | tf_op jit(solution)/shard_map/context/pallas_call | solution.py:265
  66.1 1.9 %all-to-all-done.2.parts_ref = f32[16,16,128]{2,1,0:T(8,128)S(1)} async-done(((f32[16,16,128]{2,1,0:T(8,128)}), f32[16,16,128]{2,1,0:T(8,128)S(1)}, u32[]{:S(2)}, u32[]{:S(2)}) %all-to-all-start.2) | async-done | bytes 131104 | tf_op jit(solution)/shard_map/all_to_all | solution.py:305
  67.9 0.7 finish.1
  (1 shorter events, 0.0 us)
Async XLA Ops:
  1.8 9.8 %collective-permute-start = (bf16[784,128]{1,0:T(8,128)(2,1)S(1)}, bf16[784,128]{1,0:T(8,128)(2,1)S(1)}, u32[]{:S(2)}, u32[]{:S(2)}) collective-permute-start(bf16[784,128]{1,0:T(8,128)(2,1)S(1)} %get-tuple-element.7.own_ref), channel_id=1, source_target_pairs={{0,8},{8,0},{1,9},{9,1},{2,10},{10,2},{3,11},{11,3},{4,12},{12,4},... | collective-permute-start | bytes 602120 | tf_op jit(solution)/shard_map/ppermute | solution.py:296
  48.4 19.5 %all-to-all-start.2 = ((f32[16,16,128]{2,1,0:T(8,128)}), f32[16,16,128]{2,1,0:T(8,128)S(1)}, u32[]{:S(2)}, u32[]{:S(2)}) async-start(f32[16,16,128]{2,1,0:T(8,128)} %bitcast.4), calls=%async_computation.2 | async-start | bytes 262144 | tf_op jit(solution)/shard_map/all_to_all | solution.py:305
  60.6 3.3 %copy-start = (bf16[256,512]{1,0:T(8,128)(2,1)S(1)}, bf16[256,512]{1,0:T(8,128)(2,1)}, u32[]{:S(2)}) copy-start(bf16[256,512]{1,0:T(8,128)(2,1)} %q_ref.1) | copy-start | bytes 786436
  60.7 3.3 %collective-permute-start.1 = (bf16[256,128]{1,0:T(8,128)(2,1)S(1)}, bf16[256,128]{1,0:T(8,128)(2,1)S(1)}, u32[]{:S(2)}, u32[]{:S(2)}) collective-permute-start(bf16[256,128]{1,0:T(8,128)(2,1)S(1)} %anchor_half.1.half_ref), channel_id=1, source_target_pairs={{0,8},{8,0},{1,9},{9,1},{2,10},{10,2},{3,11},{11,3},{4,12},{12,4},... | collective-permute-start | bytes 196616 | tf_op jit(solution)/shard_map/ppermute | solution.py:306

commit v10 on v9

--- a/solution.py
+++ b/solution.py
@@ -43,7 +43,7 @@
 
 def position_of():
     core = lax.axis_index("core")
-    return core, (lax.axis_index("z") * 4 + lax.axis_index("x")) * 2 + core
+    return core, ((lax.axis_index("za") * 2 + lax.axis_index("zb")) * 4 + lax.axis_index("x")) * 2 + core
 
 
 def pack_kernel(keys, values, query_keys, query_values, weight, rows, out_ref, half_ref, tail_ref, sems):
@@ -200,9 +200,9 @@
 
 def project_kernel(rows_ref, own_ref, mate_ref, out_ref):
     core, unused = position_of()
-    rows = rows_ref[:, :, : GROUP * HD].astype(F32).reshape(8, 2, 16, GROUP * HD)
-    upper = rows[:, 0].reshape(128, GROUP * HD).astype(BF16)
-    lower = rows[:, 1].reshape(128, GROUP * HD).astype(BF16)
+    rows = rows_ref[:, : GROUP * HD].reshape(8, 2, 16, GROUP * HD)
+    upper = rows[:, 0].reshape(128, GROUP * HD)
+    lower = rows[:, 1].reshape(128, GROUP * HD)
 
     def packed(ref):
         pieces = [ref[WEIGHT + h * 64 : WEIGHT + (h + 1) * 64, :] for h in range(GROUP)]
@@ -227,8 +227,7 @@
 
 
 def half_kernel(rows_ref, half_ref):
-    half = rows_ref[:, :, GROUP * HD : (GROUP + 1) * HD].astype(F32)
-    half_ref[...] = half.reshape(BLK, HD).astype(BF16)
+    half_ref[...] = rows_ref[:, GROUP * HD :]
 
 
 def anchor_half(rows):
@@ -296,10 +295,11 @@
     mate = lax.ppermute(own, "core", [(0, 1), (1, 0)])
 
     parts = query_parts(rows, own, mate, query_own(rows, own))
-    parts = lax.all_to_all(parts.reshape(PEERS, SHARE, FIRST), ("x", "z"), 0, 0)
+    parts = lax.all_to_all(parts.reshape(PEERS, SHARE, FIRST), ("x", "zb", "za"), 0, 0)
     message = merge_parts(parts)
-    gathered = lax.all_to_all(message, ("x", "z"), 0, 0)
-
+    gathered = lax.all_to_all(message, ("x", "zb", "za"), 0, 0)
+
+    gathered = gathered.reshape(HALF, SECOND)
     sums = project(gathered, own, mate)
     half = anchor_half(gathered)
     sums = lax.all_to_all(sums.reshape(16, 16, 128), ("core", "tp"), 0, 0)
@@ -310,8 +310,8 @@
 
 
 def solution(mesh):
-    fine = Mesh(mesh.devices.reshape(8, 4, 2, 8), ("z", "x", "core", "tp"))
-    ctx = ("z", "x", "core")
+    fine = Mesh(mesh.devices.reshape(4, 2, 4, 2, 8), ("za", "zb", "x", "core", "tp"))
+    ctx = ("za", "zb", "x", "core")
     return jax.shard_map(
         body,
         mesh=fine,

time: 68.9 us -> 68.8 us (level)
  no operation moved by 1% of the time
where the time goes in v10:
time: 68.8 us; the launch traced here: 68.5 us
  blocking collectives  34 us (49%)
  starting transfers between devices  22.9 us (33%)
  Pallas kernels  7.45 us (11%)
  waiting for transfers between devices  3.42 us (5%)
  between operations  0.7 us (1%)
    all_to_all x1, blocking collectives, body(): lax.all_to_all(parts.reshape(PEERS, SHARE, FIRST), ('x', 'zb', 'za'), 0, 0)  17.8 us
    all_to_all x1, blocking collectives, body(): gathered = lax.all_to_all(message, ('x', 'zb', 'za'), 0, 0)  16.2 us
    all_to_all x1, starting transfers between devices, body(): sums = lax.all_to_all(sums.reshape(16, 16, 128), ('core', 'tp'), 0, 0)  12 us
    ppermute x1, starting transfers between devices, body(): mate = lax.ppermute(own, 'core', [(0, 1), (1, 0)])  8.79 us
    ppermute x1, starting transfers between devices, body(): other = lax.ppermute(half, 'core', [(0, 1), (1, 0)])  2.14 us
    pallas_call x1, Pallas kernels, context(): pl.pallas_call(context_kernel, out_shape=jax.ShapeDtypeStruct((BLK, GROUP...  2.1 us
    all_to_all x1, waiting for transfers between devices, body(): sums = lax.all_to_all(sums.reshape(16, 16, 128), ('core', 'tp'), 0, 0)  1.88 us
    pallas_call x1, Pallas kernels, query_parts(): pl.pallas_call(mate_kernel, out_shape=pltpu.VMEM((HALF, FIRST), BF16), in...  1.48 us
  transfers between devices with their start and end apart: 3, of which 3 were waited for; matrix products, arithmetic and copies ran while one was open for 0% of the time, Pallas kernels for 4%

profile of v10, /device:TPU:1, one launch (start us, length us, event | category | flops | bytes accessed | tf_op | source)
XLA Modules:
  0.0 68.5 jit_solution(12749439992291640017)
XLA Ops:
  0.6 1.1 %pack.1 = (bf16[784,128]{1,0:T(8,128)(2,1)S(1)}, bf16[8,32,512]{2,1,0:T(8,128)(2,1)S(1)}) custom-call(bf16[256,128]{1,0:T(8,128)(2,1)} %keys.1, bf16[256,128]{1,0:T(8,128)(2,1)} %values.1, bf16[8,128]{1,0:T(8,128)(2,1)} %query_keys.1, bf16[8,128]{1,0:T(8,128)(2,1)} %query_values.1, bf16[64,512]{1,0:T(8,128)(2,1)} %bitcast.12, bf16[8,2,32,512]{3,2,1,0:T(8,128)(2,1)} %bitcast.11), custom_call_target="tpu_custom_call" | custom-call | tf_op jit(solution)/shard_map/pack/pallas_call | solution.py:71
  1.8 8.8 %collective-permute-start = (bf16[784,128]{1,0:T(8,128)(2,1)S(1)}, bf16[784,128]{1,0:T(8,128)(2,1)S(1)}, u32[]{:S(2)}, u32[]{:S(2)}) collective-permute-start(bf16[784,128]{1,0:T(8,128)(2,1)S(1)} %get-tuple-element.7.own_ref), channel_id=1, source_target_pairs={{0,8},{8,0},{1,9},{9,1},{2,10},{10,2},{3,11},{11,3},{4,12},{12,4},... | collective-permute-start | bytes 602120 | tf_op jit(solution)/shard_map/ppermute | solution.py:295
  10.6 0.6 query_own.1
  11.2 0.4 collective-permute-done.mate_ref
  11.6 1.5 %query_parts.1 = bf16[256,768]{1,0:T(8,128)(2,1)S(1)} custom-call(bf16[256,512]{1,0:T(8,128)(2,1)S(1)} %bitcast.10, bf16[784,128]{1,0:T(8,128)(2,1)S(1)} %get-tuple-element.7.own_ref, bf16[784,128]{1,0:T(8,128)(2,1)S(1)} %collective-permute-done.mate_ref, f32[1024,128]{1,0:T(8,128)S(1)} %get-tuple-element.9.top_ref, ...), custom_call_target="tpu_custom_call" | custom-call | tf_op jit(solution)/shard_map/query_parts/pallas_call | solution.py:164
  13.1 17.8 %all_to_all.15.parts_ref = bf16[32,8,768]{2,1,0:T(8,128)(2,1)S(1)} all-to-all(bf16[32,8,768]{2,1,0:T(8,128)(2,1)S(1)} %bitcast.8), channel_id=1, replica_groups=mesh['za'=4,'zb'=2,'x'=4,'core'=2,'tp'=8] {'x','zb','za'}, dimensions={0} | all-to-all | bytes 786432 | tf_op jit(solution)/shard_map/all_to_all | solution.py:298
  30.9 0.5 merge_parts.1
  31.4 16.2 %all_to_all.16 = bf16[32,8,640]{2,1,0:T(8,128)(2,1)S(1)} all-to-all(bf16[32,8,640]{2,1,0:T(8,128)(2,1)S(1)} %merge_parts.1), channel_id=1, replica_groups=mesh['za'=4,'zb'=2,'x'=4,'core'=2,'tp'=8] {'x','zb','za'}, dimensions={0} | all-to-all | bytes 655360 | tf_op jit(solution)/shard_map/all_to_all | solution.py:300
  47.6 0.9 %project.1 = f32[2,8,16,128]{3,2,1,0:T(8,128)} custom-call(bf16[256,640]{1,0:T(8,128)(2,1)S(1)} %bitcast.6, bf16[784,128]{1,0:T(8,128)(2,1)S(1)} %get-tuple-element.7.own_ref, bf16[784,128]{1,0:T(8,128)(2,1)S(1)} %collective-permute-done.mate_ref), custom_call_target="tpu_custom_call" | custom-call | tf_op jit(solution)/shard_map/project/pallas_call | solution.py:220
  48.5 12.0 %all-to-all-start.2 = ((f32[16,16,128]{2,1,0:T(8,128)}), f32[16,16,128]{2,1,0:T(8,128)S(1)}, u32[]{:S(2)}, u32[]{:S(2)}) async-start(f32[16,16,128]{2,1,0:T(8,128)} %bitcast.5), calls=%async_computation.2 | async-start | bytes 262144 | tf_op jit(solution)/shard_map/all_to_all | solution.py:305
  60.5 0.0 copy-start
  60.5 2.1 %collective-permute-start.1 = (bf16[256,128]{1,0:T(8,128)(2,1)S(1)}, bf16[256,128]{1,0:T(8,128)(2,1)S(1)}, u32[]{:S(2)}, u32[]{:S(2)}) collective-permute-start(bf16[256,128]{1,0:T(8,128)(2,1)S(1)} %anchor_half.1.half_ref), channel_id=1, source_target_pairs={{0,8},{8,0},{1,9},{9,1},{2,10},{10,2},{3,11},{11,3},{4,12},{12,4},... | collective-permute-start | bytes 196616 | tf_op jit(solution)/shard_map/ppermute | solution.py:306
  62.7 1.1 %collective-permute-done.1.other_ref = bf16[256,128]{1,0:T(8,128)(2,1)S(1)} collective-permute-done((bf16[256,128]{1,0:T(8,128)(2,1)S(1)}, bf16[256,128]{1,0:T(8,128)(2,1)S(1)}, u32[]{:S(2)}, u32[]{:S(2)}) %collective-permute-start.1) | collective-permute-done | bytes 65568 | tf_op jit(solution)/shard_map/ppermute | solution.py:306
  63.8 0.0 copy-done
  63.8 2.1 %context.1 = bf16[256,512]{1,0:T(8,128)(2,1)} custom-call(bf16[256,512]{1,0:T(8,128)(2,1)S(1)} %copy-done, bf16[784,128]{1,0:T(8,128)(2,1)S(1)} %get-tuple-element.7.own_ref, bf16[256,128]{1,0:T(8,128)(2,1)S(1)} %anchor_half.1.half_ref, bf16[256,128]{1,0:T(8,128)(2,1)S(1)} %collective-permute-done.1.other_ref), custom_call_target="tpu_custom_call" | custom-call | flops 268435456 | bytes 1048576 | tf_op jit(solution)/shard_map/context/pallas_call | solution.py:264
  65.9 1.9 %all-to-all-done.2.parts_ref = f32[16,16,128]{2,1,0:T(8,128)S(1)} async-done(((f32[16,16,128]{2,1,0:T(8,128)}), f32[16,16,128]{2,1,0:T(8,128)S(1)}, u32[]{:S(2)}, u32[]{:S(2)}) %all-to-all-start.2) | async-done | bytes 131104 | tf_op jit(solution)/shard_map/all_to_all | solution.py:305
  67.8 0.7 %finish.1 = bf16[64,64]{1,0:T(8,128)(2,1)} custom-call(f32[16,16,128]{2,1,0:T(8,128)S(1)} %all-to-all-done.2.parts_ref), custom_call_target="tpu_custom_call" | custom-call | tf_op jit(solution)/shard_map/finish/pallas_call | solution.py:285
  (1 shorter events, 0.0 us)
Async XLA Ops:
  1.8 9.8 %collective-permute-start = (bf16[784,128]{1,0:T(8,128)(2,1)S(1)}, bf16[784,128]{1,0:T(8,128)(2,1)S(1)}, u32[]{:S(2)}, u32[]{:S(2)}) collective-permute-start(bf16[784,128]{1,0:T(8,128)(2,1)S(1)} %get-tuple-element.7.own_ref), channel_id=1, source_target_pairs={{0,8},{8,0},{1,9},{9,1},{2,10},{10,2},{3,11},{11,3},{4,12},{12,4},... | collective-permute-start | bytes 602120 | tf_op jit(solution)/shard_map/ppermute | solution.py:295
  48.5 19.3 %all-to-all-start.2 = ((f32[16,16,128]{2,1,0:T(8,128)}), f32[16,16,128]{2,1,0:T(8,128)S(1)}, u32[]{:S(2)}, u32[]{:S(2)}) async-start(f32[16,16,128]{2,1,0:T(8,128)} %bitcast.5), calls=%async_computation.2 | async-start | bytes 262144 | tf_op jit(solution)/shard_map/all_to_all | solution.py:305
  60.5 3.3 %copy-start = (bf16[256,512]{1,0:T(8,128)(2,1)S(1)}, bf16[256,512]{1,0:T(8,128)(2,1)}, u32[]{:S(2)}) copy-start(bf16[256,512]{1,0:T(8,128)(2,1)} %q_ref.1) | copy-start | bytes 786436
  60.5 3.3 %collective-permute-start.1 = (bf16[256,128]{1,0:T(8,128)(2,1)S(1)}, bf16[256,128]{1,0:T(8,128)(2,1)S(1)}, u32[]{:S(2)}, u32[]{:S(2)}) collective-permute-start(bf16[256,128]{1,0:T(8,128)(2,1)S(1)} %anchor_half.1.half_ref), channel_id=1, source_target_pairs={{0,8},{8,0},{1,9},{9,1},{2,10},{10,2},{3,11},{11,3},{4,12},{12,4},... | collective-permute-start | bytes 196616 | tf_op jit(solution)/shard_map/ppermute | solution.py:306

commit v11 on v10

--- a/solution.py
+++ b/solution.py
@@ -137,17 +137,17 @@
     summed = (summed_ref[...] * factor0 + summed1 * factor1).astype(BF16)
     totals = total_ref[...] * factor0 + spread(total1) * factor1
 
-    stats = jnp.zeros((HALF, HD), F32)
+    packed = jnp.zeros((HALF, HD), F32)
     for h in range(GROUP):
         mine = slice(h * HALF, (h + 1) * HALF)
         out_ref[:, h * HD : (h + 1) * HD] = summed[mine]
-        top, total = tops[mine], totals[mine]
-        first = top.astype(BF16).astype(F32)
-        second = (top - first).astype(BF16).astype(F32)
-        high = total.astype(BF16).astype(F32)
-        terms = (first, second, top - first - second, high, total - high)
-        for i, term in enumerate(terms):
-            stats = jnp.where(lane == i * GROUP + h, term, stats)
+        value = jnp.where(lane < 3 * GROUP, tops[mine], totals[mine])
+        packed = jnp.where(lane % GROUP == h, value, packed)
+    first = packed.astype(BF16).astype(F32)
+    rest = packed - first
+    second = rest.astype(BF16).astype(F32)
+    stats = jnp.where(lane < 3 * GROUP, rest - second, jnp.where(lane < 4 * GROUP, first, rest))
+    stats = jnp.where(lane < GROUP, first, jnp.where(lane < 2 * GROUP, second, stats))
     out_ref[:, STATS:ANCHOR] = stats.astype(BF16)
 
     @pl.when(core == 0)

time: 68.8 us -> 68.7 us (level)
  no operation moved by 1% of the time
where the time goes in v11:
time: 68.7 us; the launch traced here: 68.3 us
  blocking collectives  34 us (49%)
  starting transfers between devices  22.9 us (33%)
  Pallas kernels  7.32 us (11%)
  waiting for transfers between devices  3.43 us (5%)
  between operations  0.7 us (1%)
    all_to_all x1, blocking collectives, body(): lax.all_to_all(parts.reshape(PEERS, SHARE, FIRST), ('x', 'zb', 'za'), 0, 0)  17.8 us
    all_to_all x1, blocking collectives, body(): gathered = lax.all_to_all(message, ('x', 'zb', 'za'), 0, 0)  16.2 us
    all_to_all x1, starting transfers between devices, body(): sums = lax.all_to_all(sums.reshape(16, 16, 128), ('core', 'tp'), 0, 0)  12 us
    ppermute x1, starting transfers between devices, body(): mate = lax.ppermute(own, 'core', [(0, 1), (1, 0)])  8.79 us
    ppermute x1, starting transfers between devices, body(): other = lax.ppermute(half, 'core', [(0, 1), (1, 0)])  2.14 us
    pallas_call x1, Pallas kernels, context(): pl.pallas_call(context_kernel, out_shape=jax.ShapeDtypeStruct((BLK, GROUP...  2.1 us
    all_to_all x1, waiting for transfers between devices, body(): sums = lax.all_to_all(sums.reshape(16, 16, 128), ('core', 'tp'), 0, 0)  1.88 us
  transfers between devices with their start and end apart: 3, of which 3 were waited for; matrix products, arithmetic and copies ran while one was open for 0% of the time, Pallas kernels for 4%

profile of v11, /device:TPU:1, one launch (start us, length us, event | category | flops | bytes accessed | tf_op | source)
XLA Modules:
  0.0 68.3 jit_solution(135705231143522053)
XLA Ops:
  0.6 1.1 %pack.1 = (bf16[784,128]{1,0:T(8,128)(2,1)S(1)}, bf16[8,32,512]{2,1,0:T(8,128)(2,1)S(1)}) custom-call(bf16[256,128]{1,0:T(8,128)(2,1)} %keys.1, bf16[256,128]{1,0:T(8,128)(2,1)} %values.1, bf16[8,128]{1,0:T(8,128)(2,1)} %query_keys.1, bf16[8,128]{1,0:T(8,128)(2,1)} %query_values.1, bf16[64,512]{1,0:T(8,128)(2,1)} %bitcast.12, bf16[8,2,32,512]{3,2,1,0:T(8,128)(2,1)} %bitcast.11), custom_call_target="tpu_custom_call" | custom-call | tf_op jit(solution)/shard_map/pack/pallas_call | solution.py:71
  1.8 8.8 %collective-permute-start = (bf16[784,128]{1,0:T(8,128)(2,1)S(1)}, bf16[784,128]{1,0:T(8,128)(2,1)S(1)}, u32[]{:S(2)}, u32[]{:S(2)}) collective-permute-start(bf16[784,128]{1,0:T(8,128)(2,1)S(1)} %get-tuple-element.7.own_ref), channel_id=1, source_target_pairs={{0,8},{8,0},{1,9},{9,1},{2,10},{10,2},{3,11},{11,3},{4,12},{12,4},... | collective-permute-start | bytes 602120 | tf_op jit(solution)/shard_map/ppermute | solution.py:295
  10.6 0.6 query_own.1
  11.2 0.4 collective-permute-done.mate_ref
  11.6 1.3 %query_parts.1 = bf16[256,768]{1,0:T(8,128)(2,1)S(1)} custom-call(bf16[256,512]{1,0:T(8,128)(2,1)S(1)} %bitcast.10, bf16[784,128]{1,0:T(8,128)(2,1)S(1)} %get-tuple-element.7.own_ref, bf16[784,128]{1,0:T(8,128)(2,1)S(1)} %collective-permute-done.mate_ref, f32[1024,128]{1,0:T(8,128)S(1)} %get-tuple-element.9.top_ref, ...), custom_call_target="tpu_custom_call" | custom-call | tf_op jit(solution)/shard_map/query_parts/pallas_call | solution.py:164
  13.0 17.8 %all_to_all.15.parts_ref = bf16[32,8,768]{2,1,0:T(8,128)(2,1)S(1)} all-to-all(bf16[32,8,768]{2,1,0:T(8,128)(2,1)S(1)} %bitcast.8), channel_id=1, replica_groups=mesh['za'=4,'zb'=2,'x'=4,'core'=2,'tp'=8] {'x','zb','za'}, dimensions={0} | all-to-all | bytes 786432 | tf_op jit(solution)/shard_map/all_to_all | solution.py:298
  30.8 0.5 merge_parts.1
  31.3 16.2 %all_to_all.16 = bf16[32,8,640]{2,1,0:T(8,128)(2,1)S(1)} all-to-all(bf16[32,8,640]{2,1,0:T(8,128)(2,1)S(1)} %merge_parts.1), channel_id=1, replica_groups=mesh['za'=4,'zb'=2,'x'=4,'core'=2,'tp'=8] {'x','zb','za'}, dimensions={0} | all-to-all | bytes 655360 | tf_op jit(solution)/shard_map/all_to_all | solution.py:300
  47.4 0.9 %project.1 = f32[2,8,16,128]{3,2,1,0:T(8,128)} custom-call(bf16[256,640]{1,0:T(8,128)(2,1)S(1)} %bitcast.6, bf16[784,128]{1,0:T(8,128)(2,1)S(1)} %get-tuple-element.7.own_ref, bf16[784,128]{1,0:T(8,128)(2,1)S(1)} %collective-permute-done.mate_ref), custom_call_target="tpu_custom_call" | custom-call | tf_op jit(solution)/shard_map/project/pallas_call | solution.py:220
  48.4 12.0 %all-to-all-start.2 = ((f32[16,16,128]{2,1,0:T(8,128)}), f32[16,16,128]{2,1,0:T(8,128)S(1)}, u32[]{:S(2)}, u32[]{:S(2)}) async-start(f32[16,16,128]{2,1,0:T(8,128)} %bitcast.5), calls=%async_computation.2 | async-start | bytes 262144 | tf_op jit(solution)/shard_map/all_to_all | solution.py:305
  60.4 0.0 copy-start
  60.4 2.1 %collective-permute-start.1 = (bf16[256,128]{1,0:T(8,128)(2,1)S(1)}, bf16[256,128]{1,0:T(8,128)(2,1)S(1)}, u32[]{:S(2)}, u32[]{:S(2)}) collective-permute-start(bf16[256,128]{1,0:T(8,128)(2,1)S(1)} %anchor_half.1.half_ref), channel_id=1, source_target_pairs={{0,8},{8,0},{1,9},{9,1},{2,10},{10,2},{3,11},{11,3},{4,12},{12,4},... | collective-permute-start | bytes 196616 | tf_op jit(solution)/shard_map/ppermute | solution.py:306
  62.5 1.1 %collective-permute-done.1.other_ref = bf16[256,128]{1,0:T(8,128)(2,1)S(1)} collective-permute-done((bf16[256,128]{1,0:T(8,128)(2,1)S(1)}, bf16[256,128]{1,0:T(8,128)(2,1)S(1)}, u32[]{:S(2)}, u32[]{:S(2)}) %collective-permute-start.1) | collective-permute-done | bytes 65568 | tf_op jit(solution)/shard_map/ppermute | solution.py:306
  63.7 0.0 copy-done
  63.7 2.1 %context.1 = bf16[256,512]{1,0:T(8,128)(2,1)} custom-call(bf16[256,512]{1,0:T(8,128)(2,1)S(1)} %copy-done, bf16[784,128]{1,0:T(8,128)(2,1)S(1)} %get-tuple-element.7.own_ref, bf16[256,128]{1,0:T(8,128)(2,1)S(1)} %anchor_half.1.half_ref, bf16[256,128]{1,0:T(8,128)(2,1)S(1)} %collective-permute-done.1.other_ref), custom_call_target="tpu_custom_call" | custom-call | flops 268435456 | bytes 1048576 | tf_op jit(solution)/shard_map/context/pallas_call | solution.py:264
  65.8 1.9 %all-to-all-done.2.parts_ref = f32[16,16,128]{2,1,0:T(8,128)S(1)} async-done(((f32[16,16,128]{2,1,0:T(8,128)}), f32[16,16,128]{2,1,0:T(8,128)S(1)}, u32[]{:S(2)}, u32[]{:S(2)}) %all-to-all-start.2) | async-done | bytes 131104 | tf_op jit(solution)/shard_map/all_to_all | solution.py:305
  67.7 0.7 %finish.1 = bf16[64,64]{1,0:T(8,128)(2,1)} custom-call(f32[16,16,128]{2,1,0:T(8,128)S(1)} %all-to-all-done.2.parts_ref), custom_call_target="tpu_custom_call" | custom-call | tf_op jit(solution)/shard_map/finish/pallas_call | solution.py:285
  (1 shorter events, 0.0 us)
Async XLA Ops:
  1.8 9.8 %collective-permute-start = (bf16[784,128]{1,0:T(8,128)(2,1)S(1)}, bf16[784,128]{1,0:T(8,128)(2,1)S(1)}, u32[]{:S(2)}, u32[]{:S(2)}) collective-permute-start(bf16[784,128]{1,0:T(8,128)(2,1)S(1)} %get-tuple-element.7.own_ref), channel_id=1, source_target_pairs={{0,8},{8,0},{1,9},{9,1},{2,10},{10,2},{3,11},{11,3},{4,12},{12,4},... | collective-permute-start | bytes 602120 | tf_op jit(solution)/shard_map/ppermute | solution.py:295
  48.4 19.3 %all-to-all-start.2 = ((f32[16,16,128]{2,1,0:T(8,128)}), f32[16,16,128]{2,1,0:T(8,128)S(1)}, u32[]{:S(2)}, u32[]{:S(2)}) async-start(f32[16,16,128]{2,1,0:T(8,128)} %bitcast.5), calls=%async_computation.2 | async-start | bytes 262144 | tf_op jit(solution)/shard_map/all_to_all | solution.py:305
  60.4 3.3 %copy-start = (bf16[256,512]{1,0:T(8,128)(2,1)S(1)}, bf16[256,512]{1,0:T(8,128)(2,1)}, u32[]{:S(2)}) copy-start(bf16[256,512]{1,0:T(8,128)(2,1)} %q_ref.1) | copy-start | bytes 786436
  60.4 3.3 %collective-permute-start.1 = (bf16[256,128]{1,0:T(8,128)(2,1)S(1)}, bf16[256,128]{1,0:T(8,128)(2,1)S(1)}, u32[]{:S(2)}, u32[]{:S(2)}) collective-permute-start(bf16[256,128]{1,0:T(8,128)(2,1)S(1)} %anchor_half.1.half_ref), channel_id=1, source_target_pairs={{0,8},{8,0},{1,9},{9,1},{2,10},{10,2},{3,11},{11,3},{4,12},{12,4},... | collective-permute-start | bytes 196616 | tf_op jit(solution)/shard_map/ppermute | solution.py:306

commit v12 on v10

--- a/solution.py
+++ b/solution.py
@@ -204,16 +204,16 @@
     upper = rows[:, 0].reshape(128, GROUP * HD)
     lower = rows[:, 1].reshape(128, GROUP * HD)
 
-    def packed(ref):
+    def weight(ref):
         pieces = [ref[WEIGHT + h * 64 : WEIGHT + (h + 1) * 64, :] for h in range(GROUP)]
-        weight = jnp.concatenate(pieces, 1)
-        zero = jnp.zeros_like(weight)
-        left = jnp.concatenate([weight, zero], 0)
-        right = jnp.concatenate([zero, weight], 0)
-        return (nt(upper, left) + nt(lower, right)).reshape(8, 16, 128)
-
-    out_ref[pl.ds(core, 1)] = packed(own_ref)[None]
-    out_ref[pl.ds(1 - core, 1)] = packed(mate_ref)[None]
+        return jnp.concatenate(pieces, 1)
+
+    own, mate = weight(own_ref), weight(mate_ref)
+    zero = jnp.zeros_like(own)
+    sums = nt(upper, jnp.concatenate([own, zero, mate, zero], 0))
+    sums = sums + nt(lower, jnp.concatenate([zero, own, zero, mate], 0))
+    out_ref[pl.ds(core, 1)] = sums[:, :HD].reshape(1, 8, 16, 128)
+    out_ref[pl.ds(1 - core, 1)] = sums[:, HD:].reshape(1, 8, 16, 128)
 
 
 def project(rows, own, mate):

time: 68.8 us -> 68.8 us (level)
  no operation moved by 1% of the time
where the time goes in v12:
time: 68.8 us; the launch traced here: 68.5 us
  blocking collectives  34 us (49%)
  starting transfers between devices  22.9 us (33%)
  Pallas kernels  7.45 us (11%)
  waiting for transfers between devices  3.42 us (5%)
  between operations  0.7 us (1%)
    all_to_all x1, blocking collectives, body(): lax.all_to_all(parts.reshape(PEERS, SHARE, FIRST), ('x', 'zb', 'za'), 0, 0)  17.8 us
    all_to_all x1, blocking collectives, body(): gathered = lax.all_to_all(message, ('x', 'zb', 'za'), 0, 0)  16.2 us
    all_to_all x1, starting transfers between devices, body(): sums = lax.all_to_all(sums.reshape(16, 16, 128), ('core', 'tp'), 0, 0)  12 us
    ppermute x1, starting transfers between devices, body(): mate = lax.ppermute(own, 'core', [(0, 1), (1, 0)])  8.79 us
    ppermute x1, starting transfers between devices, body(): other = lax.ppermute(half, 'core', [(0, 1), (1, 0)])  2.14 us
    pallas_call x1, Pallas kernels, context(): pl.pallas_call(context_kernel, out_shape=jax.ShapeDtypeStruct((BLK, GROUP...  2.1 us
    all_to_all x1, waiting for transfers between devices, body(): sums = lax.all_to_all(sums.reshape(16, 16, 128), ('core', 'tp'), 0, 0)  1.88 us
    pallas_call x1, Pallas kernels, query_parts(): pl.pallas_call(mate_kernel, out_shape=pltpu.VMEM((HALF, FIRST), BF16), in...  1.48 us
  transfers between devices with their start and end apart: 3, of which 3 were waited for; matrix products, arithmetic and copies ran while one was open for 0% of the time, Pallas kernels for 4%

profile of v12, /device:TPU:1, one launch (start us, length us, event | category | flops | bytes accessed | tf_op | source)
XLA Modules:
  0.0 68.5 jit_solution(3992460629344302895)
XLA Ops:
  0.6 1.1 %pack.1 = (bf16[784,128]{1,0:T(8,128)(2,1)S(1)}, bf16[8,32,512]{2,1,0:T(8,128)(2,1)S(1)}) custom-call(bf16[256,128]{1,0:T(8,128)(2,1)} %keys.1, bf16[256,128]{1,0:T(8,128)(2,1)} %values.1, bf16[8,128]{1,0:T(8,128)(2,1)} %query_keys.1, bf16[8,128]{1,0:T(8,128)(2,1)} %query_values.1, bf16[64,512]{1,0:T(8,128)(2,1)} %bitcast.12, bf16[8,2,32,512]{3,2,1,0:T(8,128)(2,1)} %bitcast.11), custom_call_target="tpu_custom_call" | custom-call | tf_op jit(solution)/shard_map/pack/pallas_call | solution.py:71
  1.8 8.8 %collective-permute-start = (bf16[784,128]{1,0:T(8,128)(2,1)S(1)}, bf16[784,128]{1,0:T(8,128)(2,1)S(1)}, u32[]{:S(2)}, u32[]{:S(2)}) collective-permute-start(bf16[784,128]{1,0:T(8,128)(2,1)S(1)} %get-tuple-element.7.own_ref), channel_id=1, source_target_pairs={{0,8},{8,0},{1,9},{9,1},{2,10},{10,2},{3,11},{11,3},{4,12},{12,4},... | collective-permute-start | bytes 602120 | tf_op jit(solution)/shard_map/ppermute | solution.py:295
  10.6 0.6 query_own.1
  11.2 0.4 collective-permute-done.mate_ref
  11.6 1.5 %query_parts.1 = bf16[256,768]{1,0:T(8,128)(2,1)S(1)} custom-call(bf16[256,512]{1,0:T(8,128)(2,1)S(1)} %bitcast.10, bf16[784,128]{1,0:T(8,128)(2,1)S(1)} %get-tuple-element.7.own_ref, bf16[784,128]{1,0:T(8,128)(2,1)S(1)} %collective-permute-done.mate_ref, f32[1024,128]{1,0:T(8,128)S(1)} %get-tuple-element.9.top_ref, ...), custom_call_target="tpu_custom_call" | custom-call | tf_op jit(solution)/shard_map/query_parts/pallas_call | solution.py:164
  13.1 17.8 %all_to_all.15.parts_ref = bf16[32,8,768]{2,1,0:T(8,128)(2,1)S(1)} all-to-all(bf16[32,8,768]{2,1,0:T(8,128)(2,1)S(1)} %bitcast.8), channel_id=1, replica_groups=mesh['za'=4,'zb'=2,'x'=4,'core'=2,'tp'=8] {'x','zb','za'}, dimensions={0} | all-to-all | bytes 786432 | tf_op jit(solution)/shard_map/all_to_all | solution.py:298
  30.9 0.5 merge_parts.1
  31.4 16.2 %all_to_all.16 = bf16[32,8,640]{2,1,0:T(8,128)(2,1)S(1)} all-to-all(bf16[32,8,640]{2,1,0:T(8,128)(2,1)S(1)} %merge_parts.1), channel_id=1, replica_groups=mesh['za'=4,'zb'=2,'x'=4,'core'=2,'tp'=8] {'x','zb','za'}, dimensions={0} | all-to-all | bytes 655360 | tf_op jit(solution)/shard_map/all_to_all | solution.py:300
  47.6 0.9 %project.1 = f32[2,8,16,128]{3,2,1,0:T(8,128)} custom-call(bf16[256,640]{1,0:T(8,128)(2,1)S(1)} %bitcast.6, bf16[784,128]{1,0:T(8,128)(2,1)S(1)} %get-tuple-element.7.own_ref, bf16[784,128]{1,0:T(8,128)(2,1)S(1)} %collective-permute-done.mate_ref), custom_call_target="tpu_custom_call" | custom-call | tf_op jit(solution)/shard_map/project/pallas_call | solution.py:220
  48.5 12.0 %all-to-all-start.2 = ((f32[16,16,128]{2,1,0:T(8,128)}), f32[16,16,128]{2,1,0:T(8,128)S(1)}, u32[]{:S(2)}, u32[]{:S(2)}) async-start(f32[16,16,128]{2,1,0:T(8,128)} %bitcast.5), calls=%async_computation.2 | async-start | bytes 262144 | tf_op jit(solution)/shard_map/all_to_all | solution.py:305
  60.5 0.0 copy-start
  60.5 2.1 %collective-permute-start.1 = (bf16[256,128]{1,0:T(8,128)(2,1)S(1)}, bf16[256,128]{1,0:T(8,128)(2,1)S(1)}, u32[]{:S(2)}, u32[]{:S(2)}) collective-permute-start(bf16[256,128]{1,0:T(8,128)(2,1)S(1)} %anchor_half.1.half_ref), channel_id=1, source_target_pairs={{0,8},{8,0},{1,9},{9,1},{2,10},{10,2},{3,11},{11,3},{4,12},{12,4},... | collective-permute-start | bytes 196616 | tf_op jit(solution)/shard_map/ppermute | solution.py:306
  62.7 1.1 %collective-permute-done.1.other_ref = bf16[256,128]{1,0:T(8,128)(2,1)S(1)} collective-permute-done((bf16[256,128]{1,0:T(8,128)(2,1)S(1)}, bf16[256,128]{1,0:T(8,128)(2,1)S(1)}, u32[]{:S(2)}, u32[]{:S(2)}) %collective-permute-start.1) | collective-permute-done | bytes 65568 | tf_op jit(solution)/shard_map/ppermute | solution.py:306
  63.8 0.0 copy-done
  63.8 2.1 %context.1 = bf16[256,512]{1,0:T(8,128)(2,1)} custom-call(bf16[256,512]{1,0:T(8,128)(2,1)S(1)} %copy-done, bf16[784,128]{1,0:T(8,128)(2,1)S(1)} %get-tuple-element.7.own_ref, bf16[256,128]{1,0:T(8,128)(2,1)S(1)} %anchor_half.1.half_ref, bf16[256,128]{1,0:T(8,128)(2,1)S(1)} %collective-permute-done.1.other_ref), custom_call_target="tpu_custom_call" | custom-call | flops 268435456 | bytes 1048576 | tf_op jit(solution)/shard_map/context/pallas_call | solution.py:264
  65.9 1.9 %all-to-all-done.2.parts_ref = f32[16,16,128]{2,1,0:T(8,128)S(1)} async-done(((f32[16,16,128]{2,1,0:T(8,128)}), f32[16,16,128]{2,1,0:T(8,128)S(1)}, u32[]{:S(2)}, u32[]{:S(2)}) %all-to-all-start.2) | async-done | bytes 131104 | tf_op jit(solution)/shard_map/all_to_all | solution.py:305
  67.8 0.7 %finish.1 = bf16[64,64]{1,0:T(8,128)(2,1)} custom-call(f32[16,16,128]{2,1,0:T(8,128)S(1)} %all-to-all-done.2.parts_ref), custom_call_target="tpu_custom_call" | custom-call | tf_op jit(solution)/shard_map/finish/pallas_call | solution.py:285
  (1 shorter events, 0.0 us)
Async XLA Ops:
  1.8 9.8 %collective-permute-start = (bf16[784,128]{1,0:T(8,128)(2,1)S(1)}, bf16[784,128]{1,0:T(8,128)(2,1)S(1)}, u32[]{:S(2)}, u32[]{:S(2)}) collective-permute-start(bf16[784,128]{1,0:T(8,128)(2,1)S(1)} %get-tuple-element.7.own_ref), channel_id=1, source_target_pairs={{0,8},{8,0},{1,9},{9,1},{2,10},{10,2},{3,11},{11,3},{4,12},{12,4},... | collective-permute-start | bytes 602120 | tf_op jit(solution)/shard_map/ppermute | solution.py:295
  48.5 19.3 %all-to-all-start.2 = ((f32[16,16,128]{2,1,0:T(8,128)}), f32[16,16,128]{2,1,0:T(8,128)S(1)}, u32[]{:S(2)}, u32[]{:S(2)}) async-start(f32[16,16,128]{2,1,0:T(8,128)} %bitcast.5), calls=%async_computation.2 | async-start | bytes 262144 | tf_op jit(solution)/shard_map/all_to_all | solution.py:305
  60.5 3.3 %copy-start = (bf16[256,512]{1,0:T(8,128)(2,1)S(1)}, bf16[256,512]{1,0:T(8,128)(2,1)}, u32[]{:S(2)}) copy-start(bf16[256,512]{1,0:T(8,128)(2,1)} %q_ref.1) | copy-start | bytes 786436
  60.5 3.3 %collective-permute-start.1 = (bf16[256,128]{1,0:T(8,128)(2,1)S(1)}, bf16[256,128]{1,0:T(8,128)(2,1)S(1)}, u32[]{:S(2)}, u32[]{:S(2)}) collective-permute-start(bf16[256,128]{1,0:T(8,128)(2,1)S(1)} %anchor_half.1.half_ref), channel_id=1, source_target_pairs={{0,8},{8,0},{1,9},{9,1},{2,10},{10,2},{3,11},{11,3},{4,12},{12,4},... | collective-permute-start | bytes 196616 | tf_op jit(solution)/shard_map/ppermute | solution.py:306

commit v13 on v10

--- a/solution.py
+++ b/solution.py
@@ -153,7 +153,7 @@
     @pl.when(core == 0)
     def _():
         out_ref[:, ANCHOR:FIRST] = own_ref[0:BLK, :]
-        pl.delay(2500)
+        pl.delay(2750)
 
     @pl.when(core != 0)
     def _():

time: 68.8 us -> 68.6 us (level)
  blocking collectives: 34 us -> 33 us
  starting transfers between devices: 22.9 us -> 23.7 us
    all_to_all x1, blocking collectives: 16.2 us -> 15.3 us  [body(): gathered = lax.all_to_all(message, ('x', 'zb', 'za'), 0, 0)]
    all_to_all x1, starting transfers between devices: 12 us -> 12.8 us  [body(): sums = lax.all_to_all(sums.reshape(16, 16, 128), ('core', 'tp'), 0, 0)]
where the time goes in v13:
time: 68.6 us; the launch traced here: 68.3 us
  blocking collectives  33 us (48%)
  starting transfers between devices  23.7 us (35%)
  Pallas kernels  7.46 us (11%)
  waiting for transfers between devices  3.42 us (5%)
  between operations  0.7 us (1%)
    all_to_all x1, blocking collectives, body(): lax.all_to_all(parts.reshape(PEERS, SHARE, FIRST), ('x', 'zb', 'za'), 0, 0)  17.7 us
    all_to_all x1, blocking collectives, body(): gathered = lax.all_to_all(message, ('x', 'zb', 'za'), 0, 0)  15.3 us
    all_to_all x1, starting transfers between devices, body(): sums = lax.all_to_all(sums.reshape(16, 16, 128), ('core', 'tp'), 0, 0)  12.8 us
    ppermute x1, starting transfers between devices, body(): mate = lax.ppermute(own, 'core', [(0, 1), (1, 0)])  8.79 us
    ppermute x1, starting transfers between devices, body(): other = lax.ppermute(half, 'core', [(0, 1), (1, 0)])  2.14 us
    pallas_call x1, Pallas kernels, context(): pl.pallas_call(context_kernel, out_shape=jax.ShapeDtypeStruct((BLK, GROUP...  2.1 us
    all_to_all x1, waiting for transfers between devices, body(): sums = lax.all_to_all(sums.reshape(16, 16, 128), ('core', 'tp'), 0, 0)  1.88 us
    pallas_call x1, Pallas kernels, query_parts(): pl.pallas_call(mate_kernel, out_shape=pltpu.VMEM((HALF, FIRST), BF16), in...  1.48 us
  transfers between devices with their start and end apart: 3, of which 3 were waited for; matrix products, arithmetic and copies ran while one was open for 0% of the time, Pallas kernels for 4%

profile of v13, /device:TPU:1, one launch (start us, length us, event | category | flops | bytes accessed | tf_op | source)
XLA Modules:
  0.0 68.3 jit_solution(3152231172988585599)
XLA Ops:
  0.6 1.1 %pack.1 = (bf16[784,128]{1,0:T(8,128)(2,1)S(1)}, bf16[8,32,512]{2,1,0:T(8,128)(2,1)S(1)}) custom-call(bf16[256,128]{1,0:T(8,128)(2,1)} %keys.1, bf16[256,128]{1,0:T(8,128)(2,1)} %values.1, bf16[8,128]{1,0:T(8,128)(2,1)} %query_keys.1, bf16[8,128]{1,0:T(8,128)(2,1)} %query_values.1, bf16[64,512]{1,0:T(8,128)(2,1)} %bitcast.12, bf16[8,2,32,512]{3,2,1,0:T(8,128)(2,1)} %bitcast.11), custom_call_target="tpu_custom_call" | custom-call | tf_op jit(solution)/shard_map/pack/pallas_call | solution.py:71
  1.8 8.8 %collective-permute-start = (bf16[784,128]{1,0:T(8,128)(2,1)S(1)}, bf16[784,128]{1,0:T(8,128)(2,1)S(1)}, u32[]{:S(2)}, u32[]{:S(2)}) collective-permute-start(bf16[784,128]{1,0:T(8,128)(2,1)S(1)} %get-tuple-element.7.own_ref), channel_id=1, source_target_pairs={{0,8},{8,0},{1,9},{9,1},{2,10},{10,2},{3,11},{11,3},{4,12},{12,4},... | collective-permute-start | bytes 602120 | tf_op jit(solution)/shard_map/ppermute | solution.py:295
  10.6 0.6 query_own.1
  11.2 0.4 collective-permute-done.mate_ref
  11.6 1.5 %query_parts.1 = bf16[256,768]{1,0:T(8,128)(2,1)S(1)} custom-call(bf16[256,512]{1,0:T(8,128)(2,1)S(1)} %bitcast.10, bf16[784,128]{1,0:T(8,128)(2,1)S(1)} %get-tuple-element.7.own_ref, bf16[784,128]{1,0:T(8,128)(2,1)S(1)} %collective-permute-done.mate_ref, f32[1024,128]{1,0:T(8,128)S(1)} %get-tuple-element.9.top_ref, ...), custom_call_target="tpu_custom_call" | custom-call | tf_op jit(solution)/shard_map/query_parts/pallas_call | solution.py:164
  13.1 17.7 %all_to_all.15.parts_ref = bf16[32,8,768]{2,1,0:T(8,128)(2,1)S(1)} all-to-all(bf16[32,8,768]{2,1,0:T(8,128)(2,1)S(1)} %bitcast.8), channel_id=1, replica_groups=mesh['za'=4,'zb'=2,'x'=4,'core'=2,'tp'=8] {'x','zb','za'}, dimensions={0} | all-to-all | bytes 786432 | tf_op jit(solution)/shard_map/all_to_all | solution.py:298
  30.8 0.5 merge_parts.1
  31.2 15.3 %all_to_all.16 = bf16[32,8,640]{2,1,0:T(8,128)(2,1)S(1)} all-to-all(bf16[32,8,640]{2,1,0:T(8,128)(2,1)S(1)} %merge_parts.1), channel_id=1, replica_groups=mesh['za'=4,'zb'=2,'x'=4,'core'=2,'tp'=8] {'x','zb','za'}, dimensions={0} | all-to-all | bytes 655360 | tf_op jit(solution)/shard_map/all_to_all | solution.py:300
  46.6 0.9 %project.1 = f32[2,8,16,128]{3,2,1,0:T(8,128)} custom-call(bf16[256,640]{1,0:T(8,128)(2,1)S(1)} %bitcast.6, bf16[784,128]{1,0:T(8,128)(2,1)S(1)} %get-tuple-element.7.own_ref, bf16[784,128]{1,0:T(8,128)(2,1)S(1)} %collective-permute-done.mate_ref), custom_call_target="tpu_custom_call" | custom-call | tf_op jit(solution)/shard_map/project/pallas_call | solution.py:220
  47.5 12.8 %all-to-all-start.2 = ((f32[16,16,128]{2,1,0:T(8,128)}), f32[16,16,128]{2,1,0:T(8,128)S(1)}, u32[]{:S(2)}, u32[]{:S(2)}) async-start(f32[16,16,128]{2,1,0:T(8,128)} %bitcast.5), calls=%async_computation.2 | async-start | bytes 262144 | tf_op jit(solution)/shard_map/all_to_all | solution.py:305
  60.3 0.0 copy-start
  60.3 2.1 %collective-permute-start.1 = (bf16[256,128]{1,0:T(8,128)(2,1)S(1)}, bf16[256,128]{1,0:T(8,128)(2,1)S(1)}, u32[]{:S(2)}, u32[]{:S(2)}) collective-permute-start(bf16[256,128]{1,0:T(8,128)(2,1)S(1)} %anchor_half.1.half_ref), channel_id=1, source_target_pairs={{0,8},{8,0},{1,9},{9,1},{2,10},{10,2},{3,11},{11,3},{4,12},{12,4},... | collective-permute-start | bytes 196616 | tf_op jit(solution)/shard_map/ppermute | solution.py:306
  62.5 1.1 %collective-permute-done.1.other_ref = bf16[256,128]{1,0:T(8,128)(2,1)S(1)} collective-permute-done((bf16[256,128]{1,0:T(8,128)(2,1)S(1)}, bf16[256,128]{1,0:T(8,128)(2,1)S(1)}, u32[]{:S(2)}, u32[]{:S(2)}) %collective-permute-start.1) | collective-permute-done | bytes 65568 | tf_op jit(solution)/shard_map/ppermute | solution.py:306
  63.6 0.0 copy-done
  63.6 2.1 %context.1 = bf16[256,512]{1,0:T(8,128)(2,1)} custom-call(bf16[256,512]{1,0:T(8,128)(2,1)S(1)} %copy-done, bf16[784,128]{1,0:T(8,128)(2,1)S(1)} %get-tuple-element.7.own_ref, bf16[256,128]{1,0:T(8,128)(2,1)S(1)} %anchor_half.1.half_ref, bf16[256,128]{1,0:T(8,128)(2,1)S(1)} %collective-permute-done.1.other_ref), custom_call_target="tpu_custom_call" | custom-call | flops 268435456 | bytes 1048576 | tf_op jit(solution)/shard_map/context/pallas_call | solution.py:264
  65.7 1.9 %all-to-all-done.2.parts_ref = f32[16,16,128]{2,1,0:T(8,128)S(1)} async-done(((f32[16,16,128]{2,1,0:T(8,128)}), f32[16,16,128]{2,1,0:T(8,128)S(1)}, u32[]{:S(2)}, u32[]{:S(2)}) %all-to-all-start.2) | async-done | bytes 131104 | tf_op jit(solution)/shard_map/all_to_all | solution.py:305
  67.6 0.7 %finish.1 = bf16[64,64]{1,0:T(8,128)(2,1)} custom-call(f32[16,16,128]{2,1,0:T(8,128)S(1)} %all-to-all-done.2.parts_ref), custom_call_target="tpu_custom_call" | custom-call | tf_op jit(solution)/shard_map/finish/pallas_call | solution.py:285
  (1 shorter events, 0.0 us)
Async XLA Ops:
  1.8 9.8 %collective-permute-start = (bf16[784,128]{1,0:T(8,128)(2,1)S(1)}, bf16[784,128]{1,0:T(8,128)(2,1)S(1)}, u32[]{:S(2)}, u32[]{:S(2)}) collective-permute-start(bf16[784,128]{1,0:T(8,128)(2,1)S(1)} %get-tuple-element.7.own_ref), channel_id=1, source_target_pairs={{0,8},{8,0},{1,9},{9,1},{2,10},{10,2},{3,11},{11,3},{4,12},{12,4},... | collective-permute-start | bytes 602120 | tf_op jit(solution)/shard_map/ppermute | solution.py:295
  47.5 20.1 %all-to-all-start.2 = ((f32[16,16,128]{2,1,0:T(8,128)}), f32[16,16,128]{2,1,0:T(8,128)S(1)}, u32[]{:S(2)}, u32[]{:S(2)}) async-start(f32[16,16,128]{2,1,0:T(8,128)} %bitcast.5), calls=%async_computation.2 | async-start | bytes 262144 | tf_op jit(solution)/shard_map/all_to_all | solution.py:305
  60.3 3.3 %copy-start = (bf16[256,512]{1,0:T(8,128)(2,1)S(1)}, bf16[256,512]{1,0:T(8,128)(2,1)}, u32[]{:S(2)}) copy-start(bf16[256,512]{1,0:T(8,128)(2,1)} %q_ref.1) | copy-start | bytes 786436
  60.3 3.3 %collective-permute-start.1 = (bf16[256,128]{1,0:T(8,128)(2,1)S(1)}, bf16[256,128]{1,0:T(8,128)(2,1)S(1)}, u32[]{:S(2)}, u32[]{:S(2)}) collective-permute-start(bf16[256,128]{1,0:T(8,128)(2,1)S(1)} %anchor_half.1.half_ref), channel_id=1, source_target_pairs={{0,8},{8,0},{1,9},{9,1},{2,10},{10,2},{3,11},{11,3},{4,12},{12,4},... | collective-permute-start | bytes 196616 | tf_op jit(solution)/shard_map/ppermute | solution.py:306
